TPU v7x, 256 devices: a whole 4x4x8 slice. The times are simulated.
256 devices in a mesh: dp: 8 (over z_lo, y), space: 32 (over x, z_hi, core).
Axes of the slice: x: 4, y: 4, z: 8 (z_hi: 4, z_lo: 2; z = z_hi * 2 + z_lo), core: 2. Of those that a mesh axis runs over, the one named last changes fastest.
Arguments:
- volumes: bfloat16 [8, 128, 32, 4096], P('dp', 'space'), may hold values from -6 to 6
- first_filter: bfloat16 [3, 3, 3, 64, 128], replicated, may hold values from -0.15625 to 0.15625
- second_filter: bfloat16 [3, 3, 3, 128, 128], replicated, may hold values from -0.109375 to 0.109375
- upstream_grad: bfloat16 [8, 32, 8, 16, 128], P('dp', 'space'), may hold values from -0.029907227 to 0.029907227
Outputs:
- second_out: bfloat16 [8, 32, 8, 16, 128], P('dp', 'space')
- first_grad: float32 [3, 3, 3, 64, 128], P(None, None, None, None, 'space')
- second_grad: float32 [3, 3, 3, 128, 128], P(None, None, None, 'space')
All inputs are finite; a program needn't handle non-finite values.
Results may differ from a plain program's by a relative error of at most 0.01.
The roundings to bfloat16 on the way count: a program that leaves them out, or rounds other values in their place, can miss the bound.
Values may be sent and summed in bfloat16 or wider, within the bound.
No kernel may reach another device: no remote copies, remote signals or barrier semaphores. Data moves between devices by JAX's collectives and lax.ppermute only.
A program may use at most 64 MiB of HBM per device.

v0:
```python
import jax
import jax.numpy as jnp
from jax import lax
from jax.sharding import PartitionSpec as P

SLOPE = 0.3


def passed_along(value, axis, by):
    size = lax.axis_size(axis)
    pairs = [(i, i + by) for i in range(size) if 0 <= i + by < size]
    return lax.ppermute(value, axis, pairs)


def leaky_relu(values):
    return jnp.where(values > 0, values, SLOPE * values)


def strided_conv(extended, weights):
    return lax.conv_general_dilated(
        extended,
        weights,
        (2, 2, 2),
        ((0, 0), (1, 1), (1, 1)),
        dimension_numbers=("NDHWC", "DHWIO", "NDHWC"),
        preferred_element_type=jnp.float32,
    )


def filter_grad(extended, out_grads):
    return lax.conv_general_dilated(
        extended,
        out_grads,
        (1, 1, 1),
        ((0, 0), (1, 0), (1, 0)),
        rhs_dilation=(2, 2, 2),
        dimension_numbers=("CDHWN", "IDHWO", "DHWNC"),
        preferred_element_type=jnp.float32,
    )


def input_grad(out_grads, weights):
    flipped = weights[::-1, ::-1, ::-1]
    return lax.conv_general_dilated(
        out_grads,
        flipped,
        (1, 1, 1),
        ((1, 0), (1, 2), (1, 2)),
        lhs_dilation=(2, 2, 2),
        dimension_numbers=("NDHWC", "DHWOI", "NDHWC"),
        preferred_element_type=jnp.float32,
    )


def local(volumes, first_filter, second_filter, upstream_grad):
    samples, planes, height, merged = volumes.shape
    in_channels = first_filter.shape[3]
    volume_view = volumes.reshape(samples, planes, height, merged // in_channels, in_channels)
    lower_rim = passed_along(volume_view[:, -1:], "space", 1)
    volume_ext = jnp.concatenate([lower_rim, volume_view], axis=1)
    pre_one = strided_conv(volume_ext, first_filter)
    hidden = leaky_relu(pre_one).astype(jnp.bfloat16)
    middle_plane = passed_along(hidden[:, -1:], "space", 1)
    hidden_ext = jnp.concatenate([middle_plane, hidden], axis=1)
    pre_two = strided_conv(hidden_ext, second_filter)
    second_out = leaky_relu(pre_two).astype(jnp.bfloat16)
    grad_pre_two = (upstream_grad.astype(jnp.float32) * jnp.where(pre_two > 0, 1.0, SLOPE)).astype(
        jnp.bfloat16
    )
    upper_plane = passed_along(grad_pre_two[:, :1], "space", -1)
    second_term = filter_grad(hidden_ext, grad_pre_two)
    second_grad = lax.psum_scatter(second_term, "space", scatter_dimension=3, tiled=True)
    extended = jnp.concatenate([grad_pre_two, upper_plane], axis=1)
    grad_hidden = input_grad(extended, second_filter).astype(jnp.bfloat16)
    grad_pre_one = (grad_hidden.astype(jnp.float32) * jnp.where(hidden > 0, 1.0, SLOPE)).astype(
        jnp.bfloat16
    )
    first_term = filter_grad(volume_ext, grad_pre_one)
    first_grad = lax.psum_scatter(first_term, "space", scatter_dimension=4, tiled=True)
    first_grad, second_grad = lax.psum((first_grad, second_grad), "dp")
    return (second_out, first_grad, second_grad)


def solution(mesh):
    placed = (P("dp", "space", None, None), P(), P(), P("dp", "space", None, None, None))
    return jax.shard_map(
        local,
        mesh=mesh,
        in_specs=placed,
        out_specs=(
            P("dp", "space", None, None, None),
            P(None, None, None, None, "space"),
            P(None, None, None, "space", None),
        ),
        check_vma=False,
    )
```

profile of v0, /device:TPU:6, one launch (start us, length us, event | category | flops | bytes accessed | tf_op | source)
XLA Modules:
  0.0 461.8 jit_solution(15137153969126217632)
XLA Ops:
  7.2 3.3 reshape.9
  10.6 1.9 collective-permute-start
  12.5 14.4 %collective-permute-done = bf16[1,1,32,64,64]{4,3,2,1,0:T(8,128)(2,1)S(1)} collective-permute-done((bf16[1,1,32,64,64]{4,3,2,1,0:T(8,128)(2,1)S(1)}, bf16[1,1,32,64,64]{4,3,2,1,0:T(8,128)(2,1)S(1)}, u32[]{:S(2)}, u32[]{:S(2)}) %collective-permute-start) | collective-permute-done | bytes 262176 | tf_op jit(solution)/shard_map/ppermute | solution.py:12
  26.9 0.5 maximum_bitcast_fusion
  27.4 1.7 copy.110
  29.1 0.7 pad.clone
  29.9 2.1 copy.70
  32.2 1.7 compare_select_fusion.1
  34.0 0.8 pad.7.clone
  34.9 1.5 fusion.69
  36.7 2.1 collective-permute-start.1
  39.0 1.4 copy.108
  40.4 1.4 copy.107
  42.0 2.5 copy.87
  44.6 1.9 fusion.10
  46.5 0.9 collective-permute-done.1
  47.6 0.6 copy_dynamic-update-slice_fusion
  48.2 0.5 copy.120
  49.1 0.5 compare_select_fusion.2
  49.7 6.0 %collective-permute-start.2 = (bf16[1,1,8,16,128]{4,2,3,1,0:T(8,128)(2,1)S(1)}, bf16[1,1,8,16,128]{4,2,3,1,0:T(8,128)(2,1)S(1)}, u32[]{:S(2)}, u32[]{:S(2)}) collective-permute-start(bf16[1,1,8,16,128]{4,2,3,1,0:T(8,128)(2,1)S(1)} %fusion.56), channel_id=1, source_target_pairs={{1,0},{2,1},{3,2},{4,3},{5,4},{6,5},{7,6},{8,7},{9,8},{10,9},{11,1... | collective-permute-start | bytes 98312 | tf_op jit(solution)/shard_map/ppermute | solution.py:12
  55.7 3.0 fusion.57
  58.9 0.9 fusion.30
  59.8 4.5 fusion.22
  64.4 2.5 copy.95
  66.9 0.6 dynamic-slice
  68.2 290.5 %all-reduce.7.cloned.1.call-done = (f32[3,3,3,64,128]{3,2,1,0,4:T(4,128)}, f32[3,3,3,128,128]{4,3,2,1,0:T(8,128)}) async-done(((f32[3,3,3,64,128]{3,2,1,0,4:T(4,128)}, f32[3,3,3,128,128]{4,3,2,1,0:T(8,128)}), (f32[3,3,3,64,128]{3,2,1,0,4:T(4,128)}, f32[3,3,3,128,128]{4,3,2,1,0:T(8,128)})) %all-reduce.7.cloned.1.call-update) | async-done | bytes 2654224
  358.7 1.5 constant_dynamic-slice_fusion.1
  360.3 1.5 constant_dynamic-slice_fusion
  361.8 0.6 copy.97
  362.4 89.6 %all-reduce.9.cloned.1.call-done = (f32[3,3,3,64,4]{3,2,1,0,4:T(4,128)}, f32[3,3,3,4,128]{4,3,2,1,0:T(4,128)}) async-done(((f32[3,3,3,64,4]{3,2,1,0,4:T(4,128)}, f32[3,3,3,4,128]{4,3,2,1,0:T(4,128)}), (f32[3,3,3,64,4]{3,2,1,0,4:T(4,128)}, f32[3,3,3,4,128]{4,3,2,1,0:T(4,128)})) %all-reduce.9.cloned.1.call-update) | async-done | bytes 82960 | tf_op jit(solution)/shard_map/psum | solution.py:80
  452.0 1.5 copy.98
  453.6 1.4 copy.126
  (44 shorter events, 1.9 us)
Async XLA Ops:
  7.2 41.9 %copy-start = (bf16[3,3,3,128,128]{4,3,2,1,0:T(8,128)(2,1)S(1)}, bf16[3,3,3,128,128]{4,3,2,1,0:T(8,128)(2,1)}, u32[]{:S(2)}) copy-start(bf16[3,3,3,128,128]{4,3,2,1,0:T(8,128)(2,1)} %param.6) | copy-start | bytes 2654212
  7.2 351.6 %all-reduce.7.cloned.1.call-start = ((), (), s32[]{:S(2)}) async-start(), calls=%async_computation | async-start | bytes 8257536
  10.6 16.3 %collective-permute-start = (bf16[1,1,32,64,64]{4,3,2,1,0:T(8,128)(2,1)S(1)}, bf16[1,1,32,64,64]{4,3,2,1,0:T(8,128)(2,1)S(1)}, u32[]{:S(2)}, u32[]{:S(2)}) collective-permute-start(bf16[1,1,32,64,64]{4,3,2,1,0:T(8,128)(2,1)S(1)} %slice.20), channel_id=1, source_target_pairs={{0,1},{1,2},{2,3},{3,4},{4,5},{5,6},{6,7},{7,8},{8,9},{9,10},{10,1... | collective-permute-start | bytes 786440 | tf_op jit(solution)/shard_map/ppermute | solution.py:12
  29.9 2.3 copy-start.2
  29.9 2.3 copy-start.5
  36.7 10.7 %collective-permute-start.1 = (bf16[1,1,16,32,128]{4,0,3,2,1:T(2,128)(2,1)S(1)}, bf16[1,1,16,32,128]{4,0,3,2,1:T(2,128)(2,1)S(1)}, u32[]{:S(2)}, u32[]{:S(2)}) collective-permute-start(bf16[1,1,16,32,128]{4,0,3,2,1:T(2,128)(2,1)S(1)} %copy.73), channel_id=1, source_target_pairs={{0,1},{1,2},{2,3},{3,4},{4,5},{5,6},{6,7},{7,8},{8,9},{9,10},{10,1... | collective-permute-start | bytes 393224 | tf_op jit(solution)/shard_map/ppermute | solution.py:12
  46.5 2.6 copy-start.6
  47.6 2.0 copy-start.1
  49.7 9.2 %copy-start.4 = (pred[8,6]{0,1:T(8,128)(4,1)S(1)}, pred[8,6]{0,1:T(8,128)(4,1)}, u32[]{:S(2)}) copy-start(pred[8,6]{0,1:T(8,128)(4,1)} %constant.33) | copy-start | bytes 148
  49.7 9.1 %collective-permute-start.2 = (bf16[1,1,8,16,128]{4,2,3,1,0:T(8,128)(2,1)S(1)}, bf16[1,1,8,16,128]{4,2,3,1,0:T(8,128)(2,1)S(1)}, u32[]{:S(2)}, u32[]{:S(2)}) collective-permute-start(bf16[1,1,8,16,128]{4,2,3,1,0:T(8,128)(2,1)S(1)} %fusion.56), channel_id=1, source_target_pairs={{1,0},{2,1},{3,2},{4,3},{5,4},{6,5},{7,6},{8,7},{9,8},{10,9},{11,1... | collective-permute-start | bytes 98312 | tf_op jit(solution)/shard_map/ppermute | solution.py:12
  64.3 2.6 copy-start.3
  66.9 385.2 %all-reduce.9.cloned.1.call-start = ((), (), s32[]{:S(2)}) async-start(), calls=%async_computation.1 | async-start | bytes 258048 | tf_op jit(solution)/shard_map/psum | solution.py:80
Sparse Core Ops, SparseCore 0:
  67.0 291.6 all-reduce.6
  362.0 89.9 all-reduce.8
where the time goes:
time: 462 us
  waiting for transfers between devices  395 us (85%)
  local copies, waits for them, and re-layouts  28.1 us (6%)
  between operations  15.1 us (3%)
  matrix products  10.7 us (2%)
  starting transfers between devices  10.1 us (2%)
    unnamed x3, waiting for transfers between devices  291 us
    psum x1, waiting for transfers between devices, local(): first_grad, second_grad = lax.psum((first_grad, second_grad), 'dp')  89.6 us
    ppermute x3, waiting for transfers between devices, passed_along(): return lax.ppermute(value, axis, pairs)  15.3 us
    unnamed x27, local copies, waits for them, and re-layouts  12.7 us
    ppermute x3, starting transfers between devices, passed_along(): return lax.ppermute(value, axis, pairs)  10.1 us
  transfers between devices with their start and end apart: 5, of which 4 were waited for; matrix products, arithmetic and copies ran while one was open for 3% of the time, Pallas kernels for 0%

commit v1 on v0

v1 whole, which is shorter than its diff:
```python
import jax
import jax.numpy as jnp
from jax import lax
from jax.experimental import pallas as pl
from jax.experimental.pallas import tpu as pltpu
from jax.sharding import PartitionSpec as P

SLOPE = 0.3
F32, BF16 = jnp.float32, jnp.bfloat16
FIRST_LANES = 14 * 128
SECOND_LANES = 27 * 128


def next_in_space(value, by):
    pairs = [(i, i + by) for i in range(32) if 0 <= i + by < 32]
    return lax.ppermute(value, "space", pairs)


def swap_core(value):
    return lax.ppermute(value, "space", [(i, i ^ 1) for i in range(32)])


def ring_x(value, k):
    return lax.ppermute(value, "space", [(i, ((i >> 3) + k) % 4 * 8 + (i & 7)) for i in range(32)])


def ring_z(value, k):
    return lax.ppermute(
        value, "space", [(i, (i & ~6) | ((((i >> 1) & 3) + k) % 4 << 1)) for i in range(32)]
    )


def ring_y(value, k):
    return lax.ppermute(value, "dp", [(i, (i & 4) | ((i & 3) + k) % 4) for i in range(8)])


def swap_z_low(value):
    return lax.ppermute(value, "dp", [(i, i ^ 4) for i in range(8)])


def leaky(values):
    return jnp.where(values > 0, values, SLOPE * values)


def dot(a, b):
    return jnp.dot(a, b, preferred_element_type=F32)


def dot_nt(a, b):
    return lax.dot_general(a, b, (((1,), (1,)), ((), ())), preferred_element_type=F32)


def rows_by_tap():
    m = lax.broadcasted_iota(jnp.int32, (48, 32), 0)
    h = lax.broadcasted_iota(jnp.int32, (48, 32), 1)
    return jnp.where(h == 2 * (m & 15) + (m >> 4) - 1, 1.0, 0.0).astype(BF16)


def channel_order():
    m = lax.broadcasted_iota(jnp.int32, (128, 128), 0)
    i = lax.broadcasted_iota(jnp.int32, (128, 128), 1)
    natural = ((m >> 4) & 3) * 32 + ((m >> 2) & 3) * 8 + (m >> 6) * 4 + (m & 3)
    return jnp.where(i == natural, 1.0, 0.0).astype(BF16)


def spread_rows(plane_ref, pick, y_ref):
    for t in range(3):
        y_ref[t, 0] = jnp.zeros((16, 128), BF16)
    for n in range(8):
        out = dot(pick, plane_ref[:, n * 512 : (n + 1) * 512]).astype(BF16)
        for t in range(3):
            for r in range(4):
                y_ref[t, 1 + 4 * n + r] = out[16 * t : 16 * t + 16, 128 * r : 128 * r + 128]


def columns(y_ref, b):
    before = y_ref[b, 0:32].reshape(512, 128)
    at = y_ref[b, 1:33].reshape(512, 128)
    return jnp.concatenate([before, at], axis=1)


def first_conv(planes, f_ref, w_ref):
    for ab in range(9):
        w_ref[ab * 256 : ab * 256 + 64] = jnp.zeros((64, 128), BF16)
        w_ref[ab * 256 + 64 : ab * 256 + 256] = f_ref[ab]
    lhs = jnp.concatenate([columns(planes[a], b) for a in range(3) for b in range(3)], axis=1)
    return leaky(dot(lhs, w_ref[...])).astype(BF16)


def core_x_z():
    s = lax.axis_index("space")
    return s & 1, s >> 3, (s >> 1) & 3


def upper_plane_kernel(v_ref, f_ref, y_ref, hid_ref, w_ref):
    pick = rows_by_tap()
    for p in range(4):
        spread_rows(v_ref.at[p], pick, y_ref.at[p])
    hid_ref[...] = first_conv([y_ref.at[p] for p in (1, 2, 3)], f_ref, w_ref)


def lower_plane_kernel(v_ref, y_ref, f_ref, yh_ref, hid_ref, w_ref):
    spread_rows(v_ref, rows_by_tap(), yh_ref)
    hid_ref[...] = first_conv([yh_ref, y_ref.at[0], y_ref.at[1]], f_ref, w_ref)


def second_conv_kernel(hm_ref, h0_ref, h1_ref, f_ref, up_ref, out_ref, gp_ref, t_ref, hs, us, os):
    for a, h_ref in enumerate((hm_ref, h0_ref, h1_ref)):
        h = h_ref[...].astype(F32).reshape(16, 2, 16, 128)
        hs[a, :, :, 0:8, :] = jnp.zeros((17, 2, 8, 128), F32)
        hs[a, 0, 0] = jnp.zeros((24, 128), F32)
        hs[a, 0:16, 1, 8:24, :] = h[:, 0]
        hs[a, 1:17, 0, 8:24, :] = h[:, 1]
    tap = 0
    for a in range(3):
        for b in range(3):
            for c in range(3):
                rows = hs[a, c // 2 : c // 2 + 16, c % 2, pl.ds(7 + b, 8, stride=2), :]
                t_ref[:, tap * 128 : tap * 128 + 128] = rows.reshape(128, 128).astype(BF16)
                tap += 1
    pre = dot(t_ref[...], f_ref[...])
    us[...] = up_ref[...].astype(F32).reshape(128, 128)
    up = jnp.concatenate([us[pl.ds(r, 8, stride=16), :] for r in range(16)], axis=0)
    gp_ref[...] = (up * jnp.where(pre > 0, 1.0, SLOPE)).astype(BF16)
    out = leaky(pre)
    for r in range(16):
        os[pl.ds(r, 8, stride=16), :] = out[8 * r : 8 * r + 8]
    out_ref[...] = os[...].astype(BF16).reshape(8, 16, 128)


def second_grad_kernel(t_ref, gp_ref, keep_ref, send_ref, g):
    order = channel_order()
    gp = gp_ref[...]
    for tap in range(27):
        lanes = slice(tap * 128, tap * 128 + 128)
        turned = dot_nt(order, t_ref[:, lanes]).astype(BF16)
        g[:, lanes] = dot(turned, gp)
    core, _, _ = core_x_z()
    keep_ref[...] = g[pl.ds(pl.multiple_of(core * 64, 64), 64), :]
    send_ref[...] = g[pl.ds(pl.multiple_of((1 - core) * 64, 64), 64), :].astype(BF16)


def first_grad_kernel(
    gp_ref, gpn_ref, f_ref, h0_ref, h1_ref, yh_ref, y_ref, keep_ref, send_ref, gs, gu, g
):
    gs[...] = jnp.zeros_like(gs)
    for s, ref in enumerate((gp_ref, gpn_ref)):
        gs[s, 0:16, 0:8, :] = ref[...].astype(F32).reshape(16, 8, 128)
    moved = {
        (s, dr, dq): gs[s, dr : dr + 16, dq : dq + 8, :].reshape(128, 128).astype(BF16)
        for s in range(2)
        for dr in range(2)
        for dq in range(2)
    }
    one_d = {0: [(0, 1)], 1: [(0, 2), (1, 0)]}
    for pu in range(2):
        for pv in range(2):
            for pw in range(2):
                lhs, rhs = [], []
                for s, a in one_d[pu]:
                    for dq, b in one_d[pv]:
                        for dr, c in one_d[pw]:
                            lhs.append(moved[s, dr, dq])
                            rhs.append(f_ref[9 * a + 3 * b + c])
                grad = dot_nt(jnp.concatenate(lhs, axis=1), jnp.concatenate(rhs, axis=1))
                grad = grad.astype(BF16).astype(F32).reshape(16, 8, 128)
                gu[pu, :, pw, pl.ds(pv, 8, stride=2), :] = grad
    grads = []
    for pu, h_ref in enumerate((h0_ref, h1_ref)):
        hid = h_ref[...].astype(F32)
        grads.append((gu[pu].reshape(512, 128) * jnp.where(hid > 0, 1.0, SLOPE)).astype(BF16))
    turned = dot_nt(channel_order(), jnp.concatenate(grads, axis=0)).astype(BF16)
    planes = [yh_ref] + [y_ref.at[p] for p in range(4)]
    low = lax.broadcasted_iota(jnp.int32, (128, 128), 1) < 64
    held = None
    for a in range(3):
        for b in range(3):
            ab = 3 * a + b
            rhs = jnp.concatenate([columns(planes[a], b), columns(planes[a + 2], b)], axis=0)
            grad = dot(turned, rhs)
            g[:, ab * 128 : ab * 128 + 128] = grad[:, 128:]
            if ab % 2 == 0:
                held = pltpu.roll(grad[:, :128], 64, axis=1)
            if ab % 2 == 1 or ab == 8:
                block = 9 + ab // 2
                upper = grad[:, :128] if ab % 2 else jnp.zeros_like(held)
                g[:, block * 128 : block * 128 + 128] = jnp.where(low, held, upper)
    core, _, _ = core_x_z()
    keep_ref[...] = g[pl.ds(pl.multiple_of(core * 64, 64), 64), :]
    send_ref[...] = g[pl.ds(pl.multiple_of((1 - core) * 64, 64), 64), :].astype(BF16)


def after_core_kernel(keep_ref, got_ref, own_ref, s1_ref, s2_ref, s3_ref, acc):
    acc[...] = keep_ref[...] + got_ref[...].astype(F32)
    _, x, _ = core_x_z()
    own_ref[...] = acc[pl.ds(pl.multiple_of(x * 16, 16), 16), :]
    for k, ref in enumerate((s1_ref, s2_ref, s3_ref)):
        at = pl.multiple_of(((x + k + 1) & 3) * 16, 16)
        ref[...] = acc[pl.ds(at, 16), :].astype(BF16)


def after_x_kernel(k1, a1, b1, c1, k2, a2, b2, c2, own_ref, s1_ref, s2_ref, s3_ref, acc):
    for start, refs in ((0, (k1, a1, b1, c1)), (FIRST_LANES, (k2, a2, b2, c2))):
        total = refs[0][...]
        for ref in refs[1:]:
            total = total + ref[...].astype(F32)
        for z in range(4):
            acc[z, :, start : start + total.shape[1]] = total[4 * z : 4 * z + 4]
    _, _, z = core_x_z()
    own_ref[...] = acc[z]
    for k, ref in enumerate((s1_ref, s2_ref, s3_ref)):
        ref[...] = acc[(z + k + 1) & 3].astype(BF16)


def after_z_kernel(own_ref, a_ref, b_ref, c_ref, out_ref):
    total = own_ref[...]
    for ref in (a_ref, b_ref, c_ref):
        total = total + ref[...].astype(F32)
    out_ref[...] = total.astype(BF16)


def after_y_kernel(own_ref, a_ref, b_ref, c_ref, out_ref):
    own, a, b, c = (ref[...].astype(F32) for ref in (own_ref, a_ref, b_ref, c_ref))
    out_ref[...] = ((own + b) + (a + c)).astype(BF16)


def final_kernel(own_ref, got_ref, first_ref, second_ref):
    total = own_ref[...].astype(F32) + got_ref[...].astype(F32)
    for ab in range(9):
        block = total[:, ab * 128 : ab * 128 + 128]
        first_ref[3 * ab + 1] = block[:, :64]
        first_ref[3 * ab + 2] = block[:, 64:]
        at = (9 + ab // 2) * 128 + (ab % 2) * 64
        first_ref[3 * ab] = total[:, at : at + 64]
    for tap in range(27):
        at = FIRST_LANES + tap * 128
        second_ref[tap] = total[:, at : at + 128]


def call(kernel, outs, *args, scratch=(), flops=0):
    size = sum(a.size * a.dtype.itemsize for a in args)
    return pl.pallas_call(
        kernel,
        out_shape=[jax.ShapeDtypeStruct(shape, dtype) for shape, dtype in outs],
        in_specs=[pl.BlockSpec(memory_space=pltpu.VMEM)] * len(args),
        out_specs=[pl.BlockSpec(memory_space=pltpu.VMEM)] * len(outs),
        scratch_shapes=[pltpu.VMEM(shape, dtype) for shape, dtype in scratch],
        compiler_params=pltpu.CompilerParams(vmem_limit_bytes=24 << 20),
        cost_estimate=pl.CostEstimate(flops=flops, bytes_accessed=size, transcendentals=0),
    )(*args)


def local(volumes, first_filter, second_filter, upstream_grad):
    slab = volumes.reshape(4, 32, 4096)
    first = first_filter.reshape(9, 192, 128)
    second = second_filter.reshape(27, 128, 128)
    upstream = upstream_grad.reshape(8, 16, 128)
    y_plane = (3, 33, 16, 128)
    w_scratch = ((2304, 128), BF16)

    rim = next_in_space(slab[3], 1)
    y, hidden_up = call(
        upper_plane_kernel,
        [((4,) + y_plane, BF16), ((512, 128), BF16)],
        slab, first, scratch=[w_scratch], flops=6 * 10**8,
    )
    hidden_rim = next_in_space(hidden_up, 1)
    y_rim, hidden_low = call(
        lower_plane_kernel,
        [(y_plane, BF16), ((512, 128), BF16)],
        rim, y, first, scratch=[w_scratch], flops=6 * 10**8,
    )
    second_out, grad_two, taps = call(
        second_conv_kernel,
        [((8, 16, 128), BF16), ((128, 128), BF16), ((128, SECOND_LANES), BF16)],
        hidden_rim, hidden_low, hidden_up, second.reshape(SECOND_LANES, 128), upstream,
        scratch=[((3, 17, 2, 24, 128), F32), ((128, 128), F32), ((128, 128), F32)],
        flops=2 * 10**8,
    )
    grad_two_next = next_in_space(grad_two, -1)
    keep, send = call(
        second_grad_kernel,
        [((64, SECOND_LANES), F32), ((64, SECOND_LANES), BF16)],
        taps, grad_two, scratch=[((128, SECOND_LANES), F32)], flops=4 * 10**8,
    )

    def over_core_and_x(keep, send):
        lanes = keep.shape[1]
        own, *pieces = call(
            after_core_kernel,
            [((16, lanes), F32)] + [((16, lanes), BF16)] * 3,
            keep, swap_core(send), scratch=[((64, lanes), F32)], flops=10**6,
        )
        return [own] + [ring_x(piece, k + 1) for k, piece in enumerate(pieces)]

    second_parts = over_core_and_x(keep, send)
    keep, send = call(
        first_grad_kernel,
        [((64, FIRST_LANES), F32), ((64, FIRST_LANES), BF16)],
        grad_two, grad_two_next, second, hidden_low, hidden_up, y_rim, y,
        scratch=[
            ((2, 17, 16, 128), F32), ((2, 16, 2, 16, 128), F32), ((128, FIRST_LANES), F32),
        ],
        flops=8 * 10**8,
    )
    first_parts = over_core_and_x(keep, send)
    lanes = FIRST_LANES + SECOND_LANES
    own, *pieces = call(
        after_x_kernel,
        [((4, lanes), F32)] + [((4, lanes), BF16)] * 3,
        *first_parts, *second_parts, scratch=[((4, 4, lanes), F32)], flops=10**6,
    )
    (total,) = call(
        after_z_kernel, [((4, lanes), BF16)],
        own, *[ring_z(piece, k + 1) for k, piece in enumerate(pieces)], flops=10**6,
    )
    (total,) = call(
        after_y_kernel, [((4, lanes), BF16)],
        total, *[ring_y(total, k) for k in (1, 2, 3)], flops=10**6,
    )
    first_grad, second_grad = call(
        final_kernel,
        [((27, 4, 64), F32), ((27, 4, 128), F32)],
        total, swap_z_low(total), flops=10**6,
    )
    return (
        second_out.reshape(1, 1, 8, 16, 128),
        jnp.swapaxes(first_grad, 1, 2).reshape(3, 3, 3, 64, 4),
        second_grad.reshape(3, 3, 3, 4, 128),
    )


def solution(mesh):
    placed = (P("dp", "space", None, None), P(), P(), P("dp", "space", None, None, None))
    return jax.shard_map(
        local,
        mesh=mesh,
        in_specs=placed,
        out_specs=(
            P("dp", "space", None, None, None),
            P(None, None, None, None, "space"),
            P(None, None, None, "space", None),
        ),
        check_vma=False,
    )
```

time: 462 us -> 74.3 us (0.16)
  waiting for transfers between devices: 395 us -> 23 us
  starting transfers between devices: 10.1 us -> 36.5 us
  local copies, waits for them, and re-layouts: 28.1 us -> 3.27 us
  between operations: 15.1 us -> 0.77 us
  matrix products: 10.7 us -> 0 us
  Pallas kernels: 0 us -> 10.2 us
    unnamed x3 -> x0, waiting for transfers between devices: 291 us -> none
    psum x1 -> x0, waiting for transfers between devices: 89.6 us -> none  [local(): first_grad, second_grad = lax.psum((first_grad, second_grad), 'dp')]
    ppermute x3 -> x18, starting transfers between devices: 10.1 us -> 36.5 us  [the longest x3 10.9 us: next_in_space(): return lax.ppermute(value, 'space', pairs)]
    conv_general_dilated x5 -> x0, matrix products: 10.7 us -> none  [the longest x2 7.57 us: filter_grad(): lax.conv_general_dilated(extended, out_grads, (1, 1, 1), ((0, 0), (1, 0),...]
    unnamed x27 -> x10, local copies, waits for them, and re-layouts: 12.7 us -> 2.25 us
    pallas_call x0 -> x11, Pallas kernels: none -> 10.2 us  [call(): pl.pallas_call(kernel, out_shape=[jax.ShapeDtypeStruct(shape, dtype) for...]
    ppermute x3 -> x18, waiting for transfers between devices: 15.3 us -> 23 us  [the longest x3 7.74 us: next_in_space(): return lax.ppermute(value, 'space', pairs)]
    concatenate x8 -> x0, local copies, waits for them, and re-layouts: 6.27 us -> none  [the longest x5 5.62 us: local(): volume_ext = jnp.concatenate([lower_rim, volume_view], axis=1)]
  transfers between devices with their start and end apart: 5 -> 18, of which waited for: 4 -> 12; matrix products, arithmetic and copies ran while one was open for 3% -> 0% of each run, Pallas kernels for 0% -> 5%
where the time goes in v1:
time: 74.3 us; the launch traced here: 73.7 us
  starting transfers between devices  36.5 us (49%)
  waiting for transfers between devices  23 us (31%)
  Pallas kernels  10.2 us (14%)
  local copies, waits for them, and re-layouts  3.27 us (4%)
  between operations  0.77 us (1%)
    ppermute x3, starting transfers between devices, next_in_space(): return lax.ppermute(value, 'space', pairs)  10.9 us
    pallas_call x11, Pallas kernels, call(): pl.pallas_call(kernel, out_shape=[jax.ShapeDtypeStruct(shape, dtype) for...  10.2 us
    ppermute x3, starting transfers between devices, ring_z(): lax.ppermute(value, 'space', [(i, i & ~6 | ((i >> 1 & 3) + k) % 4 << 1) f...  8.77 us
    ppermute x6, starting transfers between devices, ring_x(): lax.ppermute(value, 'space', [(i, ((i >> 3) + k) % 4 * 8 + (i & 7)) for i...  8.34 us
    ppermute x3, waiting for transfers between devices, next_in_space(): return lax.ppermute(value, 'space', pairs)  7.74 us
    ppermute x6, waiting for transfers between devices, ring_x(): lax.ppermute(value, 'space', [(i, ((i >> 3) + k) % 4 * 8 + (i & 7)) for i...  4.96 us
    ppermute x3, starting transfers between devices, ring_y(): lax.ppermute(value, 'dp', [(i, i & 4 | ((i & 3) + k) % 4) for i in range(...  4.7 us
    ppermute x3, waiting for transfers between devices, ring_y(): lax.ppermute(value, 'dp', [(i, i & 4 | ((i & 3) + k) % 4) for i in range(...  4.36 us
  transfers between devices with their start and end apart: 18, of which 12 were waited for; matrix products, arithmetic and copies ran while one was open for 0% of the time, Pallas kernels for 5%

profile of v1, /device:TPU:6, one launch (start us, length us, event | category | flops | bytes accessed | tf_op | source)
XLA Modules:
  0.0 73.7 jit_solution(4317839278168325546)
XLA Ops:
  0.6 1.0 %slice_bitcast_fusion = bf16[32,4096]{1,0:T(8,128)(2,1)S(1)} fusion(bf16[1,4,32,4096]{3,2,1,0:T(8,128)(2,1)} %param.4), kind=kLoop, calls=%fused_computation | loop fusion | bytes 524288 | tf_op jit(solution)/shard_map/squeeze | solution.py:261
  1.7 1.9 %collective-permute-start.1 = (bf16[32,4096]{1,0:T(8,128)(2,1)S(1)}, bf16[32,4096]{1,0:T(8,128)(2,1)S(1)}, u32[]{:S(2)}, u32[]{:S(2)}) collective-permute-start(bf16[32,4096]{1,0:T(8,128)(2,1)S(1)} %slice_bitcast_fusion), channel_id=1, source_target_pairs={{0,1},{1,2},{2,3},{3,4},{4,5},{5,6},{6,7},{7,8},{8,9},{9,10},{10,1... | collective-permute-start | bytes 786440 | tf_op jit(solution)/shard_map/ppermute | solution.py:16
  3.6 1.0 %copy-done.1 = bf16[3,3,3,64,128]{4,3,2,1,0:T(8,128)(2,1)S(1)} copy-done((bf16[3,3,3,64,128]{4,3,2,1,0:T(8,128)(2,1)S(1)}, bf16[3,3,3,64,128]{4,3,2,1,0:T(8,128)(2,1)}, u32[]{:S(2)}) %copy-start.1) | copy-done | bytes 442392
  4.6 1.2 %copy-done.3 = bf16[1,4,32,4096]{3,2,1,0:T(8,128)(2,1)S(1)} copy-done((bf16[1,4,32,4096]{3,2,1,0:T(8,128)(2,1)S(1)}, bf16[1,4,32,4096]{3,2,1,0:T(8,128)(2,1)}, u32[]{:S(2)}) %copy-start.3) | copy-done | bytes 1048600
  5.8 1.2 %shard_map.67 = (bf16[4,3,33,16,128]{4,3,2,1,0:T(8,128)(2,1)S(1)}, bf16[512,128]{1,0:T(8,128)(2,1)S(1)}) custom-call(bf16[4,32,4096]{2,1,0:T(8,128)(2,1)S(1)} %bitcast.16, bf16[9,192,128]{2,1,0:T(8,128)(2,1)S(1)} %bitcast.14), custom_call_target="tpu_custom_call" | custom-call | flops 600000000 | bytes 1490944 | tf_op jit(solution)/shard_map/pallas_call | solution.py:242
  7.1 5.4 %collective-permute-start = (bf16[512,128]{1,0:T(8,128)(2,1)S(1)}, bf16[512,128]{1,0:T(8,128)(2,1)S(1)}, u32[]{:S(2)}, u32[]{:S(2)}) collective-permute-start(bf16[512,128]{1,0:T(8,128)(2,1)S(1)} %get-tuple-element.28.h1_ref), channel_id=1, source_target_pairs={{0,1},{1,2},{2,3},{3,4},{4,5},{5,6},{6,7},{7,8},{8,9},{9,10},{10,1... | collective-permute-start | bytes 393224 | tf_op jit(solution)/shard_map/ppermute | solution.py:16
  12.5 1.7 %collective-permute-done.1.v_ref = bf16[32,4096]{1,0:T(8,128)(2,1)S(1)} collective-permute-done((bf16[32,4096]{1,0:T(8,128)(2,1)S(1)}, bf16[32,4096]{1,0:T(8,128)(2,1)S(1)}, u32[]{:S(2)}, u32[]{:S(2)}) %collective-permute-start.1) | collective-permute-done | bytes 262176 | tf_op jit(solution)/shard_map/ppermute | solution.py:16
  14.2 0.9 %shard_map.68 = (bf16[3,33,16,128]{3,2,1,0:T(8,128)(2,1)S(1)}, bf16[512,128]{1,0:T(8,128)(2,1)S(1)}) custom-call(bf16[32,4096]{1,0:T(8,128)(2,1)S(1)} %collective-permute-done.1.v_ref, bf16[4,3,33,16,128]{4,3,2,1,0:T(8,128)(2,1)S(1)} %get-tuple-element.29.y_ref, bf16[9,192,128]{2,1,0:T(8,128)(2,1)S(1)} %bitcast.15), custom_call_target="tpu_custom_call" | custom-call | flops 600000000 | bytes 2326528 | tf_op jit(solution)/shard_map/pallas_call | solution.py:242
  15.2 4.5 %collective-permute-done.hm_ref = bf16[512,128]{1,0:T(8,128)(2,1)S(1)} collective-permute-done((bf16[512,128]{1,0:T(8,128)(2,1)S(1)}, bf16[512,128]{1,0:T(8,128)(2,1)S(1)}, u32[]{:S(2)}, u32[]{:S(2)}) %collective-permute-start) | collective-permute-done | bytes 131104 | tf_op jit(solution)/shard_map/ppermute | solution.py:16
  19.6 1.2 %shard_map.69 = (bf16[8,16,128]{2,1,0:T(8,128)(2,1)}, bf16[128,128]{1,0:T(8,128)(2,1)S(1)}, bf16[128,3456]{1,0:T(8,128)(2,1)S(1)}) custom-call(bf16[512,128]{1,0:T(8,128)(2,1)S(1)} %collective-permute-done.hm_ref, bf16[512,128]{1,0:T(8,128)(2,1)S(1)} %get-tuple-element.30.h0_ref, bf16[512,128]{1,0:T(8,128)(2,1)S(1)} %get-tuple-element.28.h1_ref, ...), custom_call_target="tpu_custom_call" | custom-call | flops 200000000 | bytes 1310720 | tf_op jit(solution)/shard_map/pallas_call | solution.py:242
  20.8 4.2 %shard_map.72 = (f32[64,3456]{1,0:T(8,128)S(1)}, bf16[64,3456]{1,0:T(8,128)(2,1)S(1)}) custom-call(bf16[128,3456]{1,0:T(8,128)(2,1)S(1)} %get-tuple-element.40.t_ref, bf16[128,128]{1,0:T(8,128)(2,1)S(1)} %get-tuple-element.32.gp_ref), custom_call_target="tpu_custom_call" | custom-call | flops 400000000 | bytes 917504 | tf_op jit(solution)/shard_map/pallas_call | solution.py:242
  25.2 3.5 %collective-permute-start.2 = (bf16[128,128]{1,0:T(8,128)(2,1)S(1)}, bf16[128,128]{1,0:T(8,128)(2,1)S(1)}, u32[]{:S(2)}, u32[]{:S(2)}) collective-permute-start(bf16[128,128]{1,0:T(8,128)(2,1)S(1)} %get-tuple-element.32.gp_ref), channel_id=1, source_target_pairs={{1,0},{2,1},{3,2},{4,3},{5,4},{6,5},{7,6},{8,7},{9,8},{10,9},{11,1... | collective-permute-start | bytes 98312 | tf_op jit(solution)/shard_map/ppermute | solution.py:16
  28.7 1.6 %collective-permute-done.2.gpn_ref = bf16[128,128]{1,0:T(8,128)(2,1)S(1)} collective-permute-done((bf16[128,128]{1,0:T(8,128)(2,1)S(1)}, bf16[128,128]{1,0:T(8,128)(2,1)S(1)}, u32[]{:S(2)}, u32[]{:S(2)}) %collective-permute-start.2) | collective-permute-done | bytes 32800 | tf_op jit(solution)/shard_map/ppermute | solution.py:16
  30.3 1.5 %shard_map.70 = (f32[64,1792]{1,0:T(8,128)S(1)}, bf16[64,1792]{1,0:T(8,128)(2,1)S(1)}) custom-call(bf16[128,128]{1,0:T(8,128)(2,1)S(1)} %get-tuple-element.32.gp_ref, bf16[128,128]{1,0:T(8,128)(2,1)S(1)} %collective-permute-done.2.gpn_ref, bf16[27,128,128]{2,1,0:T(8,128)(2,1)S(1)} %bitcast.13, bf16[512,128]{1,0:T(8,128)(2,1)S(1)} %get-tuple-element.30.h0_ref, ...), custom_call_target="tpu_custom_call" | custom-call | flops 800000000 | bytes 3239936 | tf_op jit(solution)/shard_map/pallas_call | solution.py:242
  31.7 1.7 %collective-permute-start.3 = (bf16[64,1792]{1,0:T(8,128)(2,1)S(1)}, bf16[64,1792]{1,0:T(8,128)(2,1)S(1)}, u32[]{:S(2)}, u32[]{:S(2)}) collective-permute-start(bf16[64,1792]{1,0:T(8,128)(2,1)S(1)} %get-tuple-element.35), channel_id=1, source_target_pairs={{0,1},{1,0},{2,3},{3,2},{4,5},{5,4},{6,7},{7,6},{8,9},{9,8},{10,11... | collective-permute-start | bytes 688136 | tf_op jit(solution)/shard_map/ppermute | solution.py:20
  33.4 1.1 %collective-permute-done.3.got_ref = bf16[64,1792]{1,0:T(8,128)(2,1)S(1)} collective-permute-done((bf16[64,1792]{1,0:T(8,128)(2,1)S(1)}, bf16[64,1792]{1,0:T(8,128)(2,1)S(1)}, u32[]{:S(2)}, u32[]{:S(2)}) %collective-permute-start.3) | collective-permute-done | bytes 229408 | tf_op jit(solution)/shard_map/ppermute | solution.py:20
  34.9 1.8 %collective-permute-start.8 = (bf16[16,3456]{1,0:T(8,128)(2,1)S(1)}, bf16[16,3456]{1,0:T(8,128)(2,1)S(1)}, u32[]{:S(2)}, u32[]{:S(2)}) collective-permute-start(bf16[16,3456]{1,0:T(8,128)(2,1)S(1)} %get-tuple-element.44), channel_id=1, source_target_pairs={{0,8},{1,9},{2,10},{3,11},{4,12},{5,13},{6,14},{7,15},{8,16},{9,17... | collective-permute-start | bytes 331784 | tf_op jit(solution)/shard_map/ppermute | solution.py:24
  36.7 2.3 %collective-permute-start.9 = (bf16[16,3456]{1,0:T(8,128)(2,1)S(1)}, bf16[16,3456]{1,0:T(8,128)(2,1)S(1)}, u32[]{:S(2)}, u32[]{:S(2)}) collective-permute-start(bf16[16,3456]{1,0:T(8,128)(2,1)S(1)} %get-tuple-element.45), channel_id=1, source_target_pairs={{0,16},{1,17},{2,18},{3,19},{4,20},{5,21},{6,22},{7,23},{8,24},{9,... | collective-permute-start | bytes 331784 | tf_op jit(solution)/shard_map/ppermute | solution.py:24
  39.1 2.1 %collective-permute-start.5 = (bf16[16,1792]{1,0:T(8,128)(2,1)S(1)}, bf16[16,1792]{1,0:T(8,128)(2,1)S(1)}, u32[]{:S(2)}, u32[]{:S(2)}) collective-permute-start(bf16[16,1792]{1,0:T(8,128)(2,1)S(1)} %get-tuple-element.38), channel_id=1, source_target_pairs={{0,16},{1,17},{2,18},{3,19},{4,20},{5,21},{6,22},{7,23},{8,24},{9,... | collective-permute-start | bytes 172040 | tf_op jit(solution)/shard_map/ppermute | solution.py:24
  41.2 1.9 %collective-permute-start.6 = (bf16[16,1792]{1,0:T(8,128)(2,1)S(1)}, bf16[16,1792]{1,0:T(8,128)(2,1)S(1)}, u32[]{:S(2)}, u32[]{:S(2)}) collective-permute-start(bf16[16,1792]{1,0:T(8,128)(2,1)S(1)} %get-tuple-element.39), channel_id=1, source_target_pairs={{0,24},{1,25},{2,26},{3,27},{4,28},{5,29},{6,30},{7,31},{8,0},{9,1... | collective-permute-start | bytes 172040 | tf_op jit(solution)/shard_map/ppermute | solution.py:24
  43.2 4.2 %collective-permute-done.5.b1 = bf16[16,1792]{1,0:T(8,128)(2,1)S(1)} collective-permute-done((bf16[16,1792]{1,0:T(8,128)(2,1)S(1)}, bf16[16,1792]{1,0:T(8,128)(2,1)S(1)}, u32[]{:S(2)}, u32[]{:S(2)}) %collective-permute-start.5) | collective-permute-done | bytes 57376 | tf_op jit(solution)/shard_map/ppermute | solution.py:24
  47.3 0.8 %collective-permute-done.6.c1 = bf16[16,1792]{1,0:T(8,128)(2,1)S(1)} collective-permute-done((bf16[16,1792]{1,0:T(8,128)(2,1)S(1)}, bf16[16,1792]{1,0:T(8,128)(2,1)S(1)}, u32[]{:S(2)}, u32[]{:S(2)}) %collective-permute-start.6) | collective-permute-done | bytes 57376 | tf_op jit(solution)/shard_map/ppermute | solution.py:24
  48.3 2.4 %collective-permute-start.11 = (bf16[4,5248]{1,0:T(4,128)(2,1)S(1)}, bf16[4,5248]{1,0:T(4,128)(2,1)S(1)}, u32[]{:S(2)}, u32[]{:S(2)}) collective-permute-start(bf16[4,5248]{1,0:T(4,128)(2,1)S(1)} %get-tuple-element.48), channel_id=1, source_target_pairs={{0,2},{1,3},{2,4},{3,5},{4,6},{5,7},{6,0},{7,1},{8,10},{9,11},{10,... | collective-permute-start | bytes 125960 | tf_op jit(solution)/shard_map/ppermute | solution.py:28
  50.7 3.2 %collective-permute-start.12 = (bf16[4,5248]{1,0:T(4,128)(2,1)S(1)}, bf16[4,5248]{1,0:T(4,128)(2,1)S(1)}, u32[]{:S(2)}, u32[]{:S(2)}) collective-permute-start(bf16[4,5248]{1,0:T(4,128)(2,1)S(1)} %get-tuple-element.49), channel_id=1, source_target_pairs={{0,4},{1,5},{2,6},{3,7},{4,0},{5,1},{6,2},{7,3},{8,12},{9,13},{10,... | collective-permute-start | bytes 125960 | tf_op jit(solution)/shard_map/ppermute | solution.py:28
  53.9 3.1 %collective-permute-start.13 = (bf16[4,5248]{1,0:T(4,128)(2,1)S(1)}, bf16[4,5248]{1,0:T(4,128)(2,1)S(1)}, u32[]{:S(2)}, u32[]{:S(2)}) collective-permute-start(bf16[4,5248]{1,0:T(4,128)(2,1)S(1)} %get-tuple-element.50), channel_id=1, source_target_pairs={{0,6},{1,7},{2,0},{3,1},{4,2},{5,3},{6,4},{7,5},{8,14},{9,15},{10,... | collective-permute-start | bytes 125960 | tf_op jit(solution)/shard_map/ppermute | solution.py:28
  57.0 2.0 %collective-permute-done.12.b_ref = bf16[4,5248]{1,0:T(4,128)(2,1)S(1)} collective-permute-done((bf16[4,5248]{1,0:T(4,128)(2,1)S(1)}, bf16[4,5248]{1,0:T(4,128)(2,1)S(1)}, u32[]{:S(2)}, u32[]{:S(2)}) %collective-permute-start.12) | collective-permute-done | bytes 42016 | tf_op jit(solution)/shard_map/ppermute | solution.py:28
  59.0 0.8 %collective-permute-done.13.c_ref = bf16[4,5248]{1,0:T(4,128)(2,1)S(1)} collective-permute-done((bf16[4,5248]{1,0:T(4,128)(2,1)S(1)}, bf16[4,5248]{1,0:T(4,128)(2,1)S(1)}, u32[]{:S(2)}, u32[]{:S(2)}) %collective-permute-start.13) | collective-permute-done | bytes 42016 | tf_op jit(solution)/shard_map/ppermute | solution.py:28
  59.8 3.1 %collective-permute-start.16 = (bf16[4,5248]{1,0:T(4,128)(2,1)S(1)}, bf16[4,5248]{1,0:T(4,128)(2,1)S(1)}, u32[]{:S(2)}, u32[]{:S(2)}) collective-permute-start(bf16[4,5248]{1,0:T(4,128)(2,1)S(1)} %shard_map.75.own_ref), channel_id=1, source_target_pairs={{0,96},{32,0},{64,32},{96,64},{128,224},{160,128},{192,160},{224,1... | collective-permute-start | bytes 125960 | tf_op jit(solution)/shard_map/ppermute | solution.py:34
  63.5 1.0 %collective-permute-start.14 = (bf16[4,5248]{1,0:T(4,128)(2,1)S(1)}, bf16[4,5248]{1,0:T(4,128)(2,1)S(1)}, u32[]{:S(2)}, u32[]{:S(2)}) collective-permute-start(bf16[4,5248]{1,0:T(4,128)(2,1)S(1)} %shard_map.75.own_ref), channel_id=1, source_target_pairs={{0,32},{32,64},{64,96},{96,0},{128,160},{160,192},{192,224},{224,1... | collective-permute-start | bytes 125960 | tf_op jit(solution)/shard_map/ppermute | solution.py:34
  64.6 3.8 %collective-permute-done.15.b_ref = bf16[4,5248]{1,0:T(4,128)(2,1)S(1)} collective-permute-done((bf16[4,5248]{1,0:T(4,128)(2,1)S(1)}, bf16[4,5248]{1,0:T(4,128)(2,1)S(1)}, u32[]{:S(2)}, u32[]{:S(2)}) %collective-permute-start.15) | collective-permute-done | bytes 42016 | tf_op jit(solution)/shard_map/ppermute | solution.py:34
  68.9 2.0 %collective-permute-start.17 = (bf16[4,5248]{1,0:T(4,128)(2,1)S(1)}, bf16[4,5248]{1,0:T(4,128)(2,1)S(1)}, u32[]{:S(2)}, u32[]{:S(2)}) collective-permute-start(bf16[4,5248]{1,0:T(4,128)(2,1)S(1)} %shard_map.76.own_ref), channel_id=1, source_target_pairs={{0,128},{32,160},{64,192},{96,224},{128,0},{160,32},{192,64},{224,... | collective-permute-start | bytes 125960 | tf_op jit(solution)/shard_map/ppermute | solution.py:38
  70.9 2.1 %collective-permute-done.17.got_ref = bf16[4,5248]{1,0:T(4,128)(2,1)S(1)} collective-permute-done((bf16[4,5248]{1,0:T(4,128)(2,1)S(1)}, bf16[4,5248]{1,0:T(4,128)(2,1)S(1)}, u32[]{:S(2)}, u32[]{:S(2)}) %collective-permute-start.17) | collective-permute-done | bytes 42016 | tf_op jit(solution)/shard_map/ppermute | solution.py:38
  (26 shorter events, 2.6 us)
Async XLA Ops:
  0.6 13.6 %copy-start.2 = (bf16[3,3,3,64,128]{4,3,2,1,0:T(8,128)(2,1)S(1)}, bf16[3,3,3,64,128]{4,3,2,1,0:T(8,128)(2,1)}, u32[]{:S(2)}) copy-start(bf16[3,3,3,64,128]{4,3,2,1,0:T(8,128)(2,1)} %param.5) | copy-start | bytes 1327108
  1.7 12.6 %collective-permute-start.1 = (bf16[32,4096]{1,0:T(8,128)(2,1)S(1)}, bf16[32,4096]{1,0:T(8,128)(2,1)S(1)}, u32[]{:S(2)}, u32[]{:S(2)}) collective-permute-start(bf16[32,4096]{1,0:T(8,128)(2,1)S(1)} %slice_bitcast_fusion), channel_id=1, source_target_pairs={{0,1},{1,2},{2,3},{3,4},{4,5},{5,6},{6,7},{7,8},{8,9},{9,10},{10,1... | collective-permute-start | bytes 786440 | tf_op jit(solution)/shard_map/ppermute | solution.py:16
  3.6 1.0 %copy-start.1 = (bf16[3,3,3,64,128]{4,3,2,1,0:T(8,128)(2,1)S(1)}, bf16[3,3,3,64,128]{4,3,2,1,0:T(8,128)(2,1)}, u32[]{:S(2)}) copy-start(bf16[3,3,3,64,128]{4,3,2,1,0:T(8,128)(2,1)} %param.5) | copy-start | bytes 1327108
  4.6 1.2 %copy-start.3 = (bf16[1,4,32,4096]{3,2,1,0:T(8,128)(2,1)S(1)}, bf16[1,4,32,4096]{3,2,1,0:T(8,128)(2,1)}, u32[]{:S(2)}) copy-start(bf16[1,4,32,4096]{3,2,1,0:T(8,128)(2,1)} %param.4) | copy-start | bytes 3145732
  7.1 12.6 %copy-start = (bf16[3,3,3,128,128]{4,3,2,1,0:T(8,128)(2,1)S(1)}, bf16[3,3,3,128,128]{4,3,2,1,0:T(8,128)(2,1)}, u32[]{:S(2)}) copy-start(bf16[3,3,3,128,128]{4,3,2,1,0:T(8,128)(2,1)} %param.6) | copy-start | bytes 2654212
  7.1 12.6 %copy-start.4 = (bf16[1,1,8,16,128]{4,3,2,1,0:T(8,128)(2,1)S(1)}, bf16[1,1,8,16,128]{4,3,2,1,0:T(8,128)(2,1)}, u32[]{:S(2)}) copy-start(bf16[1,1,8,16,128]{4,3,2,1,0:T(8,128)(2,1)} %param.7) | copy-start | bytes 98308
  7.1 12.5 %collective-permute-start = (bf16[512,128]{1,0:T(8,128)(2,1)S(1)}, bf16[512,128]{1,0:T(8,128)(2,1)S(1)}, u32[]{:S(2)}, u32[]{:S(2)}) collective-permute-start(bf16[512,128]{1,0:T(8,128)(2,1)S(1)} %get-tuple-element.28.h1_ref), channel_id=1, source_target_pairs={{0,1},{1,2},{2,3},{3,4},{4,5},{5,6},{6,7},{7,8},{8,9},{9,10},{10,1... | collective-permute-start | bytes 393224 | tf_op jit(solution)/shard_map/ppermute | solution.py:16
  25.1 9.7 %collective-permute-start.7 = (bf16[64,3456]{1,0:T(8,128)(2,1)S(1)}, bf16[64,3456]{1,0:T(8,128)(2,1)S(1)}, u32[]{:S(2)}, u32[]{:S(2)}) collective-permute-start(bf16[64,3456]{1,0:T(8,128)(2,1)S(1)} %get-tuple-element.42), channel_id=1, source_target_pairs={{0,1},{1,0},{2,3},{3,2},{4,5},{5,4},{6,7},{7,6},{8,9},{9,8},{10,11... | collective-permute-start | bytes 1327112 | tf_op jit(solution)/shard_map/ppermute | solution.py:20
  25.2 5.1 %collective-permute-start.2 = (bf16[128,128]{1,0:T(8,128)(2,1)S(1)}, bf16[128,128]{1,0:T(8,128)(2,1)S(1)}, u32[]{:S(2)}, u32[]{:S(2)}) collective-permute-start(bf16[128,128]{1,0:T(8,128)(2,1)S(1)} %get-tuple-element.32.gp_ref), channel_id=1, source_target_pairs={{1,0},{2,1},{3,2},{4,3},{5,4},{6,5},{7,6},{8,7},{9,8},{10,9},{11,1... | collective-permute-start | bytes 98312 | tf_op jit(solution)/shard_map/ppermute | solution.py:16
  31.7 2.8 %collective-permute-start.3 = (bf16[64,1792]{1,0:T(8,128)(2,1)S(1)}, bf16[64,1792]{1,0:T(8,128)(2,1)S(1)}, u32[]{:S(2)}, u32[]{:S(2)}) collective-permute-start(bf16[64,1792]{1,0:T(8,128)(2,1)S(1)} %get-tuple-element.35), channel_id=1, source_target_pairs={{0,1},{1,0},{2,3},{3,2},{4,5},{5,4},{6,7},{7,6},{8,9},{9,8},{10,11... | collective-permute-start | bytes 688136 | tf_op jit(solution)/shard_map/ppermute | solution.py:20
  34.6 6.6 %collective-permute-start.4 = (bf16[16,1792]{1,0:T(8,128)(2,1)S(1)}, bf16[16,1792]{1,0:T(8,128)(2,1)S(1)}, u32[]{:S(2)}, u32[]{:S(2)}) collective-permute-start(bf16[16,1792]{1,0:T(8,128)(2,1)S(1)} %get-tuple-element.37), channel_id=1, source_target_pairs={{0,8},{1,9},{2,10},{3,11},{4,12},{5,13},{6,14},{7,15},{8,16},{9,17... | collective-permute-start | bytes 172040 | tf_op jit(solution)/shard_map/ppermute | solution.py:24
  34.9 13.2 %collective-permute-start.8 = (bf16[16,3456]{1,0:T(8,128)(2,1)S(1)}, bf16[16,3456]{1,0:T(8,128)(2,1)S(1)}, u32[]{:S(2)}, u32[]{:S(2)}) collective-permute-start(bf16[16,3456]{1,0:T(8,128)(2,1)S(1)} %get-tuple-element.44), channel_id=1, source_target_pairs={{0,8},{1,9},{2,10},{3,11},{4,12},{5,13},{6,14},{7,15},{8,16},{9,17... | collective-permute-start | bytes 331784 | tf_op jit(solution)/shard_map/ppermute | solution.py:24
  36.7 11.4 %collective-permute-start.9 = (bf16[16,3456]{1,0:T(8,128)(2,1)S(1)}, bf16[16,3456]{1,0:T(8,128)(2,1)S(1)}, u32[]{:S(2)}, u32[]{:S(2)}) collective-permute-start(bf16[16,3456]{1,0:T(8,128)(2,1)S(1)} %get-tuple-element.45), channel_id=1, source_target_pairs={{0,16},{1,17},{2,18},{3,19},{4,20},{5,21},{6,22},{7,23},{8,24},{9,... | collective-permute-start | bytes 331784 | tf_op jit(solution)/shard_map/ppermute | solution.py:24
  39.1 9.1 %collective-permute-start.10 = (bf16[16,3456]{1,0:T(8,128)(2,1)S(1)}, bf16[16,3456]{1,0:T(8,128)(2,1)S(1)}, u32[]{:S(2)}, u32[]{:S(2)}) collective-permute-start(bf16[16,3456]{1,0:T(8,128)(2,1)S(1)} %get-tuple-element.46), channel_id=1, source_target_pairs={{0,24},{1,25},{2,26},{3,27},{4,28},{5,29},{6,30},{7,31},{8,0},{9,1... | collective-permute-start | bytes 331784 | tf_op jit(solution)/shard_map/ppermute | solution.py:24
  39.1 8.2 %collective-permute-start.5 = (bf16[16,1792]{1,0:T(8,128)(2,1)S(1)}, bf16[16,1792]{1,0:T(8,128)(2,1)S(1)}, u32[]{:S(2)}, u32[]{:S(2)}) collective-permute-start(bf16[16,1792]{1,0:T(8,128)(2,1)S(1)} %get-tuple-element.38), channel_id=1, source_target_pairs={{0,16},{1,17},{2,18},{3,19},{4,20},{5,21},{6,22},{7,23},{8,24},{9,... | collective-permute-start | bytes 172040 | tf_op jit(solution)/shard_map/ppermute | solution.py:24
  41.2 6.9 %collective-permute-start.6 = (bf16[16,1792]{1,0:T(8,128)(2,1)S(1)}, bf16[16,1792]{1,0:T(8,128)(2,1)S(1)}, u32[]{:S(2)}, u32[]{:S(2)}) collective-permute-start(bf16[16,1792]{1,0:T(8,128)(2,1)S(1)} %get-tuple-element.39), channel_id=1, source_target_pairs={{0,24},{1,25},{2,26},{3,27},{4,28},{5,29},{6,30},{7,31},{8,0},{9,1... | collective-permute-start | bytes 172040 | tf_op jit(solution)/shard_map/ppermute | solution.py:24
  48.3 8.8 %collective-permute-start.11 = (bf16[4,5248]{1,0:T(4,128)(2,1)S(1)}, bf16[4,5248]{1,0:T(4,128)(2,1)S(1)}, u32[]{:S(2)}, u32[]{:S(2)}) collective-permute-start(bf16[4,5248]{1,0:T(4,128)(2,1)S(1)} %get-tuple-element.48), channel_id=1, source_target_pairs={{0,2},{1,3},{2,4},{3,5},{4,6},{5,7},{6,0},{7,1},{8,10},{9,11},{10,... | collective-permute-start | bytes 125960 | tf_op jit(solution)/shard_map/ppermute | solution.py:28
  50.7 8.3 %collective-permute-start.12 = (bf16[4,5248]{1,0:T(4,128)(2,1)S(1)}, bf16[4,5248]{1,0:T(4,128)(2,1)S(1)}, u32[]{:S(2)}, u32[]{:S(2)}) collective-permute-start(bf16[4,5248]{1,0:T(4,128)(2,1)S(1)} %get-tuple-element.49), channel_id=1, source_target_pairs={{0,4},{1,5},{2,6},{3,7},{4,0},{5,1},{6,2},{7,3},{8,12},{9,13},{10,... | collective-permute-start | bytes 125960 | tf_op jit(solution)/shard_map/ppermute | solution.py:28
  53.9 5.9 %collective-permute-start.13 = (bf16[4,5248]{1,0:T(4,128)(2,1)S(1)}, bf16[4,5248]{1,0:T(4,128)(2,1)S(1)}, u32[]{:S(2)}, u32[]{:S(2)}) collective-permute-start(bf16[4,5248]{1,0:T(4,128)(2,1)S(1)} %get-tuple-element.50), channel_id=1, source_target_pairs={{0,6},{1,7},{2,0},{3,1},{4,2},{5,3},{6,4},{7,5},{8,14},{9,15},{10,... | collective-permute-start | bytes 125960 | tf_op jit(solution)/shard_map/ppermute | solution.py:28
  59.8 4.8 %collective-permute-start.16 = (bf16[4,5248]{1,0:T(4,128)(2,1)S(1)}, bf16[4,5248]{1,0:T(4,128)(2,1)S(1)}, u32[]{:S(2)}, u32[]{:S(2)}) collective-permute-start(bf16[4,5248]{1,0:T(4,128)(2,1)S(1)} %shard_map.75.own_ref), channel_id=1, source_target_pairs={{0,96},{32,0},{64,32},{96,64},{128,224},{160,128},{192,160},{224,1... | collective-permute-start | bytes 125960 | tf_op jit(solution)/shard_map/ppermute | solution.py:34
  62.9 5.5 %collective-permute-start.15 = (bf16[4,5248]{1,0:T(4,128)(2,1)S(1)}, bf16[4,5248]{1,0:T(4,128)(2,1)S(1)}, u32[]{:S(2)}, u32[]{:S(2)}) collective-permute-start(bf16[4,5248]{1,0:T(4,128)(2,1)S(1)} %shard_map.75.own_ref), channel_id=1, source_target_pairs={{0,64},{32,96},{64,0},{96,32},{128,192},{160,224},{192,128},{224,1... | collective-permute-start | bytes 125960 | tf_op jit(solution)/shard_map/ppermute | solution.py:34
  63.5 5.3 %collective-permute-start.14 = (bf16[4,5248]{1,0:T(4,128)(2,1)S(1)}, bf16[4,5248]{1,0:T(4,128)(2,1)S(1)}, u32[]{:S(2)}, u32[]{:S(2)}) collective-permute-start(bf16[4,5248]{1,0:T(4,128)(2,1)S(1)} %shard_map.75.own_ref), channel_id=1, source_target_pairs={{0,32},{32,64},{64,96},{96,0},{128,160},{160,192},{192,224},{224,1... | collective-permute-start | bytes 125960 | tf_op jit(solution)/shard_map/ppermute | solution.py:34
  68.9 4.1 %collective-permute-start.17 = (bf16[4,5248]{1,0:T(4,128)(2,1)S(1)}, bf16[4,5248]{1,0:T(4,128)(2,1)S(1)}, u32[]{:S(2)}, u32[]{:S(2)}) collective-permute-start(bf16[4,5248]{1,0:T(4,128)(2,1)S(1)} %shard_map.76.own_ref), channel_id=1, source_target_pairs={{0,128},{32,160},{64,192},{96,224},{128,0},{160,32},{192,64},{224,... | collective-permute-start | bytes 125960 | tf_op jit(solution)/shard_map/ppermute | solution.py:38

commit v2 on v1

v2 whole, which is shorter than its diff:
```python
import functools

import jax
import jax.numpy as jnp
from jax import lax
from jax.experimental import pallas as pl
from jax.experimental.pallas import tpu as pltpu
from jax.sharding import PartitionSpec as P

SLOPE = 0.3
F32, BF16 = jnp.float32, jnp.bfloat16
FIRST, SECOND = 14, 27


def around_space(value, by):
    return lax.ppermute(value, "space", [(i, (i + by) % 32) for i in range(32)])


def swap(value, axis, bit):
    size = {"space": 32, "dp": 8}[axis]
    return lax.ppermute(value, axis, [(i, i ^ bit) for i in range(size)])


CORE, X_ONE, X_TWO, Z_ONE, Z_TWO = 1, 8, 24, 2, 6
Y_ONE, Y_TWO, Z_LOW = 1, 3, 4


def leaky(values):
    return jnp.where(values > 0, values, SLOPE * values)


def dot(a, b):
    return jnp.dot(a, b, preferred_element_type=F32)


def dot_nt(a, b):
    return lax.dot_general(a, b, (((1,), (1,)), ((), ())), preferred_element_type=F32)


def rows_by_tap(keep=None):
    m = lax.broadcasted_iota(jnp.int32, (48, 32), 0)
    h = lax.broadcasted_iota(jnp.int32, (48, 32), 1)
    picked = h == 2 * (m & 15) + (m >> 4) - 1
    if keep is not None:
        picked = jnp.logical_and(picked, keep)
    return jnp.where(picked, 1.0, 0.0).astype(BF16)


def channel_order():
    s = lax.axis_index("space")
    m = lax.broadcasted_iota(jnp.int32, (128, 128), 0)
    i = lax.broadcasted_iota(jnp.int32, (128, 128), 1)
    core = (m >> 6) ^ (s & 1)
    x = ((m >> 5) & 1) ^ (3 * ((m >> 4) & 1)) ^ (s >> 3)
    z = ((m >> 3) & 1) ^ (3 * ((m >> 2) & 1)) ^ ((s >> 1) & 3)
    return jnp.where(i == x * 32 + z * 8 + core * 4 + (m & 3), 1.0, 0.0).astype(BF16)


def spread_rows(plane_ref, pick, y_ref):
    for t in range(3):
        y_ref[t, 0] = jnp.zeros((16, 128), BF16)
    for n in range(8):
        out = dot(pick, plane_ref[:, n * 512 : (n + 1) * 512]).astype(BF16)
        for t in range(3):
            for r in range(4):
                y_ref[t, 1 + 4 * n + r] = out[16 * t : 16 * t + 16, 128 * r : 128 * r + 128]


def columns(y_ref, b):
    before = y_ref[b, 0:32].reshape(512, 128)
    at = y_ref[b, 1:33].reshape(512, 128)
    return jnp.concatenate([before, at], axis=1)


def first_conv(planes, f_ref, w_ref):
    for ab in range(9):
        w_ref[ab * 256 : ab * 256 + 64] = jnp.zeros((64, 128), BF16)
        w_ref[ab * 256 + 64 : ab * 256 + 256] = f_ref[ab]
    lhs = jnp.concatenate([columns(planes[a], b) for a in range(3) for b in range(3)], axis=1)
    return leaky(dot(lhs, w_ref[...])).astype(BF16)


def rim_kernel(v_ref, rim_ref, sems):
    copies = [
        pltpu.make_async_copy(
            v_ref.at[3, 8 * k : 8 * k + 8], rim_ref.at[8 * k : 8 * k + 8], sems.at[k]
        )
        for k in range(4)
    ]
    for copy in copies:
        copy.start()
    for copy in copies:
        copy.wait()


def upper_plane_kernel(v_ref, f_ref, y_ref, hid_ref, v, f, w_ref, sems):
    copies = [pltpu.make_async_copy(v_ref.at[p + 1], v.at[p], sems.at[p]) for p in range(3)]
    copies.append(pltpu.make_async_copy(f_ref, f, sems.at[3]))
    for copy in copies:
        copy.start()
    pick = rows_by_tap()
    for p in range(3):
        copies[p].wait()
        spread_rows(v.at[p], pick, y_ref.at[p])
    copies[3].wait()
    hid_ref[...] = first_conv([y_ref.at[p] for p in range(3)], f, w_ref)


def lower_plane_kernel(rim_ref, v_ref, y_ref, f_ref, yl_ref, hid_ref, v, w_ref, sems):
    copy = pltpu.make_async_copy(v_ref.at[0], v, sems.at[0])
    copy.start()
    copy.wait()
    spread_rows(v, rows_by_tap(), yl_ref.at[1])
    spread_rows(rim_ref, rows_by_tap(lax.axis_index("space") > 0), yl_ref.at[0])
    hid_ref[...] = first_conv([yl_ref.at[0], yl_ref.at[1], y_ref.at[0]], f_ref, w_ref)


def second_conv_kernel(hm_ref, h0_ref, h1_ref, f_ref, up_ref, out_ref, gp_ref, t_ref, hs, us, os):
    inside = jnp.where(lax.axis_index("space") > 0, 1.0, 0.0)
    for a, h_ref in enumerate((hm_ref, h0_ref, h1_ref)):
        h = h_ref[...].astype(F32).reshape(16, 2, 16, 128)
        if a == 0:
            h = h * inside
        hs[a, :, :, 0:8, :] = jnp.zeros((17, 2, 8, 128), F32)
        hs[a, 0, 0] = jnp.zeros((24, 128), F32)
        hs[a, 0:16, 1, 8:24, :] = h[:, 0]
        hs[a, 1:17, 0, 8:24, :] = h[:, 1]
    taps = []
    for a in range(3):
        for b in range(3):
            for c in range(3):
                rows = hs[a, c // 2 : c // 2 + 16, c % 2, pl.ds(7 + b, 8, stride=2), :]
                taps.append(rows.reshape(128, 128).astype(BF16))
                t_ref[len(taps) * 128 - 128 : len(taps) * 128] = taps[-1]
    pre = dot(jnp.concatenate(taps, axis=1), f_ref[...])
    us[...] = up_ref[...].astype(F32).reshape(128, 128)
    up = jnp.concatenate([us[pl.ds(r, 8, stride=16), :] for r in range(16)], axis=0)
    gp_ref[...] = (up * jnp.where(pre > 0, 1.0, SLOPE)).astype(BF16)
    out = leaky(pre)
    for r in range(16):
        os[pl.ds(r, 8, stride=16), :] = out[8 * r : 8 * r + 8]
    out_ref[...] = os[...].astype(BF16).reshape(8, 16, 128)


def second_grad_kernel(t_ref, gp_ref, keep_ref, send_ref):
    turned = dot_nt(channel_order(), t_ref[...]).astype(BF16)
    gp = gp_ref[...]
    for start in range(0, SECOND, 9):
        lhs = [turned[:, tap * 128 : tap * 128 + 128] for tap in range(start, start + 9)]
        grad = dot(jnp.concatenate(lhs, axis=0), gp).reshape(9, 128, 128)
        keep_ref[start : start + 9] = grad[:, :64]
        send_ref[start : start + 9] = grad[:, 64:].astype(BF16)


def first_grad_kernel(
    gp_ref, gpn_ref, f_ref, h0_ref, h1_ref, yl_ref, y_ref, keep_ref, send_ref, gs, gu
):
    inside = jnp.where(lax.axis_index("space") < 31, 1.0, 0.0)
    gs[...] = jnp.zeros_like(gs)
    gs[0, 0:16, 0:8, :] = gp_ref[...].astype(F32).reshape(16, 8, 128)
    gs[1, 0:16, 0:8, :] = gpn_ref[...].astype(F32).reshape(16, 8, 128) * inside
    moved = {
        (s, dr, dq): gs[s, dr : dr + 16, dq : dq + 8, :].reshape(128, 128).astype(BF16)
        for s in range(2)
        for dr in range(2)
        for dq in range(2)
    }
    one_d = {0: [(0, 1)], 1: [(0, 2), (1, 0)]}
    for pu in range(2):
        for pv in range(2):
            for pw in range(2):
                lhs, rhs = [], []
                for s, a in one_d[pu]:
                    for dq, b in one_d[pv]:
                        for dr, c in one_d[pw]:
                            lhs.append(moved[s, dr, dq])
                            rhs.append(f_ref[9 * a + 3 * b + c])
                grad = dot_nt(jnp.concatenate(lhs, axis=1), jnp.concatenate(rhs, axis=1))
                grad = grad.astype(BF16).astype(F32).reshape(16, 8, 128)
                gu[pu, :, pw, pl.ds(pv, 8, stride=2), :] = grad
    grads = []
    for pu, h_ref in enumerate((h0_ref, h1_ref)):
        hid = h_ref[...].astype(F32)
        grads.append((gu[pu].reshape(512, 128) * jnp.where(hid > 0, 1.0, SLOPE)).astype(BF16))
    turned = dot_nt(channel_order(), jnp.concatenate(grads, axis=0)).astype(BF16)
    planes = [yl_ref.at[0], yl_ref.at[1]] + [y_ref.at[p] for p in range(3)]
    low = lax.broadcasted_iota(jnp.int32, (128, 128), 1) < 64

    def put(block, grad):
        keep_ref[block] = grad[:64]
        send_ref[block] = grad[64:].astype(BF16)

    held = None
    for a in range(3):
        for b in range(3):
            ab = 3 * a + b
            rhs = jnp.concatenate([columns(planes[a], b), columns(planes[a + 2], b)], axis=0)
            grad = dot(turned, rhs)
            put(ab, grad[:, 128:])
            if ab % 2 == 0:
                held = pltpu.roll(grad[:, :128], 64, axis=1)
            if ab % 2 == 1 or ab == 8:
                upper = grad[:, :128] if ab % 2 else jnp.zeros_like(held)
                put(9 + ab // 2, jnp.where(low, held, upper))


def fold_kernel(groups, *refs):
    count = 2 * sum(groups)
    ins, outs = list(refs[:count]), list(refs[count:])
    for parts in groups:
        keep_ref, send_ref = outs.pop(0), outs.pop(0)
        at = 0
        for _ in range(parts):
            own_ref, got_ref = ins.pop(0), ins.pop(0)
            total = own_ref[...] + got_ref[...].astype(F32)
            blocks, rows, _ = total.shape
            keep_ref[at : at + blocks] = total[:, : rows // 2]
            send_ref[at : at + blocks] = total[:, rows // 2 :].astype(BF16)
            at += blocks


def sum_kernel(*refs):
    *ins, out_ref = refs
    at = 0
    for own_ref, got_ref in zip(ins[::2], ins[1::2]):
        total = own_ref[...].astype(F32) + got_ref[...].astype(F32)
        out_ref[at : at + total.shape[0]] = total.astype(BF16)
        at += total.shape[0]


def final_kernel(own_ref, got_ref, first_ref, second_ref):
    total = own_ref[...].astype(F32) + got_ref[...].astype(F32)
    for ab in range(9):
        first_ref[3 * ab + 1] = total[ab, :, :64]
        first_ref[3 * ab + 2] = total[ab, :, 64:]
        at = (ab % 2) * 64
        first_ref[3 * ab] = total[9 + ab // 2, :, at : at + 64]
    second_ref[...] = total[FIRST:]


VMEM, HBM = pltpu.VMEM, pltpu.HBM


def call(kernel, outs, *args, scratch=(), spaces=None, flops=10**6, vmem=24 << 20):
    size = sum(a.size * a.dtype.itemsize for a in args)
    spaces = spaces or [VMEM] * len(args)
    return pl.pallas_call(
        kernel,
        out_shape=[jax.ShapeDtypeStruct(shape, dtype) for shape, dtype in outs],
        in_specs=[pl.BlockSpec(memory_space=space) for space in spaces],
        out_specs=[pl.BlockSpec(memory_space=VMEM)] * len(outs),
        scratch_shapes=[pltpu.VMEM(*s) if isinstance(s, tuple) else s for s in scratch],
        compiler_params=pltpu.CompilerParams(vmem_limit_bytes=vmem),
        cost_estimate=pl.CostEstimate(flops=flops, bytes_accessed=size, transcendentals=0),
    )(*args)


def fold(*groups):
    outs, args = [], []
    for group in groups:
        blocks = sum(own.shape[0] for own, _ in group)
        half = (blocks, group[0][0].shape[1] // 2, 128)
        outs += [(half, F32), (half, BF16)]
        args += [array for pair in group for array in pair]
    kernel = functools.partial(fold_kernel, [len(group) for group in groups])
    done = call(kernel, outs, *args)
    return list(zip(done[::2], done[1::2]))


def local(volumes, first_filter, second_filter, upstream_grad):
    slab = volumes.reshape(4, 32, 4096)
    first = first_filter.reshape(9, 192, 128)
    second = second_filter.reshape(27, 128, 128)
    upstream = upstream_grad.reshape(8, 16, 128)
    y_plane = (3, 33, 16, 128)
    w_scratch = ((2304, 128), BF16)
    dma = pltpu.SemaphoreType.DMA((4,))

    (rim,) = call(rim_kernel, [((32, 4096), BF16)], slab, spaces=[HBM], scratch=[dma], vmem=60 << 20)
    rim = around_space(rim, 1)
    y, hidden_up = call(
        upper_plane_kernel,
        [((3,) + y_plane, BF16), ((512, 128), BF16)],
        slab, first, spaces=[HBM, HBM],
        scratch=[((3, 32, 4096), BF16), ((9, 192, 128), BF16), w_scratch, dma], flops=6 * 10**8,
    )
    hidden_rim = around_space(hidden_up, 1)
    y_low, hidden_low = call(
        lower_plane_kernel,
        [((2,) + y_plane, BF16), ((512, 128), BF16)],
        rim, slab, y, first, spaces=[VMEM, HBM, VMEM, VMEM],
        scratch=[((32, 4096), BF16), w_scratch, dma], flops=6 * 10**8,
    )
    second_out, grad_two, taps = call(
        second_conv_kernel,
        [((8, 16, 128), BF16), ((128, 128), BF16), ((SECOND * 128, 128), BF16)],
        hidden_rim, hidden_low, hidden_up, second.reshape(SECOND * 128, 128), upstream,
        scratch=[((3, 17, 2, 24, 128), F32), ((128, 128), F32), ((128, 128), F32)],
        flops=2 * 10**8,
    )
    grad_two_next = around_space(grad_two, -1)
    keep2, send2 = call(
        second_grad_kernel,
        [((SECOND, 64, 128), F32), ((SECOND, 64, 128), BF16)],
        taps, grad_two, flops=4 * 10**8,
    )
    send2, grad_two_next = lax.optimization_barrier((send2, grad_two_next))
    keep1, send1 = call(
        first_grad_kernel,
        [((FIRST, 64, 128), F32), ((FIRST, 64, 128), BF16)],
        grad_two, grad_two_next, second, hidden_low, hidden_up, y_low, y,
        scratch=[((2, 17, 16, 128), F32), ((2, 16, 2, 16, 128), F32)], flops=8 * 10**8,
    )
    s = "space"
    got2, got1 = swap(send2, s, CORE), swap(send1, s, CORE)
    ((keep, send),) = fold([(keep1, got1), (keep2, got2)])
    for bit in (X_ONE, X_TWO, Z_ONE):
        ((keep, send),) = fold([(keep, swap(send, s, bit))])
    total = ((FIRST + SECOND, 4, 128), BF16)
    (both,) = call(sum_kernel, [total], keep, swap(send, s, Z_TWO))
    (both,) = call(sum_kernel, [total], both, swap(both, "dp", Y_ONE))
    (both,) = call(sum_kernel, [total], both, swap(both, "dp", Y_TWO))
    first_grad, second_grad = call(
        final_kernel,
        [((27, 4, 64), F32), ((27, 4, 128), F32)],
        both, swap(both, "dp", Z_LOW),
    )
    return (
        second_out.reshape(1, 1, 8, 16, 128),
        jnp.swapaxes(first_grad, 1, 2).reshape(3, 3, 3, 64, 4),
        second_grad.reshape(3, 3, 3, 4, 128),
    )


def solution(mesh):
    placed = (P("dp", "space", None, None), P(), P(), P("dp", "space", None, None, None))
    return jax.shard_map(
        local,
        mesh=mesh,
        in_specs=placed,
        out_specs=(
            P("dp", "space", None, None, None),
            P(None, None, None, None, "space"),
            P(None, None, None, "space", None),
        ),
        check_vma=False,
    )
```

time: 74.3 us -> 70.7 us (0.952)
  starting transfers between devices: 36.5 us -> 21.6 us
  waiting for transfers between devices: 23 us -> 37.4 us
  local copies, waits for them, and re-layouts: 3.27 us -> 1.02 us
  Pallas kernels: 10.2 us -> 8.93 us
    ppermute x18 -> x12, starting transfers between devices: 36.5 us -> 21.6 us  [the longest x9 18.1 us: swap(): return lax.ppermute(value, axis, [(i, i ^ bit) for i in range(size)])]
    ppermute x18 -> x12, waiting for transfers between devices: 23 us -> 37.4 us  [the longest x9 30.7 us: swap(): return lax.ppermute(value, axis, [(i, i ^ bit) for i in range(size)])]
    pallas_call x11 -> x14, Pallas kernels: 10.2 us -> 8.93 us  [call(): pl.pallas_call(kernel, out_shape=[jax.ShapeDtypeStruct(shape, dtype) for...]
    unnamed x10 -> x8, local copies, waits for them, and re-layouts: 2.25 us -> 1.02 us
    squeeze x1 -> x0, local copies, waits for them, and re-layouts: 1.02 us -> none  [local(): rim = next_in_space(slab[3], 1)]
  transfers between devices with their start and end apart: 18 -> 12, of which waited for: 12 -> 11; matrix products, arithmetic and copies ran while one was open for 0% -> 0% of each run, Pallas kernels for 5% -> 7%
where the time goes in v2:
time: 70.7 us; the launch traced here: 69.6 us
  waiting for transfers between devices  37.4 us (53%)
  starting transfers between devices  21.6 us (31%)
  Pallas kernels  8.93 us (13%)
  local copies, waits for them, and re-layouts  1.02 us (1%)
  between operations  0.74 us (1%)
    ppermute x9, waiting for transfers between devices, swap(): return lax.ppermute(value, axis, [(i, i ^ bit) for i in range(size)])  30.7 us
    ppermute x9, starting transfers between devices, swap(): return lax.ppermute(value, axis, [(i, i ^ bit) for i in range(size)])  18.1 us
    pallas_call x14, Pallas kernels, call(): pl.pallas_call(kernel, out_shape=[jax.ShapeDtypeStruct(shape, dtype) for...  8.93 us
    ppermute x3, waiting for transfers between devices, around_space(): return lax.ppermute(value, 'space', [(i, (i + by) % 32) for i in range(32)])  6.66 us
    ppermute x3, starting transfers between devices, around_space(): return lax.ppermute(value, 'space', [(i, (i + by) % 32) for i in range(32)])  3.53 us
  transfers between devices with their start and end apart: 12, of which 11 were waited for; matrix products, arithmetic and copies ran while one was open for 0% of the time, Pallas kernels for 7%

profile of v2, /device:TPU:6, one launch (start us, length us, event | category | flops | bytes accessed | tf_op | source)
XLA Modules:
  0.0 69.6 jit_solution(146019199929074362)
XLA Ops:
  0.6 1.8 %shard_map.68 = bf16[32,4096]{1,0:T(8,128)(2,1)} custom-call(bf16[4,32,4096]{2,1,0:T(8,128)(2,1)} %bitcast.10), custom_call_target="tpu_custom_call" | custom-call | flops 1000000 | bytes 1048576 | tf_op jit(solution)/shard_map/pallas_call | solution.py:247
  2.4 0.1 collective-permute-start.1
  2.5 0.0 copy-start.2
  2.5 1.0 %copy-done.2 = bf16[3,3,3,64,128]{4,3,2,1,0:T(8,128)(2,1)S(1)} copy-done((bf16[3,3,3,64,128]{4,3,2,1,0:T(8,128)(2,1)S(1)}, bf16[3,3,3,64,128]{4,3,2,1,0:T(8,128)(2,1)}, u32[]{:S(2)}) %copy-start.2) | copy-done | bytes 442392
  3.5 1.9 %shard_map.67 = (bf16[3,3,33,16,128]{4,3,2,1,0:T(8,128)(2,1)S(1)}, bf16[512,128]{1,0:T(8,128)(2,1)S(1)}) custom-call(bf16[4,32,4096]{2,1,0:T(8,128)(2,1)S(1)} %bitcast.11, bf16[9,192,128]{2,1,0:T(8,128)(2,1)S(1)} %bitcast.15), custom_call_target="tpu_custom_call" | custom-call | flops 600000000 | bytes 1490944 | tf_op jit(solution)/shard_map/pallas_call | solution.py:247
  5.5 3.4 %collective-permute-start = (bf16[512,128]{1,0:T(8,128)(2,1)S(1)}, bf16[512,128]{1,0:T(8,128)(2,1)S(1)}, u32[]{:S(2)}, u32[]{:S(2)}) collective-permute-start(bf16[512,128]{1,0:T(8,128)(2,1)S(1)} %get-tuple-element.26.h1_ref), channel_id=1, source_target_pairs={{0,1},{1,2},{2,3},{3,4},{4,5},{5,6},{6,7},{7,8},{8,9},{9,10},{10,1... | collective-permute-start | bytes 393224 | tf_op jit(solution)/shard_map/ppermute | solution.py:16
  8.9 4.5 %collective-permute-done.1.rim_ref = bf16[32,4096]{1,0:T(8,128)(2,1)S(1)} collective-permute-done((bf16[32,4096]{1,0:T(8,128)(2,1)}, bf16[32,4096]{1,0:T(8,128)(2,1)S(1)}, u32[]{:S(2)}, u32[]{:S(2)}) %collective-permute-start.1) | collective-permute-done | bytes 262176 | tf_op jit(solution)/shard_map/ppermute | solution.py:16
  13.4 1.1 %shard_map.69 = (bf16[2,3,33,16,128]{4,3,2,1,0:T(8,128)(2,1)S(1)}, bf16[512,128]{1,0:T(8,128)(2,1)S(1)}) custom-call(bf16[32,4096]{1,0:T(8,128)(2,1)S(1)} %collective-permute-done.1.rim_ref, bf16[4,32,4096]{2,1,0:T(8,128)(2,1)S(1)} %bitcast.12, bf16[3,3,33,16,128]{4,3,2,1,0:T(8,128)(2,1)S(1)} %get-tuple-element.27.y_ref, bf16[9,192,128]{2,1,0:T(8,128)(2,1)S(1)} %bitcast.16), custom_call_target="tpu_custom_call" | custom-call | flops 600000000 | bytes 2969600 | tf_op jit(solution)/shard_map/pallas_call | solution.py:247
  14.5 1.2 %collective-permute-done.hm_ref = bf16[512,128]{1,0:T(8,128)(2,1)S(1)} collective-permute-done((bf16[512,128]{1,0:T(8,128)(2,1)S(1)}, bf16[512,128]{1,0:T(8,128)(2,1)S(1)}, u32[]{:S(2)}, u32[]{:S(2)}) %collective-permute-start) | collective-permute-done | bytes 131104 | tf_op jit(solution)/shard_map/ppermute | solution.py:16
  15.7 1.1 %shard_map.70 = (bf16[8,16,128]{2,1,0:T(8,128)(2,1)}, bf16[128,128]{1,0:T(8,128)(2,1)S(1)}, bf16[3456,128]{1,0:T(8,128)(2,1)S(1)}) custom-call(bf16[512,128]{1,0:T(8,128)(2,1)S(1)} %collective-permute-done.hm_ref, bf16[512,128]{1,0:T(8,128)(2,1)S(1)} %get-tuple-element.28.h0_ref, bf16[512,128]{1,0:T(8,128)(2,1)S(1)} %get-tuple-element.26.h1_ref, ...), custom_call_target="tpu_custom_call" | custom-call | flops 200000000 | bytes 1310720 | tf_op jit(solution)/shard_map/pallas_call | solution.py:247
  16.8 0.6 shard_map.71
  17.5 1.0 %collective-permute-done.2.gpn_ref = bf16[128,128]{1,0:T(8,128)(2,1)S(1)} collective-permute-done((bf16[128,128]{1,0:T(8,128)(2,1)S(1)}, bf16[128,128]{1,0:T(8,128)(2,1)S(1)}, u32[]{:S(2)}, u32[]{:S(2)}) %collective-permute-start.2) | collective-permute-done | bytes 32800 | tf_op jit(solution)/shard_map/ppermute | solution.py:16
  18.4 1.3 %shard_map.72 = (f32[14,64,128]{2,1,0:T(8,128)S(1)}, bf16[14,64,128]{2,1,0:T(8,128)(2,1)S(1)}) custom-call(bf16[128,128]{1,0:T(8,128)(2,1)S(1)} %get-tuple-element.30.gp_ref, bf16[128,128]{1,0:T(8,128)(2,1)S(1)} %collective-permute-done.2.gpn_ref, bf16[27,128,128]{2,1,0:T(8,128)(2,1)S(1)} %bitcast.14, bf16[512,128]{1,0:T(8,128)(2,1)S(1)} %get-tuple-element.28.h0_ref, ...), custom_call_target="tpu_custom_call" | custom-call | flops 800000000 | bytes 3239936 | tf_op jit(solution)/shard_map/pallas_call | solution.py:247
  19.8 0.6 collective-permute-start.3
  20.4 1.1 %collective-permute-done.3.refs_1_ = bf16[14,64,128]{2,1,0:T(8,128)(2,1)S(1)} collective-permute-done((bf16[14,64,128]{2,1,0:T(8,128)(2,1)S(1)}, bf16[14,64,128]{2,1,0:T(8,128)(2,1)S(1)}, u32[]{:S(2)}, u32[]{:S(2)}) %collective-permute-start.3) | collective-permute-done | bytes 229408 | tf_op jit(solution)/shard_map/ppermute | solution.py:21
  21.5 0.1 shard_map.73
  21.6 0.6 collective-permute-start.5
  22.3 9.6 %collective-permute-done.5.refs_1_ = bf16[41,32,128]{2,1,0:T(8,128)(2,1)S(1)} collective-permute-done((bf16[41,32,128]{2,1,0:T(8,128)(2,1)S(1)}, bf16[41,32,128]{2,1,0:T(8,128)(2,1)S(1)}, u32[]{:S(2)}, u32[]{:S(2)}) %collective-permute-start.5) | collective-permute-done | bytes 335904 | tf_op jit(solution)/shard_map/ppermute | solution.py:21
  31.9 0.1 shard_map.74
  32.0 2.5 %collective-permute-start.6 = (bf16[41,16,128]{2,1,0:T(8,128)(2,1)S(1)}, bf16[41,16,128]{2,1,0:T(8,128)(2,1)S(1)}, u32[]{:S(2)}, u32[]{:S(2)}) collective-permute-start(bf16[41,16,128]{2,1,0:T(8,128)(2,1)S(1)} %get-tuple-element.42), channel_id=1, source_target_pairs={{0,24},{1,25},{2,26},{3,27},{4,28},{5,29},{6,30},{7,31},{8,16},{9,... | collective-permute-start | bytes 503816 | tf_op jit(solution)/shard_map/ppermute | solution.py:21
  34.4 4.6 %collective-permute-done.6.refs_1_ = bf16[41,16,128]{2,1,0:T(8,128)(2,1)S(1)} collective-permute-done((bf16[41,16,128]{2,1,0:T(8,128)(2,1)S(1)}, bf16[41,16,128]{2,1,0:T(8,128)(2,1)S(1)}, u32[]{:S(2)}, u32[]{:S(2)}) %collective-permute-start.6) | collective-permute-done | bytes 167968 | tf_op jit(solution)/shard_map/ppermute | solution.py:21
  39.0 7.6 %collective-permute-start.7 = (bf16[41,8,128]{2,1,0:T(8,128)(2,1)S(1)}, bf16[41,8,128]{2,1,0:T(8,128)(2,1)S(1)}, u32[]{:S(2)}, u32[]{:S(2)}) collective-permute-start(bf16[41,8,128]{2,1,0:T(8,128)(2,1)S(1)} %get-tuple-element.44), channel_id=1, source_target_pairs={{0,2},{1,3},{2,0},{3,1},{4,6},{5,7},{6,4},{7,5},{8,10},{9,11},{10,... | collective-permute-start | bytes 251912 | tf_op jit(solution)/shard_map/ppermute | solution.py:21
  46.6 2.4 %collective-permute-done.7.refs_1_ = bf16[41,8,128]{2,1,0:T(8,128)(2,1)S(1)} collective-permute-done((bf16[41,8,128]{2,1,0:T(8,128)(2,1)S(1)}, bf16[41,8,128]{2,1,0:T(8,128)(2,1)S(1)}, u32[]{:S(2)}, u32[]{:S(2)}) %collective-permute-start.7) | collective-permute-done | bytes 84000 | tf_op jit(solution)/shard_map/ppermute | solution.py:21
  49.1 1.5 %collective-permute-start.8 = (bf16[41,4,128]{2,1,0:T(4,128)(2,1)S(1)}, bf16[41,4,128]{2,1,0:T(4,128)(2,1)S(1)}, u32[]{:S(2)}, u32[]{:S(2)}) collective-permute-start(bf16[41,4,128]{2,1,0:T(4,128)(2,1)S(1)} %get-tuple-element.46), channel_id=1, source_target_pairs={{0,6},{1,7},{2,4},{3,5},{4,2},{5,3},{6,0},{7,1},{8,14},{9,15},{10,... | collective-permute-start | bytes 125960 | tf_op jit(solution)/shard_map/ppermute | solution.py:21
  50.6 4.8 %collective-permute-done.8.refs_1_ = bf16[41,4,128]{2,1,0:T(4,128)(2,1)S(1)} collective-permute-done((bf16[41,4,128]{2,1,0:T(4,128)(2,1)S(1)}, bf16[41,4,128]{2,1,0:T(4,128)(2,1)S(1)}, u32[]{:S(2)}, u32[]{:S(2)}) %collective-permute-start.8) | collective-permute-done | bytes 42016 | tf_op jit(solution)/shard_map/ppermute | solution.py:21
  55.4 1.7 %collective-permute-start.9 = (bf16[41,4,128]{2,1,0:T(4,128)(2,1)S(1)}, bf16[41,4,128]{2,1,0:T(4,128)(2,1)S(1)}, u32[]{:S(2)}, u32[]{:S(2)}) collective-permute-start(bf16[41,4,128]{2,1,0:T(4,128)(2,1)S(1)} %shard_map.77.refs_0_), channel_id=1, source_target_pairs={{0,32},{32,0},{64,96},{96,64},{128,160},{160,128},{192,224},{224,1... | collective-permute-start | bytes 125960 | tf_op jit(solution)/shard_map/ppermute | solution.py:21
  57.0 2.4 %collective-permute-done.9.refs_1_ = bf16[41,4,128]{2,1,0:T(4,128)(2,1)S(1)} collective-permute-done((bf16[41,4,128]{2,1,0:T(4,128)(2,1)S(1)}, bf16[41,4,128]{2,1,0:T(4,128)(2,1)S(1)}, u32[]{:S(2)}, u32[]{:S(2)}) %collective-permute-start.9) | collective-permute-done | bytes 42016 | tf_op jit(solution)/shard_map/ppermute | solution.py:21
  59.5 3.1 %collective-permute-start.10 = (bf16[41,4,128]{2,1,0:T(4,128)(2,1)S(1)}, bf16[41,4,128]{2,1,0:T(4,128)(2,1)S(1)}, u32[]{:S(2)}, u32[]{:S(2)}) collective-permute-start(bf16[41,4,128]{2,1,0:T(4,128)(2,1)S(1)} %shard_map.78.refs_0_), channel_id=1, source_target_pairs={{0,96},{32,64},{64,32},{96,0},{128,224},{160,192},{192,160},{224,1... | collective-permute-start | bytes 125960 | tf_op jit(solution)/shard_map/ppermute | solution.py:21
  62.6 2.2 %collective-permute-done.10.refs_1_ = bf16[41,4,128]{2,1,0:T(4,128)(2,1)S(1)} collective-permute-done((bf16[41,4,128]{2,1,0:T(4,128)(2,1)S(1)}, bf16[41,4,128]{2,1,0:T(4,128)(2,1)S(1)}, u32[]{:S(2)}, u32[]{:S(2)}) %collective-permute-start.10) | collective-permute-done | bytes 42016 | tf_op jit(solution)/shard_map/ppermute | solution.py:21
  64.8 0.5 collective-permute-start.11
  65.4 3.6 %collective-permute-done.11.got_ref = bf16[41,4,128]{2,1,0:T(4,128)(2,1)S(1)} collective-permute-done((bf16[41,4,128]{2,1,0:T(4,128)(2,1)S(1)}, bf16[41,4,128]{2,1,0:T(4,128)(2,1)S(1)}, u32[]{:S(2)}, u32[]{:S(2)}) %collective-permute-start.11) | collective-permute-done | bytes 42016 | tf_op jit(solution)/shard_map/ppermute | solution.py:21
  68.9 0.7 %shard_map.80 = (f32[27,4,64]{2,1,0:T(4,128)}, f32[27,4,128]{2,1,0:T(4,128)}) custom-call(bf16[41,4,128]{2,1,0:T(4,128)(2,1)S(1)} %shard_map.79.own_ref, bf16[41,4,128]{2,1,0:T(4,128)(2,1)S(1)} %collective-permute-done.11.got_ref), custom_call_target="tpu_custom_call" | custom-call | flops 1000000 | bytes 83968 | tf_op jit(solution)/shard_map/pallas_call | solution.py:247
  (14 shorter events, 0.2 us)
Async XLA Ops:
  0.6 1.9 %copy-start = (bf16[1,4,32,4096]{3,2,1,0:T(8,128)(2,1)S(1)}, bf16[1,4,32,4096]{3,2,1,0:T(8,128)(2,1)}, u32[]{:S(2)}) copy-start(bf16[1,4,32,4096]{3,2,1,0:T(8,128)(2,1)} %param.4) | copy-start | bytes 3145732
  2.4 10.9 %collective-permute-start.1 = (bf16[32,4096]{1,0:T(8,128)(2,1)}, bf16[32,4096]{1,0:T(8,128)(2,1)S(1)}, u32[]{:S(2)}, u32[]{:S(2)}) collective-permute-start(bf16[32,4096]{1,0:T(8,128)(2,1)} %shard_map.68), channel_id=1, source_target_pairs={{0,1},{1,2},{2,3},{3,4},{4,5},{5,6},{6,7},{7,8},{8,9},{9,10},{10,1... | collective-permute-start | bytes 786440 | tf_op jit(solution)/shard_map/ppermute | solution.py:16
  2.5 1.0 %copy-start.2 = (bf16[3,3,3,64,128]{4,3,2,1,0:T(8,128)(2,1)S(1)}, bf16[3,3,3,64,128]{4,3,2,1,0:T(8,128)(2,1)}, u32[]{:S(2)}) copy-start(bf16[3,3,3,64,128]{4,3,2,1,0:T(8,128)(2,1)} %param.5) | copy-start | bytes 1327108
  5.5 10.3 %collective-permute-start = (bf16[512,128]{1,0:T(8,128)(2,1)S(1)}, bf16[512,128]{1,0:T(8,128)(2,1)S(1)}, u32[]{:S(2)}, u32[]{:S(2)}) collective-permute-start(bf16[512,128]{1,0:T(8,128)(2,1)S(1)} %get-tuple-element.26.h1_ref), channel_id=1, source_target_pairs={{0,1},{1,2},{2,3},{3,4},{4,5},{5,6},{6,7},{7,8},{8,9},{9,10},{10,1... | collective-permute-start | bytes 393224 | tf_op jit(solution)/shard_map/ppermute | solution.py:16
  13.4 2.4 %copy-start.1 = (bf16[3,3,3,128,128]{4,3,2,1,0:T(8,128)(2,1)S(1)}, bf16[3,3,3,128,128]{4,3,2,1,0:T(8,128)(2,1)}, u32[]{:S(2)}) copy-start(bf16[3,3,3,128,128]{4,3,2,1,0:T(8,128)(2,1)} %param.6) | copy-start | bytes 2654212
  13.4 2.4 %copy-start.3 = (bf16[1,1,8,16,128]{4,3,2,1,0:T(8,128)(2,1)S(1)}, bf16[1,1,8,16,128]{4,3,2,1,0:T(8,128)(2,1)}, u32[]{:S(2)}) copy-start(bf16[1,1,8,16,128]{4,3,2,1,0:T(8,128)(2,1)} %param.7) | copy-start | bytes 98308
  16.8 1.6 %collective-permute-start.2 = (bf16[128,128]{1,0:T(8,128)(2,1)S(1)}, bf16[128,128]{1,0:T(8,128)(2,1)S(1)}, u32[]{:S(2)}, u32[]{:S(2)}) collective-permute-start(bf16[128,128]{1,0:T(8,128)(2,1)S(1)} %get-tuple-element.30.gp_ref), channel_id=1, source_target_pairs={{0,31},{1,0},{2,1},{3,2},{4,3},{5,4},{6,5},{7,6},{8,7},{9,8},{10,9... | collective-permute-start | bytes 98312 | tf_op jit(solution)/shard_map/ppermute | solution.py:16
  18.4 3.1 %collective-permute-start.4 = (bf16[27,64,128]{2,1,0:T(8,128)(2,1)S(1)}, bf16[27,64,128]{2,1,0:T(8,128)(2,1)S(1)}, u32[]{:S(2)}, u32[]{:S(2)}) collective-permute-start(bf16[27,64,128]{2,1,0:T(8,128)(2,1)S(1)} %get-tuple-element.38), channel_id=1, source_target_pairs={{0,1},{1,0},{2,3},{3,2},{4,5},{5,4},{6,7},{7,6},{8,9},{9,8},{10,11... | collective-permute-start | bytes 1327112 | tf_op jit(solution)/shard_map/ppermute | solution.py:21
  19.8 1.7 %collective-permute-start.3 = (bf16[14,64,128]{2,1,0:T(8,128)(2,1)S(1)}, bf16[14,64,128]{2,1,0:T(8,128)(2,1)S(1)}, u32[]{:S(2)}, u32[]{:S(2)}) collective-permute-start(bf16[14,64,128]{2,1,0:T(8,128)(2,1)S(1)} %get-tuple-element.36), channel_id=1, source_target_pairs={{0,1},{1,0},{2,3},{3,2},{4,5},{5,4},{6,7},{7,6},{8,9},{9,8},{10,11... | collective-permute-start | bytes 688136 | tf_op jit(solution)/shard_map/ppermute | solution.py:21
  21.6 10.3 %collective-permute-start.5 = (bf16[41,32,128]{2,1,0:T(8,128)(2,1)S(1)}, bf16[41,32,128]{2,1,0:T(8,128)(2,1)S(1)}, u32[]{:S(2)}, u32[]{:S(2)}) collective-permute-start(bf16[41,32,128]{2,1,0:T(8,128)(2,1)S(1)} %get-tuple-element.40), channel_id=1, source_target_pairs={{0,8},{1,9},{2,10},{3,11},{4,12},{5,13},{6,14},{7,15},{8,0},{9,1},... | collective-permute-start | bytes 1007624 | tf_op jit(solution)/shard_map/ppermute | solution.py:21
  32.0 7.0 %collective-permute-start.6 = (bf16[41,16,128]{2,1,0:T(8,128)(2,1)S(1)}, bf16[41,16,128]{2,1,0:T(8,128)(2,1)S(1)}, u32[]{:S(2)}, u32[]{:S(2)}) collective-permute-start(bf16[41,16,128]{2,1,0:T(8,128)(2,1)S(1)} %get-tuple-element.42), channel_id=1, source_target_pairs={{0,24},{1,25},{2,26},{3,27},{4,28},{5,29},{6,30},{7,31},{8,16},{9,... | collective-permute-start | bytes 503816 | tf_op jit(solution)/shard_map/ppermute | solution.py:21
  39.0 10.0 %collective-permute-start.7 = (bf16[41,8,128]{2,1,0:T(8,128)(2,1)S(1)}, bf16[41,8,128]{2,1,0:T(8,128)(2,1)S(1)}, u32[]{:S(2)}, u32[]{:S(2)}) collective-permute-start(bf16[41,8,128]{2,1,0:T(8,128)(2,1)S(1)} %get-tuple-element.44), channel_id=1, source_target_pairs={{0,2},{1,3},{2,0},{3,1},{4,6},{5,7},{6,4},{7,5},{8,10},{9,11},{10,... | collective-permute-start | bytes 251912 | tf_op jit(solution)/shard_map/ppermute | solution.py:21
  49.1 6.2 %collective-permute-start.8 = (bf16[41,4,128]{2,1,0:T(4,128)(2,1)S(1)}, bf16[41,4,128]{2,1,0:T(4,128)(2,1)S(1)}, u32[]{:S(2)}, u32[]{:S(2)}) collective-permute-start(bf16[41,4,128]{2,1,0:T(4,128)(2,1)S(1)} %get-tuple-element.46), channel_id=1, source_target_pairs={{0,6},{1,7},{2,4},{3,5},{4,2},{5,3},{6,0},{7,1},{8,14},{9,15},{10,... | collective-permute-start | bytes 125960 | tf_op jit(solution)/shard_map/ppermute | solution.py:21
  55.4 4.1 %collective-permute-start.9 = (bf16[41,4,128]{2,1,0:T(4,128)(2,1)S(1)}, bf16[41,4,128]{2,1,0:T(4,128)(2,1)S(1)}, u32[]{:S(2)}, u32[]{:S(2)}) collective-permute-start(bf16[41,4,128]{2,1,0:T(4,128)(2,1)S(1)} %shard_map.77.refs_0_), channel_id=1, source_target_pairs={{0,32},{32,0},{64,96},{96,64},{128,160},{160,128},{192,224},{224,1... | collective-permute-start | bytes 125960 | tf_op jit(solution)/shard_map/ppermute | solution.py:21
  59.5 5.3 %collective-permute-start.10 = (bf16[41,4,128]{2,1,0:T(4,128)(2,1)S(1)}, bf16[41,4,128]{2,1,0:T(4,128)(2,1)S(1)}, u32[]{:S(2)}, u32[]{:S(2)}) collective-permute-start(bf16[41,4,128]{2,1,0:T(4,128)(2,1)S(1)} %shard_map.78.refs_0_), channel_id=1, source_target_pairs={{0,96},{32,64},{64,32},{96,0},{128,224},{160,192},{192,160},{224,1... | collective-permute-start | bytes 125960 | tf_op jit(solution)/shard_map/ppermute | solution.py:21
  64.8 4.1 %collective-permute-start.11 = (bf16[41,4,128]{2,1,0:T(4,128)(2,1)S(1)}, bf16[41,4,128]{2,1,0:T(4,128)(2,1)S(1)}, u32[]{:S(2)}, u32[]{:S(2)}) collective-permute-start(bf16[41,4,128]{2,1,0:T(4,128)(2,1)S(1)} %shard_map.79.own_ref), channel_id=1, source_target_pairs={{0,128},{32,160},{64,192},{96,224},{128,0},{160,32},{192,64},{224,... | collective-permute-start | bytes 125960 | tf_op jit(solution)/shard_map/ppermute | solution.py:21

commit v3 on v2

v3 whole, which is shorter than its diff:
```python
import functools

import jax
import jax.numpy as jnp
from jax import lax
from jax.experimental import pallas as pl
from jax.experimental.pallas import tpu as pltpu
from jax.sharding import PartitionSpec as P

SLOPE = 0.3
F32, BF16 = jnp.float32, jnp.bfloat16
FIRST, SECOND = 14, 27


def around_space(value, by):
    return lax.ppermute(value, "space", [(i, (i + by) % 32) for i in range(32)])


def swap(value, axis, bit):
    size = {"space": 32, "dp": 8}[axis]
    return lax.ppermute(value, axis, [(i, i ^ bit) for i in range(size)])


CORE, X_ONE, X_TWO, Z_ONE, Z_TWO = 1, 8, 24, 2, 6
Y_ONE, Y_TWO, Z_LOW = 1, 3, 4


def leaky(values):
    return jnp.where(values > 0, values, SLOPE * values)


def dot(a, b):
    return jnp.dot(a, b, preferred_element_type=F32)


def dot_nt(a, b):
    return lax.dot_general(a, b, (((1,), (1,)), ((), ())), preferred_element_type=F32)


def rows_by_tap(keep=None):
    m = lax.broadcasted_iota(jnp.int32, (48, 32), 0)
    h = lax.broadcasted_iota(jnp.int32, (48, 32), 1)
    picked = h == 2 * (m & 15) + (m >> 4) - 1
    if keep is not None:
        picked = jnp.logical_and(picked, keep)
    return jnp.where(picked, 1.0, 0.0).astype(BF16)


def channel_order(near, far):
    s = lax.axis_index("space")
    m = lax.broadcasted_iota(jnp.int32, (128, 128), 0)
    i = lax.broadcasted_iota(jnp.int32, (128, 128), 1)
    core = (m >> 6) ^ (s & 1)
    x = (near * ((m >> 5) & 1)) ^ (far * ((m >> 4) & 1)) ^ (s >> 3)
    z = ((m >> 3) & 1) ^ (3 * ((m >> 2) & 1)) ^ ((s >> 1) & 3)
    return jnp.where(i == x * 32 + z * 8 + core * 4 + (m & 3), 1.0, 0.0).astype(BF16)


def spread_rows(plane_ref, pick, y_ref):
    for t in range(3):
        y_ref[t, 0] = jnp.zeros((16, 128), BF16)
    for n in range(8):
        out = dot(pick, plane_ref[:, n * 512 : (n + 1) * 512]).astype(BF16)
        for t in range(3):
            for r in range(4):
                y_ref[t, 1 + 4 * n + r] = out[16 * t : 16 * t + 16, 128 * r : 128 * r + 128]


def columns(y_ref, b):
    before = y_ref[b, 0:32].reshape(512, 128)
    at = y_ref[b, 1:33].reshape(512, 128)
    return jnp.concatenate([before, at], axis=1)


def first_conv(planes, w):
    lhs = jnp.concatenate([columns(plane, b) for plane in planes for b in range(3)], axis=1)
    return dot(lhs, w)


def second_taps(hidden, hs):
    h = hidden.astype(F32).reshape(16, 2, 16, 128)
    hs[:, :, 0:8, :] = jnp.zeros((17, 2, 8, 128), F32)
    hs[0, 0] = jnp.zeros((24, 128), F32)
    hs[0:16, 1, 8:24, :] = h[:, 0]
    hs[1:17, 0, 8:24, :] = h[:, 1]
    taps = []
    for b in range(3):
        for c in range(3):
            rows = hs[c // 2 : c // 2 + 16, c % 2, pl.ds(7 + b, 8, stride=2), :]
            taps.append(rows.reshape(128, 128).astype(BF16))
    return taps


def upper_plane_kernel(
    v_ref, rim_ref, f_ref, f2_ref,
    y_ref, w_ref, f2a_ref, hid_ref, taps_ref, next_ref,
    v, f, hs, sems,
):
    copies = [
        pltpu.make_async_copy(v_ref.at[1], v.at[0], sems.at[0]),
        pltpu.make_async_copy(v_ref.at[2], v.at[1], sems.at[1]),
        pltpu.make_async_copy(f_ref, f, sems.at[2]),
        pltpu.make_async_copy(f2_ref.at[0:9], f2a_ref, sems.at[3]),
    ]
    for copy in copies:
        copy.start()
    pick = rows_by_tap()
    spread_rows(rim_ref, pick, y_ref.at[2])
    for p in range(2):
        copies[p].wait()
        spread_rows(v.at[p], pick, y_ref.at[p])
    copies[2].wait()
    for ab in range(9):
        w_ref[ab * 256 : ab * 256 + 64] = jnp.zeros((64, 128), BF16)
        w_ref[ab * 256 + 64 : ab * 256 + 256] = f[ab]
    hidden = leaky(first_conv([y_ref.at[p] for p in range(3)], w_ref[...])).astype(BF16)
    hid_ref[...] = hidden
    taps = second_taps(hidden, hs)
    for n, tap in enumerate(taps):
        taps_ref[n * 128 : n * 128 + 128] = tap
    copies[3].wait()
    next_ref[...] = dot(jnp.concatenate(taps, axis=1), f2a_ref[...].reshape(1152, 128))


def ahead_kernel(
    v_ref, y_ref, w_ref, f2_ref, taps_ref, y0_ref, f2b_ref, acc_ref, own_ref, v, sems
):
    copies = [
        pltpu.make_async_copy(v_ref.at[0], v, sems.at[0]),
        pltpu.make_async_copy(f2_ref.at[9:27], f2b_ref, sems.at[1]),
    ]
    for copy in copies:
        copy.start()
    copies[0].wait()
    spread_rows(v, rows_by_tap(), y0_ref)
    acc_ref[...] = first_conv([y0_ref, y_ref.at[0]], w_ref[768:])
    copies[1].wait()
    own = None
    for n in range(9):
        part = dot(taps_ref[n * 128 : n * 128 + 128], f2b_ref[9 + n])
        own = part if own is None else own + part
    own_ref[...] = own


def lower_plane_kernel(
    rim_ref, got_ref, w_ref, f2b_ref, acc_ref, own_ref, up_ref,
    yr_ref, hid_ref, taps_ref, out_ref, gp_ref,
    hs, us, os,
):
    inside = lax.axis_index("space") > 0
    spread_rows(rim_ref, rows_by_tap(inside), yr_ref)
    hidden = leaky(first_conv([yr_ref], w_ref[0:768]) + acc_ref[...]).astype(BF16)
    hid_ref[...] = hidden
    taps = second_taps(hidden, hs)
    for n, tap in enumerate(taps):
        taps_ref[n * 128 : n * 128 + 128] = tap
    pre = dot(jnp.concatenate(taps, axis=1), f2b_ref[0:9].reshape(1152, 128))
    pre = pre + own_ref[...] + got_ref[...] * jnp.where(inside, 1.0, 0.0)
    us[...] = up_ref[...].astype(F32).reshape(128, 128)
    up = jnp.concatenate([us[pl.ds(r, 8, stride=16), :] for r in range(16)], axis=0)
    gp_ref[...] = (up * jnp.where(pre > 0, 1.0, SLOPE)).astype(BF16)
    out = leaky(pre)
    for r in range(16):
        os[pl.ds(r, 8, stride=16), :] = out[8 * r : 8 * r + 8]
    out_ref[...] = os[...].astype(BF16).reshape(8, 16, 128)


def second_grad(order, taps_ref, gp):
    turned = dot_nt(order, taps_ref[...]).astype(BF16)
    lhs = [turned[:, tap * 128 : tap * 128 + 128] for tap in range(9)]
    return dot(jnp.concatenate(lhs, axis=0), gp).reshape(9, 128, 128)


def second_grad_kernel(low_ref, up_ref, gp_ref, keep_ref, send_ref):
    for n, taps_ref in enumerate((low_ref, up_ref)):
        grad = second_grad(channel_order(1, 3), taps_ref, gp_ref[...])
        keep_ref[9 * n : 9 * n + 9] = grad[:, :64]
        send_ref[9 * n : 9 * n + 9] = grad[:, 64:].astype(BF16)


def first_grad_kernel(
    gp_ref, gpn_ref, fa_ref, fb_ref, h0_ref, h1_ref, yr_ref, y0_ref, y_ref, taps_ref,
    keep_ref, send_ref, gs, gu,
):
    inside = jnp.where(lax.axis_index("space") < 31, 1.0, 0.0)
    gs[...] = jnp.zeros_like(gs)
    gs[0, 0:16, 0:8, :] = gp_ref[...].astype(F32).reshape(16, 8, 128)
    above = gpn_ref[...].astype(F32) * inside
    gs[1, 0:16, 0:8, :] = above.reshape(16, 8, 128)
    moved = {
        (s, dr, dq): gs[s, dr : dr + 16, dq : dq + 8, :].reshape(128, 128).astype(BF16)
        for s in range(2)
        for dr in range(2)
        for dq in range(2)
    }
    one_d = {0: [(0, 1)], 1: [(0, 2), (1, 0)]}
    for pu in range(2):
        for pv in range(2):
            for pw in range(2):
                lhs, rhs = [], []
                for s, a in one_d[pu]:
                    for dq, b in one_d[pv]:
                        for dr, c in one_d[pw]:
                            lhs.append(moved[s, dr, dq])
                            tap = 9 * a + 3 * b + c
                            rhs.append(fb_ref[tap - 9] if a else fa_ref[tap])
                grad = dot_nt(jnp.concatenate(lhs, axis=1), jnp.concatenate(rhs, axis=1))
                grad = grad.astype(BF16).astype(F32).reshape(16, 8, 128)
                gu[pu, :, pw, pl.ds(pv, 8, stride=2), :] = grad
    grads = []
    for pu, h_ref in enumerate((h0_ref, h1_ref)):
        hid = h_ref[...].astype(F32)
        grads.append((gu[pu].reshape(512, 128) * jnp.where(hid > 0, 1.0, SLOPE)).astype(BF16))
    order = channel_order(3, 1)
    turned = dot_nt(order, jnp.concatenate(grads, axis=0)).astype(BF16)
    planes = [yr_ref, y0_ref] + [y_ref.at[p] for p in range(3)]
    low = lax.broadcasted_iota(jnp.int32, (128, 128), 1) < 64

    def put(block, grad):
        keep_ref[block] = grad[:64]
        send_ref[block] = grad[64:].astype(BF16)

    held = None
    for a in range(3):
        for b in range(3):
            ab = 3 * a + b
            rhs = jnp.concatenate([columns(planes[a], b), columns(planes[a + 2], b)], axis=0)
            grad = dot(turned, rhs)
            put(ab, grad[:, 128:])
            if ab % 2 == 0:
                held = pltpu.roll(grad[:, :128], 64, axis=1)
            if ab % 2 == 1 or ab == 8:
                upper = grad[:, :128] if ab % 2 else jnp.zeros_like(held)
                put(9 + ab // 2, jnp.where(low, held, upper))
    grad = second_grad(order, taps_ref, above.astype(BF16))
    keep_ref[FIRST:] = grad[:, :64]
    send_ref[FIRST:] = grad[:, 64:].astype(BF16)


def fold_kernel(groups, *refs):
    count = 2 * sum(groups)
    ins, outs = list(refs[:count]), list(refs[count:])
    for parts in groups:
        keep_ref, send_ref = outs.pop(0), outs.pop(0)
        at = 0
        for _ in range(parts):
            own_ref, got_ref = ins.pop(0), ins.pop(0)
            total = own_ref[...] + got_ref[...].astype(F32)
            blocks, rows, _ = total.shape
            keep_ref[at : at + blocks] = total[:, : rows // 2]
            send_ref[at : at + blocks] = total[:, rows // 2 :].astype(BF16)
            at += blocks


def sum_kernel(*refs):
    *ins, out_ref = refs
    at = 0
    for own_ref, got_ref in zip(ins[::2], ins[1::2]):
        total = own_ref[...].astype(F32) + got_ref[...].astype(F32)
        out_ref[at : at + total.shape[0]] = total.astype(BF16)
        at += total.shape[0]


def final_kernel(own_ref, got_ref, first_ref, second_ref):
    total = own_ref[...].astype(F32) + got_ref[...].astype(F32)
    for ab in range(9):
        first_ref[3 * ab + 1] = total[18 + ab, :, :64]
        first_ref[3 * ab + 2] = total[18 + ab, :, 64:]
        at = (ab % 2) * 64
        first_ref[3 * ab] = total[27 + ab // 2, :, at : at + 64]
    second_ref[9:27] = total[:18]
    second_ref[0:9] = total[18 + FIRST :]


VMEM, HBM = pltpu.VMEM, pltpu.HBM


def call(kernel, outs, *args, scratch=(), spaces=None, flops=10**6):
    size = sum(a.size * a.dtype.itemsize for a in args)
    spaces = spaces or [VMEM] * len(args)
    return pl.pallas_call(
        kernel,
        out_shape=[jax.ShapeDtypeStruct(shape, dtype) for shape, dtype in outs],
        in_specs=[pl.BlockSpec(memory_space=space) for space in spaces],
        out_specs=[pl.BlockSpec(memory_space=VMEM)] * len(outs),
        scratch_shapes=[pltpu.VMEM(*s) if isinstance(s, tuple) else s for s in scratch],
        compiler_params=pltpu.CompilerParams(vmem_limit_bytes=24 << 20),
        cost_estimate=pl.CostEstimate(flops=flops, bytes_accessed=size, transcendentals=0),
    )(*args)


def in_hbm(value):
    return pltpu.with_memory_space_constraint(value, HBM)


def fold(*groups):
    outs, args = [], []
    for group in groups:
        blocks = sum(own.shape[0] for own, _ in group)
        half = (blocks, group[0][0].shape[1] // 2, 128)
        outs += [(half, F32), (half, BF16)]
        args += [array for pair in group for array in pair]
    kernel = functools.partial(fold_kernel, [len(group) for group in groups])
    done = call(kernel, outs, *args)
    return list(zip(done[::2], done[1::2]))


def local(volumes, first_filter, second_filter, upstream_grad):
    slab = in_hbm(volumes.reshape(4, 32, 4096))
    first = in_hbm(first_filter.reshape(9, 192, 128))
    second = in_hbm(second_filter.reshape(27, 128, 128))
    upstream = upstream_grad.reshape(8, 16, 128)
    y_plane = (3, 33, 16, 128)
    hs = ((17, 2, 24, 128), F32)
    tile = ((128, 128), F32)

    rim_up = volumes[0, 3]
    rim = around_space(rim_up, 1)
    y, w, second_a, hidden_up, taps_up, to_next = call(
        upper_plane_kernel,
        [
            ((3,) + y_plane, BF16), ((2304, 128), BF16), ((9, 128, 128), BF16),
            ((512, 128), BF16), ((1152, 128), BF16), tile,
        ],
        slab, rim_up, first, second, spaces=[HBM, VMEM, HBM, HBM],
        scratch=[((2, 32, 4096), BF16), ((9, 192, 128), BF16), hs, pltpu.SemaphoreType.DMA((4,))],
        flops=10**9,
    )
    from_below = around_space(to_next, 1)
    y_low, second_b, partial_low, from_up = call(
        ahead_kernel,
        [(y_plane, BF16), ((18, 128, 128), BF16), ((512, 128), F32), tile],
        slab, y, w, second, taps_up, spaces=[HBM, VMEM, VMEM, HBM, VMEM],
        scratch=[((32, 4096), BF16), pltpu.SemaphoreType.DMA((2,))], flops=10**9,
    )
    y_rim, hidden_low, taps_low, second_out, grad_two = call(
        lower_plane_kernel,
        [
            (y_plane, BF16), ((512, 128), BF16), ((1152, 128), BF16),
            ((8, 16, 128), BF16), ((128, 128), BF16),
        ],
        rim, from_below, w, second_b, partial_low, from_up, upstream,
        scratch=[hs, tile, tile], flops=4 * 10**8,
    )
    grad_two_next = around_space(grad_two, -1)
    keep2, send2 = call(
        second_grad_kernel,
        [((18, 64, 128), F32), ((18, 64, 128), BF16)],
        taps_low, taps_up, grad_two, flops=4 * 10**8,
    )
    send2, grad_two_next = lax.optimization_barrier((send2, grad_two_next))
    blocks = FIRST + 9
    keep1, send1 = call(
        first_grad_kernel,
        [((blocks, 64, 128), F32), ((blocks, 64, 128), BF16)],
        grad_two, grad_two_next, second_a, second_b, hidden_low, hidden_up,
        y_rim, y_low, y, taps_up,
        scratch=[((2, 17, 16, 128), F32), ((2, 16, 2, 16, 128), F32)], flops=8 * 10**8,
    )
    s = "space"
    got2, got1 = swap(send2, s, CORE), swap(send1, s, CORE)
    (keep2, send2), (keep1, send1) = fold([(keep2, got2)], [(keep1, got1)])
    got2, got1 = swap(send2, s, X_ONE), swap(send1, s, X_TWO)
    (keep2, send2), (keep1, send1) = fold([(keep2, got2)], [(keep1, got1)])
    got2, got1 = swap(send2, s, X_TWO), swap(send1, s, X_ONE)
    ((keep, send),) = fold([(keep2, got2), (keep1, got1)])
    ((keep, send),) = fold([(keep, swap(send, s, Z_ONE))])
    total = ((FIRST + SECOND, 4, 128), BF16)
    (both,) = call(sum_kernel, [total], keep, swap(send, s, Z_TWO))
    (both,) = call(sum_kernel, [total], both, swap(both, "dp", Y_ONE))
    (both,) = call(sum_kernel, [total], both, swap(both, "dp", Y_TWO))
    first_grad, second_grad = call(
        final_kernel,
        [((27, 4, 64), F32), ((27, 4, 128), F32)],
        both, swap(both, "dp", Z_LOW),
    )
    return (
        second_out.reshape(1, 1, 8, 16, 128),
        jnp.swapaxes(first_grad, 1, 2).reshape(3, 3, 3, 64, 4),
        second_grad.reshape(3, 3, 3, 4, 128),
    )


def solution(mesh):
    placed = (P("dp", "space", None, None), P(), P(), P("dp", "space", None, None, None))
    return jax.shard_map(
        local,
        mesh=mesh,
        in_specs=placed,
        out_specs=(
            P("dp", "space", None, None, None),
            P(None, None, None, None, "space"),
            P(None, None, None, "space", None),
        ),
        check_vma=False,
    )
```

time: 70.7 us -> 66.4 us (0.939)
  waiting for transfers between devices: 37.4 us -> 32.6 us
    ppermute x3, waiting for transfers between devices: 6.66 us -> 4.09 us  [around_space(): return lax.ppermute(value, 'space', [(i, (i + by) % 32) for i in range(32)])]
    ppermute x9 -> x11, waiting for transfers between devices: 30.7 us -> 28.5 us  [swap(): return lax.ppermute(value, axis, [(i, i ^ bit) for i in range(size)])]
    unnamed x8 -> x2, local copies, waits for them, and re-layouts: 1.02 us -> 0.01 us
    squeeze x0 -> x1, local copies, waits for them, and re-layouts: none -> 0.97 us  [local(): rim_up = volumes[0, 3]]
    pallas_call x14 -> x13, Pallas kernels: 8.93 us -> 9.53 us  [call(): pl.pallas_call(kernel, out_shape=[jax.ShapeDtypeStruct(shape, dtype) for...]
    ppermute x9 -> x11, starting transfers between devices: 18.1 us -> 18.1 us  [swap(): return lax.ppermute(value, axis, [(i, i ^ bit) for i in range(size)])]
  transfers between devices with their start and end apart: 12 -> 14, of which waited for: 11 -> 11; matrix products, arithmetic and copies ran while one was open for 0% -> 0% of each run, Pallas kernels for 7% -> 8%
where the time goes in v3:
time: 66.4 us; the launch traced here: 65.4 us
  waiting for transfers between devices  32.6 us (49%)
  starting transfers between devices  21.6 us (33%)
  Pallas kernels  9.53 us (14%)
  local copies, waits for them, and re-layouts  0.97 us (1%)
  between operations  0.72 us (1%)
    ppermute x11, waiting for transfers between devices, swap(): return lax.ppermute(value, axis, [(i, i ^ bit) for i in range(size)])  28.5 us
    ppermute x11, starting transfers between devices, swap(): return lax.ppermute(value, axis, [(i, i ^ bit) for i in range(size)])  18.1 us
    pallas_call x13, Pallas kernels, call(): pl.pallas_call(kernel, out_shape=[jax.ShapeDtypeStruct(shape, dtype) for...  9.53 us
    ppermute x3, waiting for transfers between devices, around_space(): return lax.ppermute(value, 'space', [(i, (i + by) % 32) for i in range(32)])  4.09 us
    ppermute x3, starting transfers between devices, around_space(): return lax.ppermute(value, 'space', [(i, (i + by) % 32) for i in range(32)])  3.52 us
  transfers between devices with their start and end apart: 14, of which 11 were waited for; matrix products, arithmetic and copies ran while one was open for 0% of the time, Pallas kernels for 8%

profile of v3, /device:TPU:6, one launch (start us, length us, event | category | flops | bytes accessed | tf_op | source)
XLA Modules:
  0.0 65.4 jit_solution(6557224901132954959)
XLA Ops:
  0.6 1.0 %slice_bitcast_fusion.rim_ref = bf16[32,4096]{1,0:T(8,128)(2,1)S(1)} fusion(bf16[1,4,32,4096]{3,2,1,0:T(8,128)(2,1)} %param.4), kind=kLoop, calls=%fused_computation | loop fusion | bytes 524288 | tf_op jit(solution)/shard_map/squeeze | solution.py:317
  1.6 0.1 collective-permute-start
  1.7 2.7 %shard_map.67 = (bf16[3,3,33,16,128]{4,3,2,1,0:T(8,128)(2,1)S(1)}, bf16[2304,128]{1,0:T(8,128)(2,1)S(1)}, bf16[9,128,128]{2,1,0:T(8,128)(2,1)S(1)}, bf16[512,128...) custom-call(bf16[4,32,4096]{2,1,0:T(8,128)(2,1)} %bitcast.12, ...), custom_call_target="tpu_custom_call" | custom-call | flops 1000000000 | bytes 2637824 | tf_op jit(solution)/shard_map/pallas_call | solution.py:281
  4.4 3.4 %collective-permute-start.1 = (f32[128,128]{1,0:T(8,128)S(1)}, f32[128,128]{1,0:T(8,128)S(1)}, u32[]{:S(2)}, u32[]{:S(2)}) collective-permute-start(f32[128,128]{1,0:T(8,128)S(1)} %get-tuple-element.38), channel_id=1, source_target_pairs={{0,1},{1,2},{2,3},{3,4},{4,5},{5,6},{6,7},{7,8},{8,9},{9,10},{10,1... | collective-permute-start | bytes 196616 | tf_op jit(solution)/shard_map/ppermute | solution.py:16
  7.9 2.1 %shard_map.68 = (bf16[3,33,16,128]{3,2,1,0:T(8,128)(2,1)S(1)}, bf16[18,128,128]{2,1,0:T(8,128)(2,1)S(1)}, f32[512,128]{1,0:T(8,128)S(1)}, f32[128,128]{1,0:T(8,128)S(1)}) custom-call(bf16[4,32,4096]{2,1,0:T(8,128)(2,1)} %bitcast.13, bf16[3,3,33,16,128]{4,3,2,1,0:T(8,128)(2,1)S(1)} %get-tuple-element.40.y_ref, bf16[2304,128]{1,0:T(8,128)(2,1)S(1)} %get-tuple-element.39.w_ref, ...), custom_call_target="tpu_custom_call" | custom-call | flops 1000000000 | bytes 4034560 | tf_op jit(solution)/shard_map/pallas_call | solution.py:281
  10.0 3.1 %collective-permute-done.1.got_ref = f32[128,128]{1,0:T(8,128)S(1)} collective-permute-done((f32[128,128]{1,0:T(8,128)S(1)}, f32[128,128]{1,0:T(8,128)S(1)}, u32[]{:S(2)}, u32[]{:S(2)}) %collective-permute-start.1) | collective-permute-done | bytes 65568 | tf_op jit(solution)/shard_map/ppermute | solution.py:16
  13.0 1.5 %shard_map.69 = (bf16[3,33,16,128]{3,2,1,0:T(8,128)(2,1)S(1)}, bf16[512,128]{1,0:T(8,128)(2,1)S(1)}, bf16[1152,128]{1,0:T(8,128)(2,1)S(1)}, bf16[8,16,128]{2,1,0:T(8,128)(2,1)}, bf16[128,128]{1,0:T(8,128)(2,1)S(1)}) custom-call(bf16[32,4096]{1,0:T(8,128)(2,1)S(1)} %collective-permute-done.rim_ref, f32[128,128]{1,0:T(8,128)S(1)} %collective-permute-done.1.got_ref, ...), custom_call_target="tpu_custom_call" | custom-call | flops 400000000 | bytes 1867776 | tf_op jit(solution)/shard_map/pallas_call | solution.py:281
  14.6 0.6 shard_map.70
  15.2 1.0 %collective-permute-done.2.gpn_ref = bf16[128,128]{1,0:T(8,128)(2,1)S(1)} collective-permute-done((bf16[128,128]{1,0:T(8,128)(2,1)S(1)}, bf16[128,128]{1,0:T(8,128)(2,1)S(1)}, u32[]{:S(2)}, u32[]{:S(2)}) %collective-permute-start.2) | collective-permute-done | bytes 32800 | tf_op jit(solution)/shard_map/ppermute | solution.py:16
  16.2 1.5 %shard_map.71 = (f32[23,64,128]{2,1,0:T(8,128)S(1)}, bf16[23,64,128]{2,1,0:T(8,128)(2,1)S(1)}) custom-call(bf16[128,128]{1,0:T(8,128)(2,1)S(1)} %get-tuple-element.47.gp_ref, bf16[128,128]{1,0:T(8,128)(2,1)S(1)} %collective-permute-done.2.gpn_ref, bf16[9,128,128]{2,1,0:T(8,128)(2,1)S(1)} %get-tuple-element.52.fa_ref, ...), custom_call_target="tpu_custom_call" | custom-call | flops 800000000 | bytes 3534848 | tf_op jit(solution)/shard_map/pallas_call | solution.py:281
  17.7 1.6 %collective-permute-start.4 = (bf16[23,64,128]{2,1,0:T(8,128)(2,1)S(1)}, bf16[23,64,128]{2,1,0:T(8,128)(2,1)S(1)}, u32[]{:S(2)}, u32[]{:S(2)}) collective-permute-start(bf16[23,64,128]{2,1,0:T(8,128)(2,1)S(1)} %get-tuple-element.58), channel_id=1, source_target_pairs={{0,1},{1,0},{2,3},{3,2},{4,5},{5,4},{6,7},{7,6},{8,9},{9,8},{10,11... | collective-permute-start | bytes 1130504 | tf_op jit(solution)/shard_map/ppermute | solution.py:21
  19.4 0.1 collective-permute-start.3
  19.5 1.6 %collective-permute-done.3.refs_1_ = bf16[18,64,128]{2,1,0:T(8,128)(2,1)S(1)} collective-permute-done((bf16[18,64,128]{2,1,0:T(8,128)(2,1)S(1)}, bf16[18,64,128]{2,1,0:T(8,128)(2,1)S(1)}, u32[]{:S(2)}, u32[]{:S(2)}) %collective-permute-start.3) | collective-permute-done | bytes 294944 | tf_op jit(solution)/shard_map/ppermute | solution.py:21
  21.1 0.1 shard_map.72
  21.2 1.3 %collective-permute-start.6 = (bf16[23,32,128]{2,1,0:T(8,128)(2,1)S(1)}, bf16[23,32,128]{2,1,0:T(8,128)(2,1)S(1)}, u32[]{:S(2)}, u32[]{:S(2)}) collective-permute-start(bf16[23,32,128]{2,1,0:T(8,128)(2,1)S(1)} %get-tuple-element.62), channel_id=1, source_target_pairs={{0,24},{1,25},{2,26},{3,27},{4,28},{5,29},{6,30},{7,31},{8,16},{9,... | collective-permute-start | bytes 565256 | tf_op jit(solution)/shard_map/ppermute | solution.py:21
  22.6 0.1 collective-permute-start.5
  22.7 5.5 %collective-permute-done.5.refs_1_ = bf16[18,32,128]{2,1,0:T(8,128)(2,1)S(1)} collective-permute-done((bf16[18,32,128]{2,1,0:T(8,128)(2,1)S(1)}, bf16[18,32,128]{2,1,0:T(8,128)(2,1)S(1)}, u32[]{:S(2)}, u32[]{:S(2)}) %collective-permute-start.5) | collective-permute-done | bytes 147488 | tf_op jit(solution)/shard_map/ppermute | solution.py:21
  28.2 1.4 %collective-permute-done.6.refs_3_ = bf16[23,32,128]{2,1,0:T(8,128)(2,1)S(1)} collective-permute-done((bf16[23,32,128]{2,1,0:T(8,128)(2,1)S(1)}, bf16[23,32,128]{2,1,0:T(8,128)(2,1)S(1)}, u32[]{:S(2)}, u32[]{:S(2)}) %collective-permute-start.6) | collective-permute-done | bytes 188448 | tf_op jit(solution)/shard_map/ppermute | solution.py:21
  29.6 0.1 collective-permute-start.8
  29.7 1.1 %collective-permute-start.7 = (bf16[18,16,128]{2,1,0:T(8,128)(2,1)S(1)}, bf16[18,16,128]{2,1,0:T(8,128)(2,1)S(1)}, u32[]{:S(2)}, u32[]{:S(2)}) collective-permute-start(bf16[18,16,128]{2,1,0:T(8,128)(2,1)S(1)} %get-tuple-element.64), channel_id=1, source_target_pairs={{0,24},{1,25},{2,26},{3,27},{4,28},{5,29},{6,30},{7,31},{8,16},{9,... | collective-permute-start | bytes 221192 | tf_op jit(solution)/shard_map/ppermute | solution.py:21
  30.9 4.5 %collective-permute-done.7.refs_1_ = bf16[18,16,128]{2,1,0:T(8,128)(2,1)S(1)} collective-permute-done((bf16[18,16,128]{2,1,0:T(8,128)(2,1)S(1)}, bf16[18,16,128]{2,1,0:T(8,128)(2,1)S(1)}, u32[]{:S(2)}, u32[]{:S(2)}) %collective-permute-start.7) | collective-permute-done | bytes 73760 | tf_op jit(solution)/shard_map/ppermute | solution.py:21
  35.4 7.0 %collective-permute-start.9 = (bf16[41,8,128]{2,1,0:T(8,128)(2,1)S(1)}, bf16[41,8,128]{2,1,0:T(8,128)(2,1)S(1)}, u32[]{:S(2)}, u32[]{:S(2)}) collective-permute-start(bf16[41,8,128]{2,1,0:T(8,128)(2,1)S(1)} %get-tuple-element.68), channel_id=1, source_target_pairs={{0,2},{1,3},{2,0},{3,1},{4,6},{5,7},{6,4},{7,5},{8,10},{9,11},{10,... | collective-permute-start | bytes 251912 | tf_op jit(solution)/shard_map/ppermute | solution.py:21
  42.4 2.4 %collective-permute-done.9.refs_1_ = bf16[41,8,128]{2,1,0:T(8,128)(2,1)S(1)} collective-permute-done((bf16[41,8,128]{2,1,0:T(8,128)(2,1)S(1)}, bf16[41,8,128]{2,1,0:T(8,128)(2,1)S(1)}, u32[]{:S(2)}, u32[]{:S(2)}) %collective-permute-start.9) | collective-permute-done | bytes 84000 | tf_op jit(solution)/shard_map/ppermute | solution.py:21
  44.9 1.4 %collective-permute-start.10 = (bf16[41,4,128]{2,1,0:T(4,128)(2,1)S(1)}, bf16[41,4,128]{2,1,0:T(4,128)(2,1)S(1)}, u32[]{:S(2)}, u32[]{:S(2)}) collective-permute-start(bf16[41,4,128]{2,1,0:T(4,128)(2,1)S(1)} %get-tuple-element.70), channel_id=1, source_target_pairs={{0,6},{1,7},{2,4},{3,5},{4,2},{5,3},{6,0},{7,1},{8,14},{9,15},{10,... | collective-permute-start | bytes 125960 | tf_op jit(solution)/shard_map/ppermute | solution.py:21
  46.3 4.8 %collective-permute-done.10.refs_1_ = bf16[41,4,128]{2,1,0:T(4,128)(2,1)S(1)} collective-permute-done((bf16[41,4,128]{2,1,0:T(4,128)(2,1)S(1)}, bf16[41,4,128]{2,1,0:T(4,128)(2,1)S(1)}, u32[]{:S(2)}, u32[]{:S(2)}) %collective-permute-start.10) | collective-permute-done | bytes 42016 | tf_op jit(solution)/shard_map/ppermute | solution.py:21
  51.1 1.7 %collective-permute-start.11 = (bf16[41,4,128]{2,1,0:T(4,128)(2,1)S(1)}, bf16[41,4,128]{2,1,0:T(4,128)(2,1)S(1)}, u32[]{:S(2)}, u32[]{:S(2)}) collective-permute-start(bf16[41,4,128]{2,1,0:T(4,128)(2,1)S(1)} %shard_map.76.refs_0_), channel_id=1, source_target_pairs={{0,32},{32,0},{64,96},{96,64},{128,160},{160,128},{192,224},{224,1... | collective-permute-start | bytes 125960 | tf_op jit(solution)/shard_map/ppermute | solution.py:21
  52.7 2.4 %collective-permute-done.11.refs_1_ = bf16[41,4,128]{2,1,0:T(4,128)(2,1)S(1)} collective-permute-done((bf16[41,4,128]{2,1,0:T(4,128)(2,1)S(1)}, bf16[41,4,128]{2,1,0:T(4,128)(2,1)S(1)}, u32[]{:S(2)}, u32[]{:S(2)}) %collective-permute-start.11) | collective-permute-done | bytes 42016 | tf_op jit(solution)/shard_map/ppermute | solution.py:21
  55.2 3.1 %collective-permute-start.12 = (bf16[41,4,128]{2,1,0:T(4,128)(2,1)S(1)}, bf16[41,4,128]{2,1,0:T(4,128)(2,1)S(1)}, u32[]{:S(2)}, u32[]{:S(2)}) collective-permute-start(bf16[41,4,128]{2,1,0:T(4,128)(2,1)S(1)} %shard_map.77.refs_0_), channel_id=1, source_target_pairs={{0,96},{32,64},{64,32},{96,0},{128,224},{160,192},{192,160},{224,1... | collective-permute-start | bytes 125960 | tf_op jit(solution)/shard_map/ppermute | solution.py:21
  58.3 2.2 %collective-permute-done.12.refs_1_ = bf16[41,4,128]{2,1,0:T(4,128)(2,1)S(1)} collective-permute-done((bf16[41,4,128]{2,1,0:T(4,128)(2,1)S(1)}, bf16[41,4,128]{2,1,0:T(4,128)(2,1)S(1)}, u32[]{:S(2)}, u32[]{:S(2)}) %collective-permute-start.12) | collective-permute-done | bytes 42016 | tf_op jit(solution)/shard_map/ppermute | solution.py:21
  60.6 0.5 collective-permute-start.13
  61.1 3.6 %collective-permute-done.13.got_ref = bf16[41,4,128]{2,1,0:T(4,128)(2,1)S(1)} collective-permute-done((bf16[41,4,128]{2,1,0:T(4,128)(2,1)S(1)}, bf16[41,4,128]{2,1,0:T(4,128)(2,1)S(1)}, u32[]{:S(2)}, u32[]{:S(2)}) %collective-permute-start.13) | collective-permute-done | bytes 42016 | tf_op jit(solution)/shard_map/ppermute | solution.py:21
  64.7 0.7 %shard_map.79 = (f32[27,4,64]{2,1,0:T(4,128)}, f32[27,4,128]{2,1,0:T(4,128)}) custom-call(bf16[41,4,128]{2,1,0:T(4,128)(2,1)S(1)} %shard_map.78.own_ref, bf16[41,4,128]{2,1,0:T(4,128)(2,1)S(1)} %collective-permute-done.13.got_ref), custom_call_target="tpu_custom_call" | custom-call | flops 1000000 | bytes 83968 | tf_op jit(solution)/shard_map/pallas_call | solution.py:281
  (12 shorter events, 0.2 us)
Async XLA Ops:
  1.6 11.4 %collective-permute-start = (bf16[32,4096]{1,0:T(8,128)(2,1)S(1)}, bf16[32,4096]{1,0:T(8,128)(2,1)S(1)}, u32[]{:S(2)}, u32[]{:S(2)}) collective-permute-start(bf16[32,4096]{1,0:T(8,128)(2,1)S(1)} %slice_bitcast_fusion.rim_ref), channel_id=1, source_target_pairs={{0,1},{1,2},{2,3},{3,4},{4,5},{5,6},{6,7},{7,8},{8,9},{9,10},{10,1... | collective-permute-start | bytes 786440 | tf_op jit(solution)/shard_map/ppermute | solution.py:16
  4.4 8.6 %collective-permute-start.1 = (f32[128,128]{1,0:T(8,128)S(1)}, f32[128,128]{1,0:T(8,128)S(1)}, u32[]{:S(2)}, u32[]{:S(2)}) collective-permute-start(f32[128,128]{1,0:T(8,128)S(1)} %get-tuple-element.38), channel_id=1, source_target_pairs={{0,1},{1,2},{2,3},{3,4},{4,5},{5,6},{6,7},{7,8},{8,9},{9,10},{10,1... | collective-permute-start | bytes 196616 | tf_op jit(solution)/shard_map/ppermute | solution.py:16
  7.9 5.2 %copy-start = (bf16[1,1,8,16,128]{4,3,2,1,0:T(8,128)(2,1)S(1)}, bf16[1,1,8,16,128]{4,3,2,1,0:T(8,128)(2,1)}, u32[]{:S(2)}) copy-start(bf16[1,1,8,16,128]{4,3,2,1,0:T(8,128)(2,1)} %param.7) | copy-start | bytes 98308
  14.6 1.6 %collective-permute-start.2 = (bf16[128,128]{1,0:T(8,128)(2,1)S(1)}, bf16[128,128]{1,0:T(8,128)(2,1)S(1)}, u32[]{:S(2)}, u32[]{:S(2)}) collective-permute-start(bf16[128,128]{1,0:T(8,128)(2,1)S(1)} %get-tuple-element.47.gp_ref), channel_id=1, source_target_pairs={{0,31},{1,0},{2,1},{3,2},{4,3},{5,4},{6,5},{7,6},{8,7},{9,8},{10,9... | collective-permute-start | bytes 98312 | tf_op jit(solution)/shard_map/ppermute | solution.py:16
  17.7 3.4 %collective-permute-start.4 = (bf16[23,64,128]{2,1,0:T(8,128)(2,1)S(1)}, bf16[23,64,128]{2,1,0:T(8,128)(2,1)S(1)}, u32[]{:S(2)}, u32[]{:S(2)}) collective-permute-start(bf16[23,64,128]{2,1,0:T(8,128)(2,1)S(1)} %get-tuple-element.58), channel_id=1, source_target_pairs={{0,1},{1,0},{2,3},{3,2},{4,5},{5,4},{6,7},{7,6},{8,9},{9,8},{10,11... | collective-permute-start | bytes 1130504 | tf_op jit(solution)/shard_map/ppermute | solution.py:21
  19.4 1.7 %collective-permute-start.3 = (bf16[18,64,128]{2,1,0:T(8,128)(2,1)S(1)}, bf16[18,64,128]{2,1,0:T(8,128)(2,1)S(1)}, u32[]{:S(2)}, u32[]{:S(2)}) collective-permute-start(bf16[18,64,128]{2,1,0:T(8,128)(2,1)S(1)} %get-tuple-element.50), channel_id=1, source_target_pairs={{0,1},{1,0},{2,3},{3,2},{4,5},{5,4},{6,7},{7,6},{8,9},{9,8},{10,11... | collective-permute-start | bytes 884744 | tf_op jit(solution)/shard_map/ppermute | solution.py:21
  21.2 8.3 %collective-permute-start.6 = (bf16[23,32,128]{2,1,0:T(8,128)(2,1)S(1)}, bf16[23,32,128]{2,1,0:T(8,128)(2,1)S(1)}, u32[]{:S(2)}, u32[]{:S(2)}) collective-permute-start(bf16[23,32,128]{2,1,0:T(8,128)(2,1)S(1)} %get-tuple-element.62), channel_id=1, source_target_pairs={{0,24},{1,25},{2,26},{3,27},{4,28},{5,29},{6,30},{7,31},{8,16},{9,... | collective-permute-start | bytes 565256 | tf_op jit(solution)/shard_map/ppermute | solution.py:21
  22.6 5.6 %collective-permute-start.5 = (bf16[18,32,128]{2,1,0:T(8,128)(2,1)S(1)}, bf16[18,32,128]{2,1,0:T(8,128)(2,1)S(1)}, u32[]{:S(2)}, u32[]{:S(2)}) collective-permute-start(bf16[18,32,128]{2,1,0:T(8,128)(2,1)S(1)} %get-tuple-element.60), channel_id=1, source_target_pairs={{0,8},{1,9},{2,10},{3,11},{4,12},{5,13},{6,14},{7,15},{8,0},{9,1},... | collective-permute-start | bytes 442376 | tf_op jit(solution)/shard_map/ppermute | solution.py:21
  29.6 5.8 %collective-permute-start.8 = (bf16[23,16,128]{2,1,0:T(8,128)(2,1)S(1)}, bf16[23,16,128]{2,1,0:T(8,128)(2,1)S(1)}, u32[]{:S(2)}, u32[]{:S(2)}) collective-permute-start(bf16[23,16,128]{2,1,0:T(8,128)(2,1)S(1)} %get-tuple-element.66), channel_id=1, source_target_pairs={{0,8},{1,9},{2,10},{3,11},{4,12},{5,13},{6,14},{7,15},{8,0},{9,1},... | collective-permute-start | bytes 282632 | tf_op jit(solution)/shard_map/ppermute | solution.py:21
  29.7 5.7 %collective-permute-start.7 = (bf16[18,16,128]{2,1,0:T(8,128)(2,1)S(1)}, bf16[18,16,128]{2,1,0:T(8,128)(2,1)S(1)}, u32[]{:S(2)}, u32[]{:S(2)}) collective-permute-start(bf16[18,16,128]{2,1,0:T(8,128)(2,1)S(1)} %get-tuple-element.64), channel_id=1, source_target_pairs={{0,24},{1,25},{2,26},{3,27},{4,28},{5,29},{6,30},{7,31},{8,16},{9,... | collective-permute-start | bytes 221192 | tf_op jit(solution)/shard_map/ppermute | solution.py:21
  35.4 9.4 %collective-permute-start.9 = (bf16[41,8,128]{2,1,0:T(8,128)(2,1)S(1)}, bf16[41,8,128]{2,1,0:T(8,128)(2,1)S(1)}, u32[]{:S(2)}, u32[]{:S(2)}) collective-permute-start(bf16[41,8,128]{2,1,0:T(8,128)(2,1)S(1)} %get-tuple-element.68), channel_id=1, source_target_pairs={{0,2},{1,3},{2,0},{3,1},{4,6},{5,7},{6,4},{7,5},{8,10},{9,11},{10,... | collective-permute-start | bytes 251912 | tf_op jit(solution)/shard_map/ppermute | solution.py:21
  44.9 6.2 %collective-permute-start.10 = (bf16[41,4,128]{2,1,0:T(4,128)(2,1)S(1)}, bf16[41,4,128]{2,1,0:T(4,128)(2,1)S(1)}, u32[]{:S(2)}, u32[]{:S(2)}) collective-permute-start(bf16[41,4,128]{2,1,0:T(4,128)(2,1)S(1)} %get-tuple-element.70), channel_id=1, source_target_pairs={{0,6},{1,7},{2,4},{3,5},{4,2},{5,3},{6,0},{7,1},{8,14},{9,15},{10,... | collective-permute-start | bytes 125960 | tf_op jit(solution)/shard_map/ppermute | solution.py:21
  51.1 4.1 %collective-permute-start.11 = (bf16[41,4,128]{2,1,0:T(4,128)(2,1)S(1)}, bf16[41,4,128]{2,1,0:T(4,128)(2,1)S(1)}, u32[]{:S(2)}, u32[]{:S(2)}) collective-permute-start(bf16[41,4,128]{2,1,0:T(4,128)(2,1)S(1)} %shard_map.76.refs_0_), channel_id=1, source_target_pairs={{0,32},{32,0},{64,96},{96,64},{128,160},{160,128},{192,224},{224,1... | collective-permute-start | bytes 125960 | tf_op jit(solution)/shard_map/ppermute | solution.py:21
  55.2 5.3 %collective-permute-start.12 = (bf16[41,4,128]{2,1,0:T(4,128)(2,1)S(1)}, bf16[41,4,128]{2,1,0:T(4,128)(2,1)S(1)}, u32[]{:S(2)}, u32[]{:S(2)}) collective-permute-start(bf16[41,4,128]{2,1,0:T(4,128)(2,1)S(1)} %shard_map.77.refs_0_), channel_id=1, source_target_pairs={{0,96},{32,64},{64,32},{96,0},{128,224},{160,192},{192,160},{224,1... | collective-permute-start | bytes 125960 | tf_op jit(solution)/shard_map/ppermute | solution.py:21
  60.6 4.1 %collective-permute-start.13 = (bf16[41,4,128]{2,1,0:T(4,128)(2,1)S(1)}, bf16[41,4,128]{2,1,0:T(4,128)(2,1)S(1)}, u32[]{:S(2)}, u32[]{:S(2)}) collective-permute-start(bf16[41,4,128]{2,1,0:T(4,128)(2,1)S(1)} %shard_map.78.own_ref), channel_id=1, source_target_pairs={{0,128},{32,160},{64,192},{96,224},{128,0},{160,32},{192,64},{224,... | collective-permute-start | bytes 125960 | tf_op jit(solution)/shard_map/ppermute | solution.py:21

commit v4 on v3

--- a/solution.py
+++ b/solution.py
@@ -1,5 +1,3 @@
-import functools
-
 import jax
 import jax.numpy as jnp
 from jax import lax
@@ -16,13 +14,26 @@
     return lax.ppermute(value, "space", [(i, (i + by) % 32) for i in range(32)])
 
 
-def swap(value, axis, bit):
-    size = {"space": 32, "dp": 8}[axis]
-    return lax.ppermute(value, axis, [(i, i ^ bit) for i in range(size)])
-
-
-CORE, X_ONE, X_TWO, Z_ONE, Z_TWO = 1, 8, 24, 2, 6
-Y_ONE, Y_TWO, Z_LOW = 1, 3, 4
+def swap_core(value):
+    return lax.ppermute(value, "space", [(i, i ^ 1) for i in range(32)])
+
+
+def partner(axis, step, core):
+    near = 1 if (step + core) % 2 == 0 else 3
+    return near << {"x": 3, "z": 1, "y": 0}[axis]
+
+
+def swap(value, axis, step):
+    if axis == "y":
+        pairs = [
+            (d * 32 + s, (d ^ partner(axis, step, s & 1)) * 32 + s) for d in range(8) for s in range(32)
+        ]
+        return lax.ppermute(value, ("dp", "space"), pairs)
+    return lax.ppermute(value, "space", [(s, s ^ partner(axis, step, s & 1)) for s in range(32)])
+
+
+def swap_z_low(value):
+    return lax.ppermute(value, "dp", [(d, d ^ 4) for d in range(8)])
 
 
 def leaky(values):
@@ -46,13 +57,14 @@
     return jnp.where(picked, 1.0, 0.0).astype(BF16)
 
 
-def channel_order(near, far):
+def channel_order():
     s = lax.axis_index("space")
     m = lax.broadcasted_iota(jnp.int32, (128, 128), 0)
     i = lax.broadcasted_iota(jnp.int32, (128, 128), 1)
     core = (m >> 6) ^ (s & 1)
+    near, far = 1 + 2 * core, 3 - 2 * core
     x = (near * ((m >> 5) & 1)) ^ (far * ((m >> 4) & 1)) ^ (s >> 3)
-    z = ((m >> 3) & 1) ^ (3 * ((m >> 2) & 1)) ^ ((s >> 1) & 3)
+    z = (near * ((m >> 3) & 1)) ^ (far * ((m >> 2) & 1)) ^ ((s >> 1) & 3)
     return jnp.where(i == x * 32 + z * 8 + core * 4 + (m & 3), 1.0, 0.0).astype(BF16)
 
 
@@ -145,7 +157,7 @@
 def lower_plane_kernel(
     rim_ref, got_ref, w_ref, f2b_ref, acc_ref, own_ref, up_ref,
     yr_ref, hid_ref, taps_ref, out_ref, gp_ref,
-    hs, us, os,
+    hs, us,
 ):
     inside = lax.axis_index("space") > 0
     spread_rows(rim_ref, rows_by_tap(inside), yr_ref)
@@ -159,10 +171,7 @@
     us[...] = up_ref[...].astype(F32).reshape(128, 128)
     up = jnp.concatenate([us[pl.ds(r, 8, stride=16), :] for r in range(16)], axis=0)
     gp_ref[...] = (up * jnp.where(pre > 0, 1.0, SLOPE)).astype(BF16)
-    out = leaky(pre)
-    for r in range(16):
-        os[pl.ds(r, 8, stride=16), :] = out[8 * r : 8 * r + 8]
-    out_ref[...] = os[...].astype(BF16).reshape(8, 16, 128)
+    out_ref[...] = leaky(pre)
 
 
 def second_grad(order, taps_ref, gp):
@@ -171,11 +180,15 @@
     return dot(jnp.concatenate(lhs, axis=0), gp).reshape(9, 128, 128)
 
 
-def second_grad_kernel(low_ref, up_ref, gp_ref, keep_ref, send_ref):
+def second_grad_kernel(low_ref, up_ref, gp_ref, pre_ref, keep_ref, send_ref, out_ref, os):
+    order = channel_order()
     for n, taps_ref in enumerate((low_ref, up_ref)):
-        grad = second_grad(channel_order(1, 3), taps_ref, gp_ref[...])
+        grad = second_grad(order, taps_ref, gp_ref[...])
         keep_ref[9 * n : 9 * n + 9] = grad[:, :64]
         send_ref[9 * n : 9 * n + 9] = grad[:, 64:].astype(BF16)
+    for r in range(16):
+        os[pl.ds(r, 8, stride=16), :] = pre_ref[8 * r : 8 * r + 8]
+    out_ref[...] = os[...].astype(BF16).reshape(8, 16, 128)
 
 
 def first_grad_kernel(
@@ -211,7 +224,7 @@
     for pu, h_ref in enumerate((h0_ref, h1_ref)):
         hid = h_ref[...].astype(F32)
         grads.append((gu[pu].reshape(512, 128) * jnp.where(hid > 0, 1.0, SLOPE)).astype(BF16))
-    order = channel_order(3, 1)
+    order = channel_order()
     turned = dot_nt(order, jnp.concatenate(grads, axis=0)).astype(BF16)
     planes = [yr_ref, y0_ref] + [y_ref.at[p] for p in range(3)]
     low = lax.broadcasted_iota(jnp.int32, (128, 128), 1) < 64
@@ -237,28 +250,20 @@
     send_ref[FIRST:] = grad[:, 64:].astype(BF16)
 
 
-def fold_kernel(groups, *refs):
-    count = 2 * sum(groups)
-    ins, outs = list(refs[:count]), list(refs[count:])
-    for parts in groups:
-        keep_ref, send_ref = outs.pop(0), outs.pop(0)
-        at = 0
-        for _ in range(parts):
-            own_ref, got_ref = ins.pop(0), ins.pop(0)
-            total = own_ref[...] + got_ref[...].astype(F32)
-            blocks, rows, _ = total.shape
-            keep_ref[at : at + blocks] = total[:, : rows // 2]
-            send_ref[at : at + blocks] = total[:, rows // 2 :].astype(BF16)
-            at += blocks
-
-
-def sum_kernel(*refs):
-    *ins, out_ref = refs
-    at = 0
-    for own_ref, got_ref in zip(ins[::2], ins[1::2]):
-        total = own_ref[...].astype(F32) + got_ref[...].astype(F32)
-        out_ref[at : at + total.shape[0]] = total.astype(BF16)
-        at += total.shape[0]
+def fold_kernel(own_ref, got_ref, keep_ref, send_ref):
+    total = own_ref[...] + got_ref[...].astype(F32)
+    half = total.shape[1] // 2
+    keep_ref[...] = total[:, :half]
+    send_ref[...] = total[:, half:].astype(BF16)
+
+
+def join_kernel(own_ref, got_ref, own2_ref, got2_ref, out_ref):
+    out_ref[:18] = (own_ref[...] + got_ref[...].astype(F32)).astype(BF16)
+    out_ref[18:] = (own2_ref[...] + got2_ref[...].astype(F32)).astype(BF16)
+
+
+def sum_kernel(own_ref, got_ref, out_ref):
+    out_ref[...] = (own_ref[...].astype(F32) + got_ref[...].astype(F32)).astype(BF16)
 
 
 def final_kernel(own_ref, got_ref, first_ref, second_ref):
@@ -293,16 +298,9 @@
     return pltpu.with_memory_space_constraint(value, HBM)
 
 
-def fold(*groups):
-    outs, args = [], []
-    for group in groups:
-        blocks = sum(own.shape[0] for own, _ in group)
-        half = (blocks, group[0][0].shape[1] // 2, 128)
-        outs += [(half, F32), (half, BF16)]
-        args += [array for pair in group for array in pair]
-    kernel = functools.partial(fold_kernel, [len(group) for group in groups])
-    done = call(kernel, outs, *args)
-    return list(zip(done[::2], done[1::2]))
+def fold(own, got):
+    half = (own.shape[0], own.shape[1] // 2, 128)
+    return call(fold_kernel, [(half, F32), (half, BF16)], own, got)
 
 
 def local(volumes, first_filter, second_filter, upstream_grad):
@@ -333,46 +331,44 @@
         slab, y, w, second, taps_up, spaces=[HBM, VMEM, VMEM, HBM, VMEM],
         scratch=[((32, 4096), BF16), pltpu.SemaphoreType.DMA((2,))], flops=10**9,
     )
-    y_rim, hidden_low, taps_low, second_out, grad_two = call(
+    y_rim, hidden_low, taps_low, out, grad_two = call(
         lower_plane_kernel,
         [
             (y_plane, BF16), ((512, 128), BF16), ((1152, 128), BF16),
-            ((8, 16, 128), BF16), ((128, 128), BF16),
+            tile, ((128, 128), BF16),
         ],
         rim, from_below, w, second_b, partial_low, from_up, upstream,
-        scratch=[hs, tile, tile], flops=4 * 10**8,
+        scratch=[hs, tile], flops=4 * 10**8,
     )
     grad_two_next = around_space(grad_two, -1)
-    keep2, send2 = call(
+    keep_a, send_a, second_out = call(
         second_grad_kernel,
-        [((18, 64, 128), F32), ((18, 64, 128), BF16)],
-        taps_low, taps_up, grad_two, flops=4 * 10**8,
-    )
-    send2, grad_two_next = lax.optimization_barrier((send2, grad_two_next))
-    blocks = FIRST + 9
-    keep1, send1 = call(
+        [((18, 64, 128), F32), ((18, 64, 128), BF16), ((8, 16, 128), BF16)],
+        taps_low, taps_up, grad_two, out, scratch=[tile], flops=4 * 10**8,
+    )
+    send_a, grad_two_next = lax.optimization_barrier((send_a, grad_two_next))
+    keep_b, send_b = call(
         first_grad_kernel,
-        [((blocks, 64, 128), F32), ((blocks, 64, 128), BF16)],
+        [((23, 64, 128), F32), ((23, 64, 128), BF16)],
         grad_two, grad_two_next, second_a, second_b, hidden_low, hidden_up,
         y_rim, y_low, y, taps_up,
         scratch=[((2, 17, 16, 128), F32), ((2, 16, 2, 16, 128), F32)], flops=8 * 10**8,
     )
-    s = "space"
-    got2, got1 = swap(send2, s, CORE), swap(send1, s, CORE)
-    (keep2, send2), (keep1, send1) = fold([(keep2, got2)], [(keep1, got1)])
-    got2, got1 = swap(send2, s, X_ONE), swap(send1, s, X_TWO)
-    (keep2, send2), (keep1, send1) = fold([(keep2, got2)], [(keep1, got1)])
-    got2, got1 = swap(send2, s, X_TWO), swap(send1, s, X_ONE)
-    ((keep, send),) = fold([(keep2, got2), (keep1, got1)])
-    ((keep, send),) = fold([(keep, swap(send, s, Z_ONE))])
+    keep_a, send_a = fold(keep_a, swap_core(send_a))
+    keep_b, send_b = fold(keep_b, swap_core(send_b))
+    for axis, step in (("x", 0), ("x", 1), ("z", 0)):
+        keep_a, send_a = fold(keep_a, swap(send_a, axis, step))
+        keep_b, send_b = fold(keep_b, swap(send_b, axis, step))
     total = ((FIRST + SECOND, 4, 128), BF16)
-    (both,) = call(sum_kernel, [total], keep, swap(send, s, Z_TWO))
-    (both,) = call(sum_kernel, [total], both, swap(both, "dp", Y_ONE))
-    (both,) = call(sum_kernel, [total], both, swap(both, "dp", Y_TWO))
+    (both,) = call(
+        join_kernel, [total], keep_a, swap(send_a, "z", 1), keep_b, swap(send_b, "z", 1)
+    )
+    (both,) = call(sum_kernel, [total], both, swap(both, "y", 0))
+    (both,) = call(sum_kernel, [total], both, swap(both, "y", 1))
     first_grad, second_grad = call(
         final_kernel,
         [((27, 4, 64), F32), ((27, 4, 128), F32)],
-        both, swap(both, "dp", Z_LOW),
+        both, swap_z_low(both),
     )
     return (
         second_out.reshape(1, 1, 8, 16, 128),

time: 66.4 us -> 64.4 us (0.970); the launches traced: 65.4 us -> 64.1 us
  waiting for transfers between devices: 32.6 us -> 24.4 us
  starting transfers between devices: 21.6 us -> 28.5 us
    ppermute x11 -> x13, waiting for transfers between devices: 28.5 us -> 20.9 us  [the longest x8 12.9 us: swap(): lax.ppermute(value, 'space', [(s, s ^ partner(axis, step, s & 1)) for s i...]
    ppermute x11 -> x13, starting transfers between devices: 18.1 us -> 24.9 us  [the longest x8 16.4 us: swap(): lax.ppermute(value, 'space', [(s, s ^ partner(axis, step, s & 1)) for s i...]
    pallas_call x13 -> x17, Pallas kernels: 9.53 us -> 9.45 us  [call(): pl.pallas_call(kernel, out_shape=[jax.ShapeDtypeStruct(shape, dtype) for...]
  transfers between devices with their start and end apart: 14 -> 16, of which waited for: 11 -> 12; matrix products, arithmetic and copies ran while one was open for 0% -> 0% of each run, Pallas kernels for 8% -> 10%
where the time goes in v4:
time: 64.4 us; the launch traced here: 64.1 us
  starting transfers between devices  28.5 us (44%)
  waiting for transfers between devices  24.4 us (38%)
  Pallas kernels  9.45 us (15%)
  local copies, waits for them, and re-layouts  0.97 us (2%)
  between operations  0.74 us (1%)
    ppermute x8, starting transfers between devices, swap(): lax.ppermute(value, 'space', [(s, s ^ partner(axis, step, s & 1)) for s i...  16.4 us
    ppermute x8, waiting for transfers between devices, swap(): lax.ppermute(value, 'space', [(s, s ^ partner(axis, step, s & 1)) for s i...  12.9 us
    pallas_call x17, Pallas kernels, call(): pl.pallas_call(kernel, out_shape=[jax.ShapeDtypeStruct(shape, dtype) for...  9.45 us
    ppermute x2, starting transfers between devices, swap(): return lax.ppermute(value, ('dp', 'space'), pairs)  4.75 us
    ppermute x2, waiting for transfers between devices, swap(): return lax.ppermute(value, ('dp', 'space'), pairs)  4.66 us
    ppermute x3, starting transfers between devices, around_space(): return lax.ppermute(value, 'space', [(i, (i + by) % 32) for i in range(32)])  3.6 us
    ppermute x3, waiting for transfers between devices, around_space(): return lax.ppermute(value, 'space', [(i, (i + by) % 32) for i in range(32)])  3.53 us
    ppermute x1, starting transfers between devices, swap_z_low(): return lax.ppermute(value, 'dp', [(d, d ^ 4) for d in range(8)])  2.06 us
  transfers between devices with their start and end apart: 16, of which 12 were waited for; matrix products, arithmetic and copies ran while one was open for 0% of the time, Pallas kernels for 10%

profile of v4, /device:TPU:6, one launch (start us, length us, event | category | flops | bytes accessed | tf_op | source)
XLA Modules:
  0.0 64.1 jit_solution(17111859037673372501)
XLA Ops:
  0.6 1.0 %slice_bitcast_fusion.rim_ref = bf16[32,4096]{1,0:T(8,128)(2,1)S(1)} fusion(bf16[1,4,32,4096]{3,2,1,0:T(8,128)(2,1)} %param.4), kind=kLoop, calls=%fused_computation | loop fusion | bytes 524288 | tf_op jit(solution)/shard_map/squeeze | solution.py:315
  1.7 2.7 %shard_map.67 = (bf16[3,3,33,16,128]{4,3,2,1,0:T(8,128)(2,1)S(1)}, bf16[2304,128]{1,0:T(8,128)(2,1)S(1)}, bf16[9,128,128]{2,1,0:T(8,128)(2,1)S(1)}, bf16[512,128...) custom-call(bf16[4,32,4096]{2,1,0:T(8,128)(2,1)} %bitcast.12, ...), custom_call_target="tpu_custom_call" | custom-call | flops 1000000000 | bytes 2637824 | tf_op jit(solution)/shard_map/pallas_call | solution.py:286
  4.4 3.4 %collective-permute-start.1 = (f32[128,128]{1,0:T(8,128)S(1)}, f32[128,128]{1,0:T(8,128)S(1)}, u32[]{:S(2)}, u32[]{:S(2)}) collective-permute-start(f32[128,128]{1,0:T(8,128)S(1)} %get-tuple-element.43), channel_id=1, source_target_pairs={{0,1},{1,2},{2,3},{3,4},{4,5},{5,6},{6,7},{7,8},{8,9},{9,10},{10,1... | collective-permute-start | bytes 196616 | tf_op jit(solution)/shard_map/ppermute | solution.py:14
  7.9 2.1 %shard_map.68 = (bf16[3,33,16,128]{3,2,1,0:T(8,128)(2,1)S(1)}, bf16[18,128,128]{2,1,0:T(8,128)(2,1)S(1)}, f32[512,128]{1,0:T(8,128)S(1)}, f32[128,128]{1,0:T(8,128)S(1)}) custom-call(bf16[4,32,4096]{2,1,0:T(8,128)(2,1)} %bitcast.13, bf16[3,3,33,16,128]{4,3,2,1,0:T(8,128)(2,1)S(1)} %get-tuple-element.45.y_ref, bf16[2304,128]{1,0:T(8,128)(2,1)S(1)} %get-tuple-element.44.w_ref, ...), custom_call_target="tpu_custom_call" | custom-call | flops 1000000000 | bytes 4034560 | tf_op jit(solution)/shard_map/pallas_call | solution.py:286
  10.0 3.1 %collective-permute-done.1.got_ref = f32[128,128]{1,0:T(8,128)S(1)} collective-permute-done((f32[128,128]{1,0:T(8,128)S(1)}, f32[128,128]{1,0:T(8,128)S(1)}, u32[]{:S(2)}, u32[]{:S(2)}) %collective-permute-start.1) | collective-permute-done | bytes 65568 | tf_op jit(solution)/shard_map/ppermute | solution.py:14
  13.0 0.9 %shard_map.69 = (bf16[3,33,16,128]{3,2,1,0:T(8,128)(2,1)S(1)}, bf16[512,128]{1,0:T(8,128)(2,1)S(1)}, bf16[1152,128]{1,0:T(8,128)(2,1)S(1)}, f32[128,128]{1,0:T(8,128)S(1)}, bf16[128,128]{1,0:T(8,128)(2,1)S(1)}) custom-call(bf16[32,4096]{1,0:T(8,128)(2,1)S(1)} %collective-permute-done.rim_ref, f32[128,128]{1,0:T(8,128)S(1)} %collective-permute-done.1.got_ref, ...), custom_call_target="tpu_custom_call" | custom-call | flops 400000000 | bytes 1867776 | tf_op jit(solution)/shard_map/pallas_call | solution.py:286
  14.1 1.1 %shard_map.70 = (f32[18,64,128]{2,1,0:T(8,128)S(1)}, bf16[18,64,128]{2,1,0:T(8,128)(2,1)S(1)}, bf16[8,16,128]{2,1,0:T(8,128)(2,1)}) custom-call(bf16[1152,128]{1,0:T(8,128)(2,1)S(1)} %get-tuple-element.50.low_ref, bf16[1152,128]{1,0:T(8,128)(2,1)S(1)} %get-tuple-element.46.taps_ref.up_ref, bf16[128,128]{1,0:T(8,128)(2,1)S(1)} %get-tuple-element.51.gp_ref, ...), custom_call_target="tpu_custom_call" | custom-call | flops 400000000 | bytes 688128 | tf_op jit(solution)/shard_map/pallas_call | solution.py:286
  15.2 0.4 collective-permute-done.2.gpn_ref
  15.6 1.5 %shard_map.75 = (f32[23,64,128]{2,1,0:T(8,128)S(1)}, bf16[23,64,128]{2,1,0:T(8,128)(2,1)S(1)}) custom-call(bf16[128,128]{1,0:T(8,128)(2,1)S(1)} %get-tuple-element.51.gp_ref, bf16[128,128]{1,0:T(8,128)(2,1)S(1)} %collective-permute-done.2.gpn_ref, bf16[9,128,128]{2,1,0:T(8,128)(2,1)S(1)} %get-tuple-element.66.fa_ref, ...), custom_call_target="tpu_custom_call" | custom-call | flops 800000000 | bytes 3534848 | tf_op jit(solution)/shard_map/pallas_call | solution.py:286
  17.2 1.6 %collective-permute-start.8 = (bf16[23,64,128]{2,1,0:T(8,128)(2,1)S(1)}, bf16[23,64,128]{2,1,0:T(8,128)(2,1)S(1)}, u32[]{:S(2)}, u32[]{:S(2)}) collective-permute-start(bf16[23,64,128]{2,1,0:T(8,128)(2,1)S(1)} %get-tuple-element.72), channel_id=1, source_target_pairs={{0,1},{1,0},{2,3},{3,2},{4,5},{5,4},{6,7},{7,6},{8,9},{9,8},{10,11... | collective-permute-start | bytes 1130504 | tf_op jit(solution)/shard_map/ppermute | solution.py:18
  18.9 1.2 %collective-permute-done.8.got_ref = bf16[23,64,128]{2,1,0:T(8,128)(2,1)S(1)} collective-permute-done((bf16[23,64,128]{2,1,0:T(8,128)(2,1)S(1)}, bf16[23,64,128]{2,1,0:T(8,128)(2,1)S(1)}, u32[]{:S(2)}, u32[]{:S(2)}) %collective-permute-start.8) | collective-permute-done | bytes 376864 | tf_op jit(solution)/shard_map/ppermute | solution.py:18
  20.2 0.9 %collective-permute-start.9 = (bf16[23,32,128]{2,1,0:T(8,128)(2,1)S(1)}, bf16[23,32,128]{2,1,0:T(8,128)(2,1)S(1)}, u32[]{:S(2)}, u32[]{:S(2)}) collective-permute-start(bf16[23,32,128]{2,1,0:T(8,128)(2,1)S(1)} %get-tuple-element.74), channel_id=1, source_target_pairs={{0,8},{1,25},{2,10},{3,27},{4,12},{5,29},{6,14},{7,31},{8,0},{9,17... | collective-permute-start | bytes 565256 | tf_op jit(solution)/shard_map/ppermute | solution.py:32
  21.2 1.3 %collective-permute-start.4 = (bf16[18,32,128]{2,1,0:T(8,128)(2,1)S(1)}, bf16[18,32,128]{2,1,0:T(8,128)(2,1)S(1)}, u32[]{:S(2)}, u32[]{:S(2)}) collective-permute-start(bf16[18,32,128]{2,1,0:T(8,128)(2,1)S(1)} %get-tuple-element.58), channel_id=1, source_target_pairs={{0,8},{1,25},{2,10},{3,27},{4,12},{5,29},{6,14},{7,31},{8,0},{9,17... | collective-permute-start | bytes 442376 | tf_op jit(solution)/shard_map/ppermute | solution.py:32
  22.5 3.4 %collective-permute-done.9.got_ref = bf16[23,32,128]{2,1,0:T(8,128)(2,1)S(1)} collective-permute-done((bf16[23,32,128]{2,1,0:T(8,128)(2,1)S(1)}, bf16[23,32,128]{2,1,0:T(8,128)(2,1)S(1)}, u32[]{:S(2)}, u32[]{:S(2)}) %collective-permute-start.9) | collective-permute-done | bytes 188448 | tf_op jit(solution)/shard_map/ppermute | solution.py:32
  25.9 1.3 %collective-permute-start.10 = (bf16[23,16,128]{2,1,0:T(8,128)(2,1)S(1)}, bf16[23,16,128]{2,1,0:T(8,128)(2,1)S(1)}, u32[]{:S(2)}, u32[]{:S(2)}) collective-permute-start(bf16[23,16,128]{2,1,0:T(8,128)(2,1)S(1)} %get-tuple-element.76), channel_id=1, source_target_pairs={{0,24},{1,9},{2,26},{3,11},{4,28},{5,13},{6,30},{7,15},{8,16},{9,1... | collective-permute-start | bytes 282632 | tf_op jit(solution)/shard_map/ppermute | solution.py:32
  27.2 0.2 collective-permute-done.4.got_ref
  27.5 1.9 %collective-permute-start.5 = (bf16[18,16,128]{2,1,0:T(8,128)(2,1)S(1)}, bf16[18,16,128]{2,1,0:T(8,128)(2,1)S(1)}, u32[]{:S(2)}, u32[]{:S(2)}) collective-permute-start(bf16[18,16,128]{2,1,0:T(8,128)(2,1)S(1)} %get-tuple-element.60), channel_id=1, source_target_pairs={{0,24},{1,9},{2,26},{3,11},{4,28},{5,13},{6,30},{7,15},{8,16},{9,1... | collective-permute-start | bytes 221192 | tf_op jit(solution)/shard_map/ppermute | solution.py:32
  29.4 2.4 %collective-permute-done.10.got_ref = bf16[23,16,128]{2,1,0:T(8,128)(2,1)S(1)} collective-permute-done((bf16[23,16,128]{2,1,0:T(8,128)(2,1)S(1)}, bf16[23,16,128]{2,1,0:T(8,128)(2,1)S(1)}, u32[]{:S(2)}, u32[]{:S(2)}) %collective-permute-start.10) | collective-permute-done | bytes 94240 | tf_op jit(solution)/shard_map/ppermute | solution.py:32
  31.8 7.0 %collective-permute-start.11 = (bf16[23,8,128]{2,1,0:T(8,128)(2,1)S(1)}, bf16[23,8,128]{2,1,0:T(8,128)(2,1)S(1)}, u32[]{:S(2)}, u32[]{:S(2)}) collective-permute-start(bf16[23,8,128]{2,1,0:T(8,128)(2,1)S(1)} %get-tuple-element.78), channel_id=1, source_target_pairs={{0,2},{1,7},{2,0},{3,5},{4,6},{5,3},{6,4},{7,1},{8,10},{9,15},{10,... | collective-permute-start | bytes 141320 | tf_op jit(solution)/shard_map/ppermute | solution.py:32
  38.8 1.3 %collective-permute-start.6 = (bf16[18,8,128]{2,1,0:T(8,128)(2,1)S(1)}, bf16[18,8,128]{2,1,0:T(8,128)(2,1)S(1)}, u32[]{:S(2)}, u32[]{:S(2)}) collective-permute-start(bf16[18,8,128]{2,1,0:T(8,128)(2,1)S(1)} %get-tuple-element.62), channel_id=1, source_target_pairs={{0,2},{1,7},{2,0},{3,5},{4,6},{5,3},{6,4},{7,1},{8,10},{9,15},{10,... | collective-permute-start | bytes 110600 | tf_op jit(solution)/shard_map/ppermute | solution.py:32
  40.1 0.7 %collective-permute-done.11.got_ref = bf16[23,8,128]{2,1,0:T(8,128)(2,1)S(1)} collective-permute-done((bf16[23,8,128]{2,1,0:T(8,128)(2,1)S(1)}, bf16[23,8,128]{2,1,0:T(8,128)(2,1)S(1)}, u32[]{:S(2)}, u32[]{:S(2)}) %collective-permute-start.11) | collective-permute-done | bytes 47136 | tf_op jit(solution)/shard_map/ppermute | solution.py:32
  40.8 1.3 %collective-permute-start.12 = (bf16[23,4,128]{2,1,0:T(4,128)(2,1)S(1)}, bf16[23,4,128]{2,1,0:T(4,128)(2,1)S(1)}, u32[]{:S(2)}, u32[]{:S(2)}) collective-permute-start(bf16[23,4,128]{2,1,0:T(4,128)(2,1)S(1)} %get-tuple-element.80), channel_id=1, source_target_pairs={{0,6},{1,3},{2,4},{3,1},{4,2},{5,7},{6,0},{7,5},{8,14},{9,11},{10,... | collective-permute-start | bytes 70664 | tf_op jit(solution)/shard_map/ppermute | solution.py:32
  42.1 1.6 %collective-permute-done.6.got_ref = bf16[18,8,128]{2,1,0:T(8,128)(2,1)S(1)} collective-permute-done((bf16[18,8,128]{2,1,0:T(8,128)(2,1)S(1)}, bf16[18,8,128]{2,1,0:T(8,128)(2,1)S(1)}, u32[]{:S(2)}, u32[]{:S(2)}) %collective-permute-start.6) | collective-permute-done | bytes 36896 | tf_op jit(solution)/shard_map/ppermute | solution.py:32
  43.8 1.4 %collective-permute-start.7 = (bf16[18,4,128]{2,1,0:T(4,128)(2,1)S(1)}, bf16[18,4,128]{2,1,0:T(4,128)(2,1)S(1)}, u32[]{:S(2)}, u32[]{:S(2)}) collective-permute-start(bf16[18,4,128]{2,1,0:T(4,128)(2,1)S(1)} %get-tuple-element.64), channel_id=1, source_target_pairs={{0,6},{1,3},{2,4},{3,1},{4,2},{5,7},{6,0},{7,5},{8,14},{9,11},{10,... | collective-permute-start | bytes 55304 | tf_op jit(solution)/shard_map/ppermute | solution.py:32
  45.2 4.6 %collective-permute-done.7.got_ref = bf16[18,4,128]{2,1,0:T(4,128)(2,1)S(1)} collective-permute-done((bf16[18,4,128]{2,1,0:T(4,128)(2,1)S(1)}, bf16[18,4,128]{2,1,0:T(4,128)(2,1)S(1)}, u32[]{:S(2)}, u32[]{:S(2)}) %collective-permute-start.7) | collective-permute-done | bytes 18464 | tf_op jit(solution)/shard_map/ppermute | solution.py:32
  49.8 1.7 %collective-permute-start.13 = (bf16[41,4,128]{2,1,0:T(4,128)(2,1)S(1)}, bf16[41,4,128]{2,1,0:T(4,128)(2,1)S(1)}, u32[]{:S(2)}, u32[]{:S(2)}) collective-permute-start(bf16[41,4,128]{2,1,0:T(4,128)(2,1)S(1)} %shard_map.80.own_ref), channel_id=1, source_target_pairs={{0,32},{1,97},{2,34},{3,99},{4,36},{5,101},{6,38},{7,103},{8,40},{... | collective-permute-start | bytes 125960 | tf_op jit(solution)/shard_map/ppermute | solution.py:31
  51.4 2.4 %collective-permute-done.13.got_ref = bf16[41,4,128]{2,1,0:T(4,128)(2,1)S(1)} collective-permute-done((bf16[41,4,128]{2,1,0:T(4,128)(2,1)S(1)}, bf16[41,4,128]{2,1,0:T(4,128)(2,1)S(1)}, u32[]{:S(2)}, u32[]{:S(2)}) %collective-permute-start.13) | collective-permute-done | bytes 42016 | tf_op jit(solution)/shard_map/ppermute | solution.py:31
  53.9 3.1 %collective-permute-start.14 = (bf16[41,4,128]{2,1,0:T(4,128)(2,1)S(1)}, bf16[41,4,128]{2,1,0:T(4,128)(2,1)S(1)}, u32[]{:S(2)}, u32[]{:S(2)}) collective-permute-start(bf16[41,4,128]{2,1,0:T(4,128)(2,1)S(1)} %shard_map.81.own_ref), channel_id=1, source_target_pairs={{0,96},{1,33},{2,98},{3,35},{4,100},{5,37},{6,102},{7,39},{8,104},... | collective-permute-start | bytes 125960 | tf_op jit(solution)/shard_map/ppermute | solution.py:31
  57.0 2.2 %collective-permute-done.14.got_ref = bf16[41,4,128]{2,1,0:T(4,128)(2,1)S(1)} collective-permute-done((bf16[41,4,128]{2,1,0:T(4,128)(2,1)S(1)}, bf16[41,4,128]{2,1,0:T(4,128)(2,1)S(1)}, u32[]{:S(2)}, u32[]{:S(2)}) %collective-permute-start.14) | collective-permute-done | bytes 42016 | tf_op jit(solution)/shard_map/ppermute | solution.py:31
  59.2 2.1 %collective-permute-start.15 = (bf16[41,4,128]{2,1,0:T(4,128)(2,1)S(1)}, bf16[41,4,128]{2,1,0:T(4,128)(2,1)S(1)}, u32[]{:S(2)}, u32[]{:S(2)}) collective-permute-start(bf16[41,4,128]{2,1,0:T(4,128)(2,1)S(1)} %shard_map.82.own_ref), channel_id=1, source_target_pairs={{0,128},{32,160},{64,192},{96,224},{128,0},{160,32},{192,64},{224,... | collective-permute-start | bytes 125960 | tf_op jit(solution)/shard_map/ppermute | solution.py:36
  61.3 2.0 %collective-permute-done.15.got_ref = bf16[41,4,128]{2,1,0:T(4,128)(2,1)S(1)} collective-permute-done((bf16[41,4,128]{2,1,0:T(4,128)(2,1)S(1)}, bf16[41,4,128]{2,1,0:T(4,128)(2,1)S(1)}, u32[]{:S(2)}, u32[]{:S(2)}) %collective-permute-start.15) | collective-permute-done | bytes 42016 | tf_op jit(solution)/shard_map/ppermute | solution.py:36
  63.3 0.7 %shard_map.83 = (f32[27,4,64]{2,1,0:T(4,128)}, f32[27,4,128]{2,1,0:T(4,128)}) custom-call(bf16[41,4,128]{2,1,0:T(4,128)(2,1)S(1)} %shard_map.82.own_ref, bf16[41,4,128]{2,1,0:T(4,128)(2,1)S(1)} %collective-permute-done.15.got_ref), custom_call_target="tpu_custom_call" | custom-call | flops 1000000 | bytes 83968 | tf_op jit(solution)/shard_map/pallas_call | solution.py:286
  (20 shorter events, 0.6 us)
Async XLA Ops:
  1.6 11.4 %collective-permute-start = (bf16[32,4096]{1,0:T(8,128)(2,1)S(1)}, bf16[32,4096]{1,0:T(8,128)(2,1)S(1)}, u32[]{:S(2)}, u32[]{:S(2)}) collective-permute-start(bf16[32,4096]{1,0:T(8,128)(2,1)S(1)} %slice_bitcast_fusion.rim_ref), channel_id=1, source_target_pairs={{0,1},{1,2},{2,3},{3,4},{4,5},{5,6},{6,7},{7,8},{8,9},{9,10},{10,1... | collective-permute-start | bytes 786440 | tf_op jit(solution)/shard_map/ppermute | solution.py:14
  4.4 8.6 %collective-permute-start.1 = (f32[128,128]{1,0:T(8,128)S(1)}, f32[128,128]{1,0:T(8,128)S(1)}, u32[]{:S(2)}, u32[]{:S(2)}) collective-permute-start(f32[128,128]{1,0:T(8,128)S(1)} %get-tuple-element.43), channel_id=1, source_target_pairs={{0,1},{1,2},{2,3},{3,4},{4,5},{5,6},{6,7},{7,8},{8,9},{9,10},{10,1... | collective-permute-start | bytes 196616 | tf_op jit(solution)/shard_map/ppermute | solution.py:14
  7.9 5.2 %copy-start = (bf16[1,1,8,16,128]{4,3,2,1,0:T(8,128)(2,1)S(1)}, bf16[1,1,8,16,128]{4,3,2,1,0:T(8,128)(2,1)}, u32[]{:S(2)}) copy-start(bf16[1,1,8,16,128]{4,3,2,1,0:T(8,128)(2,1)} %param.7) | copy-start | bytes 98308
  14.0 1.7 %collective-permute-start.2 = (bf16[128,128]{1,0:T(8,128)(2,1)S(1)}, bf16[128,128]{1,0:T(8,128)(2,1)S(1)}, u32[]{:S(2)}, u32[]{:S(2)}) collective-permute-start(bf16[128,128]{1,0:T(8,128)(2,1)S(1)} %get-tuple-element.51.gp_ref), channel_id=1, source_target_pairs={{0,31},{1,0},{2,1},{3,2},{4,3},{5,4},{6,5},{7,6},{8,7},{9,8},{10,9... | collective-permute-start | bytes 98312 | tf_op jit(solution)/shard_map/ppermute | solution.py:14
  17.2 2.9 %collective-permute-start.8 = (bf16[23,64,128]{2,1,0:T(8,128)(2,1)S(1)}, bf16[23,64,128]{2,1,0:T(8,128)(2,1)S(1)}, u32[]{:S(2)}, u32[]{:S(2)}) collective-permute-start(bf16[23,64,128]{2,1,0:T(8,128)(2,1)S(1)} %get-tuple-element.72), channel_id=1, source_target_pairs={{0,1},{1,0},{2,3},{3,2},{4,5},{5,4},{6,7},{7,6},{8,9},{9,8},{10,11... | collective-permute-start | bytes 1130504 | tf_op jit(solution)/shard_map/ppermute | solution.py:18
  18.8 2.3 %collective-permute-start.3 = (bf16[18,64,128]{2,1,0:T(8,128)(2,1)S(1)}, bf16[18,64,128]{2,1,0:T(8,128)(2,1)S(1)}, u32[]{:S(2)}, u32[]{:S(2)}) collective-permute-start(bf16[18,64,128]{2,1,0:T(8,128)(2,1)S(1)} %get-tuple-element.56), channel_id=1, source_target_pairs={{0,1},{1,0},{2,3},{3,2},{4,5},{5,4},{6,7},{7,6},{8,9},{9,8},{10,11... | collective-permute-start | bytes 884744 | tf_op jit(solution)/shard_map/ppermute | solution.py:18
  20.2 5.7 %collective-permute-start.9 = (bf16[23,32,128]{2,1,0:T(8,128)(2,1)S(1)}, bf16[23,32,128]{2,1,0:T(8,128)(2,1)S(1)}, u32[]{:S(2)}, u32[]{:S(2)}) collective-permute-start(bf16[23,32,128]{2,1,0:T(8,128)(2,1)S(1)} %get-tuple-element.74), channel_id=1, source_target_pairs={{0,8},{1,25},{2,10},{3,27},{4,12},{5,29},{6,14},{7,31},{8,0},{9,17... | collective-permute-start | bytes 565256 | tf_op jit(solution)/shard_map/ppermute | solution.py:32
  21.2 6.3 %collective-permute-start.4 = (bf16[18,32,128]{2,1,0:T(8,128)(2,1)S(1)}, bf16[18,32,128]{2,1,0:T(8,128)(2,1)S(1)}, u32[]{:S(2)}, u32[]{:S(2)}) collective-permute-start(bf16[18,32,128]{2,1,0:T(8,128)(2,1)S(1)} %get-tuple-element.58), channel_id=1, source_target_pairs={{0,8},{1,25},{2,10},{3,27},{4,12},{5,29},{6,14},{7,31},{8,0},{9,17... | collective-permute-start | bytes 442376 | tf_op jit(solution)/shard_map/ppermute | solution.py:32
  25.9 5.9 %collective-permute-start.10 = (bf16[23,16,128]{2,1,0:T(8,128)(2,1)S(1)}, bf16[23,16,128]{2,1,0:T(8,128)(2,1)S(1)}, u32[]{:S(2)}, u32[]{:S(2)}) collective-permute-start(bf16[23,16,128]{2,1,0:T(8,128)(2,1)S(1)} %get-tuple-element.76), channel_id=1, source_target_pairs={{0,24},{1,9},{2,26},{3,11},{4,28},{5,13},{6,30},{7,15},{8,16},{9,1... | collective-permute-start | bytes 282632 | tf_op jit(solution)/shard_map/ppermute | solution.py:32
  27.5 11.3 %collective-permute-start.5 = (bf16[18,16,128]{2,1,0:T(8,128)(2,1)S(1)}, bf16[18,16,128]{2,1,0:T(8,128)(2,1)S(1)}, u32[]{:S(2)}, u32[]{:S(2)}) collective-permute-start(bf16[18,16,128]{2,1,0:T(8,128)(2,1)S(1)} %get-tuple-element.60), channel_id=1, source_target_pairs={{0,24},{1,9},{2,26},{3,11},{4,28},{5,13},{6,30},{7,15},{8,16},{9,1... | collective-permute-start | bytes 221192 | tf_op jit(solution)/shard_map/ppermute | solution.py:32
  31.8 9.0 %collective-permute-start.11 = (bf16[23,8,128]{2,1,0:T(8,128)(2,1)S(1)}, bf16[23,8,128]{2,1,0:T(8,128)(2,1)S(1)}, u32[]{:S(2)}, u32[]{:S(2)}) collective-permute-start(bf16[23,8,128]{2,1,0:T(8,128)(2,1)S(1)} %get-tuple-element.78), channel_id=1, source_target_pairs={{0,2},{1,7},{2,0},{3,5},{4,6},{5,3},{6,4},{7,1},{8,10},{9,15},{10,... | collective-permute-start | bytes 141320 | tf_op jit(solution)/shard_map/ppermute | solution.py:32
  38.8 5.0 %collective-permute-start.6 = (bf16[18,8,128]{2,1,0:T(8,128)(2,1)S(1)}, bf16[18,8,128]{2,1,0:T(8,128)(2,1)S(1)}, u32[]{:S(2)}, u32[]{:S(2)}) collective-permute-start(bf16[18,8,128]{2,1,0:T(8,128)(2,1)S(1)} %get-tuple-element.62), channel_id=1, source_target_pairs={{0,2},{1,7},{2,0},{3,5},{4,6},{5,3},{6,4},{7,1},{8,10},{9,15},{10,... | collective-permute-start | bytes 110600 | tf_op jit(solution)/shard_map/ppermute | solution.py:32
  40.8 8.9 %collective-permute-start.12 = (bf16[23,4,128]{2,1,0:T(4,128)(2,1)S(1)}, bf16[23,4,128]{2,1,0:T(4,128)(2,1)S(1)}, u32[]{:S(2)}, u32[]{:S(2)}) collective-permute-start(bf16[23,4,128]{2,1,0:T(4,128)(2,1)S(1)} %get-tuple-element.80), channel_id=1, source_target_pairs={{0,6},{1,3},{2,4},{3,1},{4,2},{5,7},{6,0},{7,5},{8,14},{9,11},{10,... | collective-permute-start | bytes 70664 | tf_op jit(solution)/shard_map/ppermute | solution.py:32
  43.8 6.0 %collective-permute-start.7 = (bf16[18,4,128]{2,1,0:T(4,128)(2,1)S(1)}, bf16[18,4,128]{2,1,0:T(4,128)(2,1)S(1)}, u32[]{:S(2)}, u32[]{:S(2)}) collective-permute-start(bf16[18,4,128]{2,1,0:T(4,128)(2,1)S(1)} %get-tuple-element.64), channel_id=1, source_target_pairs={{0,6},{1,3},{2,4},{3,1},{4,2},{5,7},{6,0},{7,5},{8,14},{9,11},{10,... | collective-permute-start | bytes 55304 | tf_op jit(solution)/shard_map/ppermute | solution.py:32
  49.8 4.1 %collective-permute-start.13 = (bf16[41,4,128]{2,1,0:T(4,128)(2,1)S(1)}, bf16[41,4,128]{2,1,0:T(4,128)(2,1)S(1)}, u32[]{:S(2)}, u32[]{:S(2)}) collective-permute-start(bf16[41,4,128]{2,1,0:T(4,128)(2,1)S(1)} %shard_map.80.own_ref), channel_id=1, source_target_pairs={{0,32},{1,97},{2,34},{3,99},{4,36},{5,101},{6,38},{7,103},{8,40},{... | collective-permute-start | bytes 125960 | tf_op jit(solution)/shard_map/ppermute | solution.py:31
  53.9 5.3 %collective-permute-start.14 = (bf16[41,4,128]{2,1,0:T(4,128)(2,1)S(1)}, bf16[41,4,128]{2,1,0:T(4,128)(2,1)S(1)}, u32[]{:S(2)}, u32[]{:S(2)}) collective-permute-start(bf16[41,4,128]{2,1,0:T(4,128)(2,1)S(1)} %shard_map.81.own_ref), channel_id=1, source_target_pairs={{0,96},{1,33},{2,98},{3,35},{4,100},{5,37},{6,102},{7,39},{8,104},... | collective-permute-start | bytes 125960 | tf_op jit(solution)/shard_map/ppermute | solution.py:31
  59.2 4.1 %collective-permute-start.15 = (bf16[41,4,128]{2,1,0:T(4,128)(2,1)S(1)}, bf16[41,4,128]{2,1,0:T(4,128)(2,1)S(1)}, u32[]{:S(2)}, u32[]{:S(2)}) collective-permute-start(bf16[41,4,128]{2,1,0:T(4,128)(2,1)S(1)} %shard_map.82.own_ref), channel_id=1, source_target_pairs={{0,128},{32,160},{64,192},{96,224},{128,0},{160,32},{192,64},{224,... | collective-permute-start | bytes 125960 | tf_op jit(solution)/shard_map/ppermute | solution.py:36

commit v5 on v4

--- a/solution.py
+++ b/solution.py
@@ -1,3 +1,5 @@
+import functools
+
 import jax
 import jax.numpy as jnp
 from jax import lax
@@ -18,18 +20,20 @@
     return lax.ppermute(value, "space", [(i, i ^ 1) for i in range(32)])
 
 
-def partner(axis, step, core):
-    near = 1 if (step + core) % 2 == 0 else 3
-    return near << {"x": 3, "z": 1, "y": 0}[axis]
-
-
-def swap(value, axis, step):
-    if axis == "y":
-        pairs = [
-            (d * 32 + s, (d ^ partner(axis, step, s & 1)) * 32 + s) for d in range(8) for s in range(32)
-        ]
-        return lax.ppermute(value, ("dp", "space"), pairs)
-    return lax.ppermute(value, "space", [(s, s ^ partner(axis, step, s & 1)) for s in range(32)])
+def partner(step, core):
+    return 1 if (step + core) % 2 == 0 else 3
+
+
+def swap_x(value, step):
+    return lax.ppermute(value, "space", [(s, s ^ (partner(step, s & 1) << 3)) for s in range(32)])
+
+
+def swap_z(value, slot):
+    return lax.ppermute(value, "space", [(s, s ^ (slot << 1)) for s in range(32)])
+
+
+def swap_y(value, slot):
+    return lax.ppermute(value, "dp", [(d, d ^ slot) for d in range(8)])
 
 
 def swap_z_low(value):
@@ -64,7 +68,7 @@
     core = (m >> 6) ^ (s & 1)
     near, far = 1 + 2 * core, 3 - 2 * core
     x = (near * ((m >> 5) & 1)) ^ (far * ((m >> 4) & 1)) ^ (s >> 3)
-    z = (near * ((m >> 3) & 1)) ^ (far * ((m >> 2) & 1)) ^ ((s >> 1) & 3)
+    z = ((m >> 2) & 3) ^ ((s >> 1) & 3)
     return jnp.where(i == x * 32 + z * 8 + core * 4 + (m & 3), 1.0, 0.0).astype(BF16)
 
 
@@ -180,7 +184,40 @@
     return dot(jnp.concatenate(lhs, axis=0), gp).reshape(9, 128, 128)
 
 
-def second_grad_kernel(low_ref, up_ref, gp_ref, pre_ref, keep_ref, send_ref, out_ref, os):
+def lay_out(gs, at, grad):
+    gs[at] = jnp.zeros((17, 16, 128), F32)
+    gs[at, 0:16, 0:8, :] = grad.reshape(16, 8, 128)
+
+
+def hidden_grad(gs, gu, sources, hid_ref, order):
+    moved = {
+        (s, dr, dq): gs[s, dr : dr + 16, dq : dq + 8, :].reshape(128, 128).astype(BF16)
+        for s, _ in sources
+        for dr in range(2)
+        for dq in range(2)
+    }
+    one_d = {0: [(0, 1)], 1: [(0, 2), (1, 0)]}
+    for pv in range(2):
+        for pw in range(2):
+            lhs, rhs = [], []
+            for s, f_ref in sources:
+                for dq, b in one_d[pv]:
+                    for dr, c in one_d[pw]:
+                        lhs.append(moved[s, dr, dq])
+                        rhs.append(f_ref[3 * b + c])
+            grad = dot_nt(jnp.concatenate(lhs, axis=1), jnp.concatenate(rhs, axis=1))
+            grad = grad.astype(BF16).astype(F32).reshape(16, 8, 128)
+            gu[:, pw, pl.ds(pv, 8, stride=2), :] = grad
+    hid = hid_ref[...].astype(F32)
+    grad = (gu[...].reshape(512, 128) * jnp.where(hid > 0, 1.0, SLOPE)).astype(BF16)
+    return dot_nt(order, grad).astype(BF16)
+
+
+def second_grad_kernel(
+    low_ref, up_ref, gp_ref, pre_ref, fb_ref, hid_ref, yr_ref, y0_ref, y_ref,
+    keep_ref, send_ref, out_ref, part_ref,
+    os, gs, gu,
+):
     order = channel_order()
     for n, taps_ref in enumerate((low_ref, up_ref)):
         grad = second_grad(order, taps_ref, gp_ref[...])
@@ -189,44 +226,23 @@
     for r in range(16):
         os[pl.ds(r, 8, stride=16), :] = pre_ref[8 * r : 8 * r + 8]
     out_ref[...] = os[...].astype(BF16).reshape(8, 16, 128)
+    lay_out(gs, 0, gp_ref[...].astype(F32))
+    turned = hidden_grad(gs, gu, [(0, fb_ref.at[0:9])], hid_ref, order)
+    for a, plane in enumerate((yr_ref, y0_ref, y_ref.at[0])):
+        for b in range(3):
+            part_ref[3 * a + b] = dot(turned, columns(plane, b))
 
 
 def first_grad_kernel(
-    gp_ref, gpn_ref, fa_ref, fb_ref, h0_ref, h1_ref, yr_ref, y0_ref, y_ref, taps_ref,
-    keep_ref, send_ref, gs, gu,
+    gp_ref, gpn_ref, fa_ref, fb_ref, hid_ref, y_ref, taps_ref, part_ref,
+    keep_ref, send_ref,
+    gs, gu,
 ):
-    inside = jnp.where(lax.axis_index("space") < 31, 1.0, 0.0)
-    gs[...] = jnp.zeros_like(gs)
-    gs[0, 0:16, 0:8, :] = gp_ref[...].astype(F32).reshape(16, 8, 128)
-    above = gpn_ref[...].astype(F32) * inside
-    gs[1, 0:16, 0:8, :] = above.reshape(16, 8, 128)
-    moved = {
-        (s, dr, dq): gs[s, dr : dr + 16, dq : dq + 8, :].reshape(128, 128).astype(BF16)
-        for s in range(2)
-        for dr in range(2)
-        for dq in range(2)
-    }
-    one_d = {0: [(0, 1)], 1: [(0, 2), (1, 0)]}
-    for pu in range(2):
-        for pv in range(2):
-            for pw in range(2):
-                lhs, rhs = [], []
-                for s, a in one_d[pu]:
-                    for dq, b in one_d[pv]:
-                        for dr, c in one_d[pw]:
-                            lhs.append(moved[s, dr, dq])
-                            tap = 9 * a + 3 * b + c
-                            rhs.append(fb_ref[tap - 9] if a else fa_ref[tap])
-                grad = dot_nt(jnp.concatenate(lhs, axis=1), jnp.concatenate(rhs, axis=1))
-                grad = grad.astype(BF16).astype(F32).reshape(16, 8, 128)
-                gu[pu, :, pw, pl.ds(pv, 8, stride=2), :] = grad
-    grads = []
-    for pu, h_ref in enumerate((h0_ref, h1_ref)):
-        hid = h_ref[...].astype(F32)
-        grads.append((gu[pu].reshape(512, 128) * jnp.where(hid > 0, 1.0, SLOPE)).astype(BF16))
+    above = gpn_ref[...].astype(F32) * jnp.where(lax.axis_index("space") < 31, 1.0, 0.0)
+    lay_out(gs, 0, gp_ref[...].astype(F32))
+    lay_out(gs, 1, above)
     order = channel_order()
-    turned = dot_nt(order, jnp.concatenate(grads, axis=0)).astype(BF16)
-    planes = [yr_ref, y0_ref] + [y_ref.at[p] for p in range(3)]
+    turned = hidden_grad(gs, gu, [(0, fb_ref.at[9:18]), (1, fa_ref)], hid_ref, order)
     low = lax.broadcasted_iota(jnp.int32, (128, 128), 1) < 64
 
     def put(block, grad):
@@ -237,8 +253,7 @@
     for a in range(3):
         for b in range(3):
             ab = 3 * a + b
-            rhs = jnp.concatenate([columns(planes[a], b), columns(planes[a + 2], b)], axis=0)
-            grad = dot(turned, rhs)
+            grad = part_ref[ab] + dot(turned, columns(y_ref.at[a], b))
             put(ab, grad[:, 128:])
             if ab % 2 == 0:
                 held = pltpu.roll(grad[:, :128], 64, axis=1)
@@ -257,13 +272,20 @@
     send_ref[...] = total[:, half:].astype(BF16)
 
 
-def join_kernel(own_ref, got_ref, own2_ref, got2_ref, out_ref):
-    out_ref[:18] = (own_ref[...] + got_ref[...].astype(F32)).astype(BF16)
-    out_ref[18:] = (own2_ref[...] + got2_ref[...].astype(F32)).astype(BF16)
-
-
-def sum_kernel(own_ref, got_ref, out_ref):
-    out_ref[...] = (own_ref[...].astype(F32) + got_ref[...].astype(F32)).astype(BF16)
+def join_kernel(own_ref, got_ref, own2_ref, got2_ref, keep_ref, far_ref, s1_ref, s3_ref):
+    for blocks, own, got in ((slice(0, 18), own_ref, got_ref), (slice(18, 41), own2_ref, got2_ref)):
+        total = own[...] + got[...].astype(F32)
+        keep_ref[blocks] = total[:, 0:4]
+        s1_ref[blocks] = total[:, 4:8].astype(BF16)
+        far_ref[blocks] = total[:, 8:12].astype(BF16)
+        s3_ref[blocks] = total[:, 12:16].astype(BF16)
+
+
+def four_kernel(far_at, own_ref, *refs):
+    far_ref, a_ref, b_ref = (refs[(n + far_at) % 3] for n in range(3))
+    out_ref = refs[3]
+    own, far, a, b = (ref[...].astype(F32) for ref in (own_ref, far_ref, a_ref, b_ref))
+    out_ref[...] = ((own + a) + (b + far)).astype(BF16)
 
 
 def final_kernel(own_ref, got_ref, first_ref, second_ref):
@@ -341,30 +363,41 @@
         scratch=[hs, tile], flops=4 * 10**8,
     )
     grad_two_next = around_space(grad_two, -1)
-    keep_a, send_a, second_out = call(
+    rows = ((2, 17, 16, 128), F32)
+    plane = ((16, 2, 16, 128), F32)
+    keep_a, send_a, second_out, part = call(
         second_grad_kernel,
-        [((18, 64, 128), F32), ((18, 64, 128), BF16), ((8, 16, 128), BF16)],
-        taps_low, taps_up, grad_two, out, scratch=[tile], flops=4 * 10**8,
-    )
-    send_a, grad_two_next = lax.optimization_barrier((send_a, grad_two_next))
+        [
+            ((18, 64, 128), F32), ((18, 64, 128), BF16), ((8, 16, 128), BF16),
+            ((9, 128, 256), F32),
+        ],
+        taps_low, taps_up, grad_two, out, second_b, hidden_low, y_rim, y_low, y,
+        scratch=[tile, rows, plane], flops=8 * 10**8,
+    )
     keep_b, send_b = call(
         first_grad_kernel,
         [((23, 64, 128), F32), ((23, 64, 128), BF16)],
-        grad_two, grad_two_next, second_a, second_b, hidden_low, hidden_up,
-        y_rim, y_low, y, taps_up,
-        scratch=[((2, 17, 16, 128), F32), ((2, 16, 2, 16, 128), F32)], flops=8 * 10**8,
-    )
+        grad_two, grad_two_next, second_a, second_b, hidden_up, y, taps_up, part,
+        scratch=[rows, plane], flops=8 * 10**8,
+    )
+    send_a, send_b = lax.optimization_barrier((send_a, send_b))
     keep_a, send_a = fold(keep_a, swap_core(send_a))
     keep_b, send_b = fold(keep_b, swap_core(send_b))
-    for axis, step in (("x", 0), ("x", 1), ("z", 0)):
-        keep_a, send_a = fold(keep_a, swap(send_a, axis, step))
-        keep_b, send_b = fold(keep_b, swap(send_b, axis, step))
-    total = ((FIRST + SECOND, 4, 128), BF16)
+    keep_a, send_a = fold(keep_a, swap_x(send_a, 0))
+    keep_b, send_b = fold(keep_b, swap_x(send_b, 0))
+    part = (FIRST + SECOND, 4, 128)
+    keep, far, one, three = call(
+        join_kernel, [(part, F32), (part, BF16), (part, BF16), (part, BF16)],
+        keep_a, swap_x(send_a, 1), keep_b, swap_x(send_b, 1),
+    )
     (both,) = call(
-        join_kernel, [total], keep_a, swap(send_a, "z", 1), keep_b, swap(send_b, "z", 1)
-    )
-    (both,) = call(sum_kernel, [total], both, swap(both, "y", 0))
-    (both,) = call(sum_kernel, [total], both, swap(both, "y", 1))
+        functools.partial(four_kernel, 1), [(part, BF16)],
+        keep, swap_z(one, 1), swap_z(far, 2), swap_z(three, 3),
+    )
+    (both,) = call(
+        functools.partial(four_kernel, 0), [(part, BF16)],
+        both, swap_y(both, 2), swap_y(both, 1), swap_y(both, 3),
+    )
     first_grad, second_grad = call(
         final_kernel,
         [((27, 4, 64), F32), ((27, 4, 128), F32)],

time: 64.4 us -> 62.6 us (0.972)
  starting transfers between devices: 28.5 us -> 25.5 us
  waiting for transfers between devices: 24.4 us -> 25.4 us
    ppermute x1, starting transfers between devices: 2.06 us -> 0.09 us  [swap_z_low(): return lax.ppermute(value, 'dp', [(d, d ^ 4) for d in range(8)])]
    ppermute x1, waiting for transfers between devices: 2.04 us -> 4 us  [swap_z_low(): return lax.ppermute(value, 'dp', [(d, d ^ 4) for d in range(8)])]
    ppermute x10, starting transfers between devices: 21.1 us -> 20.3 us  [the longest x3 10.4 us: swap_z(): return lax.ppermute(value, 'space', [(s, s ^ slot << 1) for s in range(32)])]
    pallas_call x17 -> x13, Pallas kernels: 9.45 us -> 9.84 us  [call(): pl.pallas_call(kernel, out_shape=[jax.ShapeDtypeStruct(shape, dtype) for...]
  transfers between devices with their start and end apart: 16 -> 16, of which waited for: 12 -> 10; matrix products, arithmetic and copies ran while one was open for 0% -> 0% of each run, Pallas kernels for 10% -> 11%
where the time goes in v5:
time: 62.6 us; the launch traced here: 62.4 us
  starting transfers between devices  25.5 us (41%)
  waiting for transfers between devices  25.4 us (41%)
  Pallas kernels  9.84 us (16%)
  local copies, waits for them, and re-layouts  0.97 us (2%)
  between operations  0.73 us (1%)
    ppermute x3, starting transfers between devices, swap_z(): return lax.ppermute(value, 'space', [(s, s ^ slot << 1) for s in range(32)])  10.4 us
    pallas_call x13, Pallas kernels, call(): pl.pallas_call(kernel, out_shape=[jax.ShapeDtypeStruct(shape, dtype) for...  9.84 us
    ppermute x4, waiting for transfers between devices, swap_x(): lax.ppermute(value, 'space', [(s, s ^ partner(step, s & 1) << 3) for s in...  7.32 us
    ppermute x4, starting transfers between devices, swap_x(): lax.ppermute(value, 'space', [(s, s ^ partner(step, s & 1) << 3) for s in...  5.61 us
    ppermute x3, waiting for transfers between devices, swap_z(): return lax.ppermute(value, 'space', [(s, s ^ slot << 1) for s in range(32)])  4.91 us
    ppermute x3, waiting for transfers between devices, swap_y(): return lax.ppermute(value, 'dp', [(d, d ^ slot) for d in range(8)])  4.83 us
    ppermute x3, starting transfers between devices, swap_y(): return lax.ppermute(value, 'dp', [(d, d ^ slot) for d in range(8)])  4.35 us
    ppermute x1, waiting for transfers between devices, swap_z_low(): return lax.ppermute(value, 'dp', [(d, d ^ 4) for d in range(8)])  4 us
  transfers between devices with their start and end apart: 16, of which 10 were waited for; matrix products, arithmetic and copies ran while one was open for 0% of the time, Pallas kernels for 11%

profile of v5, /device:TPU:6, one launch (start us, length us, event | category | flops | bytes accessed | tf_op | source)
XLA Modules:
  0.0 62.4 jit_solution(134176533083013597)
XLA Ops:
  0.6 1.0 %slice_bitcast_fusion.rim_ref = bf16[32,4096]{1,0:T(8,128)(2,1)S(1)} fusion(bf16[1,4,32,4096]{3,2,1,0:T(8,128)(2,1)} %param.4), kind=kLoop, calls=%fused_computation | loop fusion | bytes 524288 | tf_op jit(solution)/shard_map/squeeze | solution.py:337
  1.6 0.1 collective-permute-start
  1.7 2.7 %shard_map.67 = (bf16[3,3,33,16,128]{4,3,2,1,0:T(8,128)(2,1)S(1)}, bf16[2304,128]{1,0:T(8,128)(2,1)S(1)}, bf16[9,128,128]{2,1,0:T(8,128)(2,1)S(1)}, bf16[512,128...) custom-call(bf16[4,32,4096]{2,1,0:T(8,128)(2,1)} %bitcast.12, ...), custom_call_target="tpu_custom_call" | custom-call | flops 1000000000 | bytes 2637824 | tf_op jit(solution)/shard_map/pallas_call | solution.py:308
  4.4 3.4 %collective-permute-start.1 = (f32[128,128]{1,0:T(8,128)S(1)}, f32[128,128]{1,0:T(8,128)S(1)}, u32[]{:S(2)}, u32[]{:S(2)}) collective-permute-start(f32[128,128]{1,0:T(8,128)S(1)} %get-tuple-element.40), channel_id=1, source_target_pairs={{0,1},{1,2},{2,3},{3,4},{4,5},{5,6},{6,7},{7,8},{8,9},{9,10},{10,1... | collective-permute-start | bytes 196616 | tf_op jit(solution)/shard_map/ppermute | solution.py:16
  7.9 2.1 %shard_map.68 = (bf16[3,33,16,128]{3,2,1,0:T(8,128)(2,1)S(1)}, bf16[18,128,128]{2,1,0:T(8,128)(2,1)S(1)}, f32[512,128]{1,0:T(8,128)S(1)}, f32[128,128]{1,0:T(8,128)S(1)}) custom-call(bf16[4,32,4096]{2,1,0:T(8,128)(2,1)} %bitcast.13, bf16[3,3,33,16,128]{4,3,2,1,0:T(8,128)(2,1)S(1)} %get-tuple-element.42.y_ref, bf16[2304,128]{1,0:T(8,128)(2,1)S(1)} %get-tuple-element.41.w_ref, ...), custom_call_target="tpu_custom_call" | custom-call | flops 1000000000 | bytes 4034560 | tf_op jit(solution)/shard_map/pallas_call | solution.py:308
  10.0 3.1 %collective-permute-done.1.got_ref = f32[128,128]{1,0:T(8,128)S(1)} collective-permute-done((f32[128,128]{1,0:T(8,128)S(1)}, f32[128,128]{1,0:T(8,128)S(1)}, u32[]{:S(2)}, u32[]{:S(2)}) %collective-permute-start.1) | collective-permute-done | bytes 65568 | tf_op jit(solution)/shard_map/ppermute | solution.py:16
  13.0 0.9 %shard_map.69 = (bf16[3,33,16,128]{3,2,1,0:T(8,128)(2,1)S(1)}, bf16[512,128]{1,0:T(8,128)(2,1)S(1)}, bf16[1152,128]{1,0:T(8,128)(2,1)S(1)}, f32[128,128]{1,0:T(8,128)S(1)}, bf16[128,128]{1,0:T(8,128)(2,1)S(1)}) custom-call(bf16[32,4096]{1,0:T(8,128)(2,1)S(1)} %collective-permute-done.rim_ref, f32[128,128]{1,0:T(8,128)S(1)} %collective-permute-done.1.got_ref, ...), custom_call_target="tpu_custom_call" | custom-call | flops 400000000 | bytes 1867776 | tf_op jit(solution)/shard_map/pallas_call | solution.py:308
  14.0 0.1 collective-permute-start.2
  14.1 1.8 %shard_map.70 = (f32[18,64,128]{2,1,0:T(8,128)S(1)}, bf16[18,64,128]{2,1,0:T(8,128)(2,1)S(1)}, bf16[8,16,128]{2,1,0:T(8,128)(2,1)}, f32[9,128,256]{2,1,0:T(8,128)S(1)}) custom-call(bf16[1152,128]{1,0:T(8,128)(2,1)S(1)} %get-tuple-element.47.low_ref, bf16[1152,128]{1,0:T(8,128)(2,1)S(1)} %get-tuple-element.43.taps_ref.up_ref, ...), custom_call_target="tpu_custom_call" | custom-call | flops 800000000 | bytes 3436544 | tf_op jit(solution)/shard_map/pallas_call | solution.py:308
  15.9 1.2 %shard_map.71 = (f32[23,64,128]{2,1,0:T(8,128)S(1)}, bf16[23,64,128]{2,1,0:T(8,128)(2,1)S(1)}) custom-call(bf16[128,128]{1,0:T(8,128)(2,1)S(1)} %get-tuple-element.48.gp_ref, bf16[128,128]{1,0:T(8,128)(2,1)S(1)} %collective-permute-done.2.gpn_ref, bf16[9,128,128]{2,1,0:T(8,128)(2,1)S(1)} %get-tuple-element.56.fa_ref, ...), custom_call_target="tpu_custom_call" | custom-call | flops 800000000 | bytes 3772416 | tf_op jit(solution)/shard_map/pallas_call | solution.py:308
  17.1 1.4 %collective-permute-start.6 = (bf16[23,64,128]{2,1,0:T(8,128)(2,1)S(1)}, bf16[23,64,128]{2,1,0:T(8,128)(2,1)S(1)}, u32[]{:S(2)}, u32[]{:S(2)}) collective-permute-start(bf16[23,64,128]{2,1,0:T(8,128)(2,1)S(1)} %get-tuple-element.66), channel_id=1, source_target_pairs={{0,1},{1,0},{2,3},{3,2},{4,5},{5,4},{6,7},{7,6},{8,9},{9,8},{10,11... | collective-permute-start | bytes 1130504 | tf_op jit(solution)/shard_map/ppermute | solution.py:20
  18.5 0.1 collective-permute-start.3
  18.6 1.2 %collective-permute-done.6.got_ref = bf16[23,64,128]{2,1,0:T(8,128)(2,1)S(1)} collective-permute-done((bf16[23,64,128]{2,1,0:T(8,128)(2,1)S(1)}, bf16[23,64,128]{2,1,0:T(8,128)(2,1)S(1)}, u32[]{:S(2)}, u32[]{:S(2)}) %collective-permute-start.6) | collective-permute-done | bytes 376864 | tf_op jit(solution)/shard_map/ppermute | solution.py:20
  19.9 0.9 %collective-permute-start.7 = (bf16[23,32,128]{2,1,0:T(8,128)(2,1)S(1)}, bf16[23,32,128]{2,1,0:T(8,128)(2,1)S(1)}, u32[]{:S(2)}, u32[]{:S(2)}) collective-permute-start(bf16[23,32,128]{2,1,0:T(8,128)(2,1)S(1)} %get-tuple-element.68), channel_id=1, source_target_pairs={{0,8},{1,25},{2,10},{3,27},{4,12},{5,29},{6,14},{7,31},{8,0},{9,17... | collective-permute-start | bytes 565256 | tf_op jit(solution)/shard_map/ppermute | solution.py:28
  20.9 1.3 %collective-permute-start.4 = (bf16[18,32,128]{2,1,0:T(8,128)(2,1)S(1)}, bf16[18,32,128]{2,1,0:T(8,128)(2,1)S(1)}, u32[]{:S(2)}, u32[]{:S(2)}) collective-permute-start(bf16[18,32,128]{2,1,0:T(8,128)(2,1)S(1)} %get-tuple-element.62), channel_id=1, source_target_pairs={{0,8},{1,25},{2,10},{3,27},{4,12},{5,29},{6,14},{7,31},{8,0},{9,17... | collective-permute-start | bytes 442376 | tf_op jit(solution)/shard_map/ppermute | solution.py:28
  22.2 3.4 %collective-permute-done.7.got_ref = bf16[23,32,128]{2,1,0:T(8,128)(2,1)S(1)} collective-permute-done((bf16[23,32,128]{2,1,0:T(8,128)(2,1)S(1)}, bf16[23,32,128]{2,1,0:T(8,128)(2,1)S(1)}, u32[]{:S(2)}, u32[]{:S(2)}) %collective-permute-start.7) | collective-permute-done | bytes 188448 | tf_op jit(solution)/shard_map/ppermute | solution.py:28
  25.6 1.7 %collective-permute-start.8 = (bf16[23,16,128]{2,1,0:T(8,128)(2,1)S(1)}, bf16[23,16,128]{2,1,0:T(8,128)(2,1)S(1)}, u32[]{:S(2)}, u32[]{:S(2)}) collective-permute-start(bf16[23,16,128]{2,1,0:T(8,128)(2,1)S(1)} %get-tuple-element.70), channel_id=1, source_target_pairs={{0,24},{1,9},{2,26},{3,11},{4,28},{5,13},{6,30},{7,15},{8,16},{9,1... | collective-permute-start | bytes 282632 | tf_op jit(solution)/shard_map/ppermute | solution.py:28
  27.4 1.7 %collective-permute-start.5 = (bf16[18,16,128]{2,1,0:T(8,128)(2,1)S(1)}, bf16[18,16,128]{2,1,0:T(8,128)(2,1)S(1)}, u32[]{:S(2)}, u32[]{:S(2)}) collective-permute-start(bf16[18,16,128]{2,1,0:T(8,128)(2,1)S(1)} %get-tuple-element.64), channel_id=1, source_target_pairs={{0,24},{1,9},{2,26},{3,11},{4,28},{5,13},{6,30},{7,15},{8,16},{9,1... | collective-permute-start | bytes 221192 | tf_op jit(solution)/shard_map/ppermute | solution.py:28
  29.1 3.9 %collective-permute-done.5.got_ref = bf16[18,16,128]{2,1,0:T(8,128)(2,1)S(1)} collective-permute-done((bf16[18,16,128]{2,1,0:T(8,128)(2,1)S(1)}, bf16[18,16,128]{2,1,0:T(8,128)(2,1)S(1)}, u32[]{:S(2)}, u32[]{:S(2)}) %collective-permute-start.5) | collective-permute-done | bytes 73760 | tf_op jit(solution)/shard_map/ppermute | solution.py:28
  33.1 7.2 %collective-permute-start.10 = (bf16[41,4,128]{2,1,0:T(4,128)(2,1)S(1)}, bf16[41,4,128]{2,1,0:T(4,128)(2,1)S(1)}, u32[]{:S(2)}, u32[]{:S(2)}) collective-permute-start(bf16[41,4,128]{2,1,0:T(4,128)(2,1)S(1)} %get-tuple-element.73), channel_id=1, source_target_pairs={{0,4},{1,5},{2,6},{3,7},{4,0},{5,1},{6,2},{7,3},{8,12},{9,13},{10,... | collective-permute-start | bytes 125960 | tf_op jit(solution)/shard_map/ppermute | solution.py:32
  40.3 3.2 %collective-permute-start.11 = (bf16[41,4,128]{2,1,0:T(4,128)(2,1)S(1)}, bf16[41,4,128]{2,1,0:T(4,128)(2,1)S(1)}, u32[]{:S(2)}, u32[]{:S(2)}) collective-permute-start(bf16[41,4,128]{2,1,0:T(4,128)(2,1)S(1)} %get-tuple-element.74), channel_id=1, source_target_pairs={{0,6},{1,7},{2,4},{3,5},{4,2},{5,3},{6,0},{7,1},{8,14},{9,15},{10,... | collective-permute-start | bytes 125960 | tf_op jit(solution)/shard_map/ppermute | solution.py:32
  43.4 2.9 %collective-permute-done.11.refs_2_ = bf16[41,4,128]{2,1,0:T(4,128)(2,1)S(1)} collective-permute-done((bf16[41,4,128]{2,1,0:T(4,128)(2,1)S(1)}, bf16[41,4,128]{2,1,0:T(4,128)(2,1)S(1)}, u32[]{:S(2)}, u32[]{:S(2)}) %collective-permute-start.11) | collective-permute-done | bytes 42016 | tf_op jit(solution)/shard_map/ppermute | solution.py:32
  46.4 2.0 %collective-permute-done.9.refs_0_ = bf16[41,4,128]{2,1,0:T(4,128)(2,1)S(1)} collective-permute-done((bf16[41,4,128]{2,1,0:T(4,128)(2,1)S(1)}, bf16[41,4,128]{2,1,0:T(4,128)(2,1)S(1)}, u32[]{:S(2)}, u32[]{:S(2)}) %collective-permute-start.9) | collective-permute-done | bytes 42016 | tf_op jit(solution)/shard_map/ppermute | solution.py:32
  48.4 3.3 %collective-permute-start.12 = (bf16[41,4,128]{2,1,0:T(4,128)(2,1)S(1)}, bf16[41,4,128]{2,1,0:T(4,128)(2,1)S(1)}, u32[]{:S(2)}, u32[]{:S(2)}) collective-permute-start(bf16[41,4,128]{2,1,0:T(4,128)(2,1)S(1)} %shard_map.77.own_ref), channel_id=1, source_target_pairs={{0,64},{32,96},{64,0},{96,32},{128,192},{160,224},{192,128},{224,1... | collective-permute-start | bytes 125960 | tf_op jit(solution)/shard_map/ppermute | solution.py:36
  51.7 0.7 %collective-permute-start.13 = (bf16[41,4,128]{2,1,0:T(4,128)(2,1)S(1)}, bf16[41,4,128]{2,1,0:T(4,128)(2,1)S(1)}, u32[]{:S(2)}, u32[]{:S(2)}) collective-permute-start(bf16[41,4,128]{2,1,0:T(4,128)(2,1)S(1)} %shard_map.77.own_ref), channel_id=1, source_target_pairs={{0,32},{32,0},{64,96},{96,64},{128,160},{160,128},{192,224},{224,1... | collective-permute-start | bytes 125960 | tf_op jit(solution)/shard_map/ppermute | solution.py:36
  52.4 0.4 collective-permute-start.14
  52.8 1.2 %collective-permute-done.12.refs_0_ = bf16[41,4,128]{2,1,0:T(4,128)(2,1)S(1)} collective-permute-done((bf16[41,4,128]{2,1,0:T(4,128)(2,1)S(1)}, bf16[41,4,128]{2,1,0:T(4,128)(2,1)S(1)}, u32[]{:S(2)}, u32[]{:S(2)}) %collective-permute-start.12) | collective-permute-done | bytes 42016 | tf_op jit(solution)/shard_map/ppermute | solution.py:36
  54.0 1.7 %collective-permute-done.13.refs_1_ = bf16[41,4,128]{2,1,0:T(4,128)(2,1)S(1)} collective-permute-done((bf16[41,4,128]{2,1,0:T(4,128)(2,1)S(1)}, bf16[41,4,128]{2,1,0:T(4,128)(2,1)S(1)}, u32[]{:S(2)}, u32[]{:S(2)}) %collective-permute-start.13) | collective-permute-done | bytes 42016 | tf_op jit(solution)/shard_map/ppermute | solution.py:36
  55.7 1.9 %collective-permute-done.14.refs_2_ = bf16[41,4,128]{2,1,0:T(4,128)(2,1)S(1)} collective-permute-done((bf16[41,4,128]{2,1,0:T(4,128)(2,1)S(1)}, bf16[41,4,128]{2,1,0:T(4,128)(2,1)S(1)}, u32[]{:S(2)}, u32[]{:S(2)}) %collective-permute-start.14) | collective-permute-done | bytes 42016 | tf_op jit(solution)/shard_map/ppermute | solution.py:36
  57.6 0.1 collective-permute-start.15
  57.7 4.0 %collective-permute-done.15.got_ref = bf16[41,4,128]{2,1,0:T(4,128)(2,1)S(1)} collective-permute-done((bf16[41,4,128]{2,1,0:T(4,128)(2,1)S(1)}, bf16[41,4,128]{2,1,0:T(4,128)(2,1)S(1)}, u32[]{:S(2)}, u32[]{:S(2)}) %collective-permute-start.15) | collective-permute-done | bytes 42016 | tf_op jit(solution)/shard_map/ppermute | solution.py:40
  61.7 0.7 %shard_map.79 = (f32[27,4,64]{2,1,0:T(4,128)}, f32[27,4,128]{2,1,0:T(4,128)}) custom-call(bf16[41,4,128]{2,1,0:T(4,128)(2,1)S(1)} %shard_map.78.own_ref, bf16[41,4,128]{2,1,0:T(4,128)(2,1)S(1)} %collective-permute-done.15.got_ref), custom_call_target="tpu_custom_call" | custom-call | flops 1000000 | bytes 83968 | tf_op jit(solution)/shard_map/pallas_call | solution.py:308
  (16 shorter events, 0.4 us)
Async XLA Ops:
  1.6 11.4 %collective-permute-start = (bf16[32,4096]{1,0:T(8,128)(2,1)S(1)}, bf16[32,4096]{1,0:T(8,128)(2,1)S(1)}, u32[]{:S(2)}, u32[]{:S(2)}) collective-permute-start(bf16[32,4096]{1,0:T(8,128)(2,1)S(1)} %slice_bitcast_fusion.rim_ref), channel_id=1, source_target_pairs={{0,1},{1,2},{2,3},{3,4},{4,5},{5,6},{6,7},{7,8},{8,9},{9,10},{10,1... | collective-permute-start | bytes 786440 | tf_op jit(solution)/shard_map/ppermute | solution.py:16
  4.4 8.6 %collective-permute-start.1 = (f32[128,128]{1,0:T(8,128)S(1)}, f32[128,128]{1,0:T(8,128)S(1)}, u32[]{:S(2)}, u32[]{:S(2)}) collective-permute-start(f32[128,128]{1,0:T(8,128)S(1)} %get-tuple-element.40), channel_id=1, source_target_pairs={{0,1},{1,2},{2,3},{3,4},{4,5},{5,6},{6,7},{7,8},{8,9},{9,10},{10,1... | collective-permute-start | bytes 196616 | tf_op jit(solution)/shard_map/ppermute | solution.py:16
  7.9 5.2 %copy-start = (bf16[1,1,8,16,128]{4,3,2,1,0:T(8,128)(2,1)S(1)}, bf16[1,1,8,16,128]{4,3,2,1,0:T(8,128)(2,1)}, u32[]{:S(2)}) copy-start(bf16[1,1,8,16,128]{4,3,2,1,0:T(8,128)(2,1)} %param.7) | copy-start | bytes 98308
  14.0 1.9 %collective-permute-start.2 = (bf16[128,128]{1,0:T(8,128)(2,1)S(1)}, bf16[128,128]{1,0:T(8,128)(2,1)S(1)}, u32[]{:S(2)}, u32[]{:S(2)}) collective-permute-start(bf16[128,128]{1,0:T(8,128)(2,1)S(1)} %get-tuple-element.48.gp_ref), channel_id=1, source_target_pairs={{0,31},{1,0},{2,1},{3,2},{4,3},{5,4},{6,5},{7,6},{8,7},{9,8},{10,9... | collective-permute-start | bytes 98312 | tf_op jit(solution)/shard_map/ppermute | solution.py:16
  17.1 2.7 %collective-permute-start.6 = (bf16[23,64,128]{2,1,0:T(8,128)(2,1)S(1)}, bf16[23,64,128]{2,1,0:T(8,128)(2,1)S(1)}, u32[]{:S(2)}, u32[]{:S(2)}) collective-permute-start(bf16[23,64,128]{2,1,0:T(8,128)(2,1)S(1)} %get-tuple-element.66), channel_id=1, source_target_pairs={{0,1},{1,0},{2,3},{3,2},{4,5},{5,4},{6,7},{7,6},{8,9},{9,8},{10,11... | collective-permute-start | bytes 1130504 | tf_op jit(solution)/shard_map/ppermute | solution.py:20
  18.5 2.3 %collective-permute-start.3 = (bf16[18,64,128]{2,1,0:T(8,128)(2,1)S(1)}, bf16[18,64,128]{2,1,0:T(8,128)(2,1)S(1)}, u32[]{:S(2)}, u32[]{:S(2)}) collective-permute-start(bf16[18,64,128]{2,1,0:T(8,128)(2,1)S(1)} %get-tuple-element.60), channel_id=1, source_target_pairs={{0,1},{1,0},{2,3},{3,2},{4,5},{5,4},{6,7},{7,6},{8,9},{9,8},{10,11... | collective-permute-start | bytes 884744 | tf_op jit(solution)/shard_map/ppermute | solution.py:20
  19.9 5.7 %collective-permute-start.7 = (bf16[23,32,128]{2,1,0:T(8,128)(2,1)S(1)}, bf16[23,32,128]{2,1,0:T(8,128)(2,1)S(1)}, u32[]{:S(2)}, u32[]{:S(2)}) collective-permute-start(bf16[23,32,128]{2,1,0:T(8,128)(2,1)S(1)} %get-tuple-element.68), channel_id=1, source_target_pairs={{0,8},{1,25},{2,10},{3,27},{4,12},{5,29},{6,14},{7,31},{8,0},{9,17... | collective-permute-start | bytes 565256 | tf_op jit(solution)/shard_map/ppermute | solution.py:28
  20.9 6.4 %collective-permute-start.4 = (bf16[18,32,128]{2,1,0:T(8,128)(2,1)S(1)}, bf16[18,32,128]{2,1,0:T(8,128)(2,1)S(1)}, u32[]{:S(2)}, u32[]{:S(2)}) collective-permute-start(bf16[18,32,128]{2,1,0:T(8,128)(2,1)S(1)} %get-tuple-element.62), channel_id=1, source_target_pairs={{0,8},{1,25},{2,10},{3,27},{4,12},{5,29},{6,14},{7,31},{8,0},{9,17... | collective-permute-start | bytes 442376 | tf_op jit(solution)/shard_map/ppermute | solution.py:28
  25.6 7.4 %collective-permute-start.8 = (bf16[23,16,128]{2,1,0:T(8,128)(2,1)S(1)}, bf16[23,16,128]{2,1,0:T(8,128)(2,1)S(1)}, u32[]{:S(2)}, u32[]{:S(2)}) collective-permute-start(bf16[23,16,128]{2,1,0:T(8,128)(2,1)S(1)} %get-tuple-element.70), channel_id=1, source_target_pairs={{0,24},{1,9},{2,26},{3,11},{4,28},{5,13},{6,30},{7,15},{8,16},{9,1... | collective-permute-start | bytes 282632 | tf_op jit(solution)/shard_map/ppermute | solution.py:28
  27.4 5.7 %collective-permute-start.5 = (bf16[18,16,128]{2,1,0:T(8,128)(2,1)S(1)}, bf16[18,16,128]{2,1,0:T(8,128)(2,1)S(1)}, u32[]{:S(2)}, u32[]{:S(2)}) collective-permute-start(bf16[18,16,128]{2,1,0:T(8,128)(2,1)S(1)} %get-tuple-element.64), channel_id=1, source_target_pairs={{0,24},{1,9},{2,26},{3,11},{4,28},{5,13},{6,30},{7,15},{8,16},{9,1... | collective-permute-start | bytes 221192 | tf_op jit(solution)/shard_map/ppermute | solution.py:28
  33.1 10.4 %collective-permute-start.10 = (bf16[41,4,128]{2,1,0:T(4,128)(2,1)S(1)}, bf16[41,4,128]{2,1,0:T(4,128)(2,1)S(1)}, u32[]{:S(2)}, u32[]{:S(2)}) collective-permute-start(bf16[41,4,128]{2,1,0:T(4,128)(2,1)S(1)} %get-tuple-element.73), channel_id=1, source_target_pairs={{0,4},{1,5},{2,6},{3,7},{4,0},{5,1},{6,2},{7,3},{8,12},{9,13},{10,... | collective-permute-start | bytes 125960 | tf_op jit(solution)/shard_map/ppermute | solution.py:32
  40.3 6.1 %collective-permute-start.11 = (bf16[41,4,128]{2,1,0:T(4,128)(2,1)S(1)}, bf16[41,4,128]{2,1,0:T(4,128)(2,1)S(1)}, u32[]{:S(2)}, u32[]{:S(2)}) collective-permute-start(bf16[41,4,128]{2,1,0:T(4,128)(2,1)S(1)} %get-tuple-element.74), channel_id=1, source_target_pairs={{0,6},{1,7},{2,4},{3,5},{4,2},{5,3},{6,0},{7,1},{8,14},{9,15},{10,... | collective-permute-start | bytes 125960 | tf_op jit(solution)/shard_map/ppermute | solution.py:32
  43.4 4.9 %collective-permute-start.9 = (bf16[41,4,128]{2,1,0:T(4,128)(2,1)S(1)}, bf16[41,4,128]{2,1,0:T(4,128)(2,1)S(1)}, u32[]{:S(2)}, u32[]{:S(2)}) collective-permute-start(bf16[41,4,128]{2,1,0:T(4,128)(2,1)S(1)} %get-tuple-element.72), channel_id=1, source_target_pairs={{0,2},{1,3},{2,0},{3,1},{4,6},{5,7},{6,4},{7,5},{8,10},{9,11},{10,... | collective-permute-start | bytes 125960 | tf_op jit(solution)/shard_map/ppermute | solution.py:32
  48.4 5.6 %collective-permute-start.12 = (bf16[41,4,128]{2,1,0:T(4,128)(2,1)S(1)}, bf16[41,4,128]{2,1,0:T(4,128)(2,1)S(1)}, u32[]{:S(2)}, u32[]{:S(2)}) collective-permute-start(bf16[41,4,128]{2,1,0:T(4,128)(2,1)S(1)} %shard_map.77.own_ref), channel_id=1, source_target_pairs={{0,64},{32,96},{64,0},{96,32},{128,192},{160,224},{192,128},{224,1... | collective-permute-start | bytes 125960 | tf_op jit(solution)/shard_map/ppermute | solution.py:36
  51.7 4.0 %collective-permute-start.13 = (bf16[41,4,128]{2,1,0:T(4,128)(2,1)S(1)}, bf16[41,4,128]{2,1,0:T(4,128)(2,1)S(1)}, u32[]{:S(2)}, u32[]{:S(2)}) collective-permute-start(bf16[41,4,128]{2,1,0:T(4,128)(2,1)S(1)} %shard_map.77.own_ref), channel_id=1, source_target_pairs={{0,32},{32,0},{64,96},{96,64},{128,160},{160,128},{192,224},{224,1... | collective-permute-start | bytes 125960 | tf_op jit(solution)/shard_map/ppermute | solution.py:36
  52.4 5.2 %collective-permute-start.14 = (bf16[41,4,128]{2,1,0:T(4,128)(2,1)S(1)}, bf16[41,4,128]{2,1,0:T(4,128)(2,1)S(1)}, u32[]{:S(2)}, u32[]{:S(2)}) collective-permute-start(bf16[41,4,128]{2,1,0:T(4,128)(2,1)S(1)} %shard_map.77.own_ref), channel_id=1, source_target_pairs={{0,96},{32,64},{64,32},{96,0},{128,224},{160,192},{192,160},{224,1... | collective-permute-start | bytes 125960 | tf_op jit(solution)/shard_map/ppermute | solution.py:36
  57.6 4.1 %collective-permute-start.15 = (bf16[41,4,128]{2,1,0:T(4,128)(2,1)S(1)}, bf16[41,4,128]{2,1,0:T(4,128)(2,1)S(1)}, u32[]{:S(2)}, u32[]{:S(2)}) collective-permute-start(bf16[41,4,128]{2,1,0:T(4,128)(2,1)S(1)} %shard_map.78.own_ref), channel_id=1, source_target_pairs={{0,128},{32,160},{64,192},{96,224},{128,0},{160,32},{192,64},{224,... | collective-permute-start | bytes 125960 | tf_op jit(solution)/shard_map/ppermute | solution.py:40

commit v6 on v5

--- a/solution.py
+++ b/solution.py
@@ -178,8 +178,7 @@
     out_ref[...] = leaky(pre)
 
 
-def second_grad(order, taps_ref, gp):
-    turned = dot_nt(order, taps_ref[...]).astype(BF16)
+def second_grad(turned, gp):
     lhs = [turned[:, tap * 128 : tap * 128 + 128] for tap in range(9)]
     return dot(jnp.concatenate(lhs, axis=0), gp).reshape(9, 128, 128)
 
@@ -189,7 +188,7 @@
     gs[at, 0:16, 0:8, :] = grad.reshape(16, 8, 128)
 
 
-def hidden_grad(gs, gu, sources, hid_ref, order):
+def class_sums(gs, sources):
     moved = {
         (s, dr, dq): gs[s, dr : dr + 16, dq : dq + 8, :].reshape(128, 128).astype(BF16)
         for s, _ in sources
@@ -197,6 +196,7 @@
         for dq in range(2)
     }
     one_d = {0: [(0, 1)], 1: [(0, 2), (1, 0)]}
+    sums = []
     for pv in range(2):
         for pw in range(2):
             lhs, rhs = [], []
@@ -205,9 +205,14 @@
                     for dr, c in one_d[pw]:
                         lhs.append(moved[s, dr, dq])
                         rhs.append(f_ref[3 * b + c])
-            grad = dot_nt(jnp.concatenate(lhs, axis=1), jnp.concatenate(rhs, axis=1))
-            grad = grad.astype(BF16).astype(F32).reshape(16, 8, 128)
-            gu[:, pw, pl.ds(pv, 8, stride=2), :] = grad
+            sums.append(dot_nt(jnp.concatenate(lhs, axis=1), jnp.concatenate(rhs, axis=1)))
+    return sums
+
+
+def hidden_grad(gu, sums, hid_ref, order):
+    for n, grad in enumerate(sums):
+        grad = grad.astype(BF16).astype(F32).reshape(16, 8, 128)
+        gu[:, n % 2, pl.ds(n // 2, 8, stride=2), :] = grad
     hid = hid_ref[...].astype(F32)
     grad = (gu[...].reshape(512, 128) * jnp.where(hid > 0, 1.0, SLOPE)).astype(BF16)
     return dot_nt(order, grad).astype(BF16)
@@ -215,34 +220,37 @@
 
 def second_grad_kernel(
     low_ref, up_ref, gp_ref, pre_ref, fb_ref, hid_ref, yr_ref, y0_ref, y_ref,
-    keep_ref, send_ref, out_ref, part_ref,
+    keep_ref, send_ref, out_ref, part_ref, turned_ref, lead_ref,
     os, gs, gu,
 ):
     order = channel_order()
     for n, taps_ref in enumerate((low_ref, up_ref)):
-        grad = second_grad(order, taps_ref, gp_ref[...])
+        turned = dot_nt(order, taps_ref[...]).astype(BF16)
+        grad = second_grad(turned, gp_ref[...])
         keep_ref[9 * n : 9 * n + 9] = grad[:, :64]
         send_ref[9 * n : 9 * n + 9] = grad[:, 64:].astype(BF16)
+    turned_ref[...] = turned
     for r in range(16):
         os[pl.ds(r, 8, stride=16), :] = pre_ref[8 * r : 8 * r + 8]
     out_ref[...] = os[...].astype(BF16).reshape(8, 16, 128)
     lay_out(gs, 0, gp_ref[...].astype(F32))
-    turned = hidden_grad(gs, gu, [(0, fb_ref.at[0:9])], hid_ref, order)
+    turned = hidden_grad(gu, class_sums(gs, [(0, fb_ref.at[0:9])]), hid_ref, order)
+    for n, grad in enumerate(class_sums(gs, [(0, fb_ref.at[9:18])])):
+        lead_ref[n] = grad
     for a, plane in enumerate((yr_ref, y0_ref, y_ref.at[0])):
         for b in range(3):
             part_ref[3 * a + b] = dot(turned, columns(plane, b))
 
 
 def first_grad_kernel(
-    gp_ref, gpn_ref, fa_ref, fb_ref, hid_ref, y_ref, taps_ref, part_ref,
+    gpn_ref, fa_ref, hid_ref, y_ref, turned_ref, part_ref, lead_ref,
     keep_ref, send_ref,
     gs, gu,
 ):
     above = gpn_ref[...].astype(F32) * jnp.where(lax.axis_index("space") < 31, 1.0, 0.0)
-    lay_out(gs, 0, gp_ref[...].astype(F32))
-    lay_out(gs, 1, above)
-    order = channel_order()
-    turned = hidden_grad(gs, gu, [(0, fb_ref.at[9:18]), (1, fa_ref)], hid_ref, order)
+    lay_out(gs, 0, above)
+    sums = [lead_ref[n] + grad for n, grad in enumerate(class_sums(gs, [(0, fa_ref)]))]
+    turned = hidden_grad(gu, sums, hid_ref, channel_order())
     low = lax.broadcasted_iota(jnp.int32, (128, 128), 1) < 64
 
     def put(block, grad):
@@ -260,7 +268,7 @@
             if ab % 2 == 1 or ab == 8:
                 upper = grad[:, :128] if ab % 2 else jnp.zeros_like(held)
                 put(9 + ab // 2, jnp.where(low, held, upper))
-    grad = second_grad(order, taps_ref, above.astype(BF16))
+    grad = second_grad(turned_ref[...], above.astype(BF16))
     keep_ref[FIRST:] = grad[:, :64]
     send_ref[FIRST:] = grad[:, 64:].astype(BF16)
 
@@ -363,13 +371,13 @@
         scratch=[hs, tile], flops=4 * 10**8,
     )
     grad_two_next = around_space(grad_two, -1)
-    rows = ((2, 17, 16, 128), F32)
+    rows = ((1, 17, 16, 128), F32)
     plane = ((16, 2, 16, 128), F32)
-    keep_a, send_a, second_out, part = call(
+    keep_a, send_a, second_out, part, turned, lead = call(
         second_grad_kernel,
         [
             ((18, 64, 128), F32), ((18, 64, 128), BF16), ((8, 16, 128), BF16),
-            ((9, 128, 256), F32),
+            ((9, 128, 256), F32), ((128, 1152), BF16), ((4, 128, 128), F32),
         ],
         taps_low, taps_up, grad_two, out, second_b, hidden_low, y_rim, y_low, y,
         scratch=[tile, rows, plane], flops=8 * 10**8,
@@ -377,7 +385,7 @@
     keep_b, send_b = call(
         first_grad_kernel,
         [((23, 64, 128), F32), ((23, 64, 128), BF16)],
-        grad_two, grad_two_next, second_a, second_b, hidden_up, y, taps_up, part,
+        grad_two_next, second_a, hidden_up, y, turned, part, lead,
         scratch=[rows, plane], flops=8 * 10**8,
     )
     send_a, send_b = lax.optimization_barrier((send_a, send_b))

time: 62.6 us -> 62.3 us (level)
  no operation moved by 1% of the time
where the time goes in v6:
time: 62.3 us; the launch traced here: 62.2 us
  starting transfers between devices  25.5 us (41%)
  waiting for transfers between devices  25.4 us (41%)
  Pallas kernels  9.56 us (15%)
  local copies, waits for them, and re-layouts  0.97 us (2%)
  between operations  0.73 us (1%)
    ppermute x3, starting transfers between devices, swap_z(): return lax.ppermute(value, 'space', [(s, s ^ slot << 1) for s in range(32)])  10.4 us
    pallas_call x13, Pallas kernels, call(): pl.pallas_call(kernel, out_shape=[jax.ShapeDtypeStruct(shape, dtype) for...  9.56 us
    ppermute x4, waiting for transfers between devices, swap_x(): lax.ppermute(value, 'space', [(s, s ^ partner(step, s & 1) << 3) for s in...  7.32 us
    ppermute x4, starting transfers between devices, swap_x(): lax.ppermute(value, 'space', [(s, s ^ partner(step, s & 1) << 3) for s in...  5.61 us
    ppermute x3, waiting for transfers between devices, swap_z(): return lax.ppermute(value, 'space', [(s, s ^ slot << 1) for s in range(32)])  4.91 us
    ppermute x3, waiting for transfers between devices, swap_y(): return lax.ppermute(value, 'dp', [(d, d ^ slot) for d in range(8)])  4.85 us
    ppermute x3, starting transfers between devices, swap_y(): return lax.ppermute(value, 'dp', [(d, d ^ slot) for d in range(8)])  4.34 us
    ppermute x1, waiting for transfers between devices, swap_z_low(): return lax.ppermute(value, 'dp', [(d, d ^ 4) for d in range(8)])  4 us
  transfers between devices with their start and end apart: 16, of which 10 were waited for; matrix products, arithmetic and copies ran while one was open for 0% of the time, Pallas kernels for 11%

profile of v6, /device:TPU:6, one launch (start us, length us, event | category | flops | bytes accessed | tf_op | source)
XLA Modules:
  0.0 62.2 jit_solution(3891590010166250220)
XLA Ops:
  0.6 1.0 %slice_bitcast_fusion.rim_ref = bf16[32,4096]{1,0:T(8,128)(2,1)S(1)} fusion(bf16[1,4,32,4096]{3,2,1,0:T(8,128)(2,1)} %param.4), kind=kLoop, calls=%fused_computation | loop fusion | bytes 524288 | tf_op jit(solution)/shard_map/squeeze | solution.py:345
  1.6 0.1 collective-permute-start
  1.7 2.7 %shard_map.67 = (bf16[3,3,33,16,128]{4,3,2,1,0:T(8,128)(2,1)S(1)}, bf16[2304,128]{1,0:T(8,128)(2,1)S(1)}, bf16[9,128,128]{2,1,0:T(8,128)(2,1)S(1)}, bf16[512,128...) custom-call(bf16[4,32,4096]{2,1,0:T(8,128)(2,1)} %bitcast.12, ...), custom_call_target="tpu_custom_call" | custom-call | flops 1000000000 | bytes 2637824 | tf_op jit(solution)/shard_map/pallas_call | solution.py:316
  4.4 3.4 %collective-permute-start.1 = (f32[128,128]{1,0:T(8,128)S(1)}, f32[128,128]{1,0:T(8,128)S(1)}, u32[]{:S(2)}, u32[]{:S(2)}) collective-permute-start(f32[128,128]{1,0:T(8,128)S(1)} %get-tuple-element.42), channel_id=1, source_target_pairs={{0,1},{1,2},{2,3},{3,4},{4,5},{5,6},{6,7},{7,8},{8,9},{9,10},{10,1... | collective-permute-start | bytes 196616 | tf_op jit(solution)/shard_map/ppermute | solution.py:16
  7.9 2.1 %shard_map.68 = (bf16[3,33,16,128]{3,2,1,0:T(8,128)(2,1)S(1)}, bf16[18,128,128]{2,1,0:T(8,128)(2,1)S(1)}, f32[512,128]{1,0:T(8,128)S(1)}, f32[128,128]{1,0:T(8,128)S(1)}) custom-call(bf16[4,32,4096]{2,1,0:T(8,128)(2,1)} %bitcast.13, bf16[3,3,33,16,128]{4,3,2,1,0:T(8,128)(2,1)S(1)} %get-tuple-element.44.y_ref, bf16[2304,128]{1,0:T(8,128)(2,1)S(1)} %get-tuple-element.43.w_ref, ...), custom_call_target="tpu_custom_call" | custom-call | flops 1000000000 | bytes 4034560 | tf_op jit(solution)/shard_map/pallas_call | solution.py:316
  10.0 3.1 %collective-permute-done.1.got_ref = f32[128,128]{1,0:T(8,128)S(1)} collective-permute-done((f32[128,128]{1,0:T(8,128)S(1)}, f32[128,128]{1,0:T(8,128)S(1)}, u32[]{:S(2)}, u32[]{:S(2)}) %collective-permute-start.1) | collective-permute-done | bytes 65568 | tf_op jit(solution)/shard_map/ppermute | solution.py:16
  13.0 0.9 %shard_map.69 = (bf16[3,33,16,128]{3,2,1,0:T(8,128)(2,1)S(1)}, bf16[512,128]{1,0:T(8,128)(2,1)S(1)}, bf16[1152,128]{1,0:T(8,128)(2,1)S(1)}, f32[128,128]{1,0:T(8,128)S(1)}, bf16[128,128]{1,0:T(8,128)(2,1)S(1)}) custom-call(bf16[32,4096]{1,0:T(8,128)(2,1)S(1)} %collective-permute-done.rim_ref, f32[128,128]{1,0:T(8,128)S(1)} %collective-permute-done.1.got_ref, ...), custom_call_target="tpu_custom_call" | custom-call | flops 400000000 | bytes 1867776 | tf_op jit(solution)/shard_map/pallas_call | solution.py:316
  14.0 0.1 collective-permute-start.2
  14.1 1.8 %shard_map.70 = (f32[18,64,128]{2,1,0:T(8,128)S(1)}, bf16[18,64,128]{2,1,0:T(8,128)(2,1)S(1)}, bf16[8,16,128]{2,1,0:T(8,128)(2,1)}, f32[9,128,256]{2,1,0:T(8,128...) custom-call(bf16[1152,128]{1,0:T(8,128)(2,1)S(1)} %get-tuple-element.49.low_ref, ...), custom_call_target="tpu_custom_call" | custom-call | flops 800000000 | bytes 3436544 | tf_op jit(solution)/shard_map/pallas_call | solution.py:316
  15.9 1.0 %shard_map.71 = (f32[23,64,128]{2,1,0:T(8,128)S(1)}, bf16[23,64,128]{2,1,0:T(8,128)(2,1)S(1)}) custom-call(bf16[128,128]{1,0:T(8,128)(2,1)S(1)} %collective-permute-done.2.gpn_ref, bf16[9,128,128]{2,1,0:T(8,128)(2,1)S(1)} %get-tuple-element.58.fa_ref, bf16[512,128]{1,0:T(8,128)(2,1)S(1)} %get-tuple-element.59.hid_ref, ...), custom_call_target="tpu_custom_call" | custom-call | flops 800000000 | bytes 3411968 | tf_op jit(solution)/shard_map/pallas_call | solution.py:316
  16.9 1.4 %collective-permute-start.6 = (bf16[23,64,128]{2,1,0:T(8,128)(2,1)S(1)}, bf16[23,64,128]{2,1,0:T(8,128)(2,1)S(1)}, u32[]{:S(2)}, u32[]{:S(2)}) collective-permute-start(bf16[23,64,128]{2,1,0:T(8,128)(2,1)S(1)} %get-tuple-element.70), channel_id=1, source_target_pairs={{0,1},{1,0},{2,3},{3,2},{4,5},{5,4},{6,7},{7,6},{8,9},{9,8},{10,11... | collective-permute-start | bytes 1130504 | tf_op jit(solution)/shard_map/ppermute | solution.py:20
  18.3 0.1 collective-permute-start.3
  18.4 1.2 %collective-permute-done.6.got_ref = bf16[23,64,128]{2,1,0:T(8,128)(2,1)S(1)} collective-permute-done((bf16[23,64,128]{2,1,0:T(8,128)(2,1)S(1)}, bf16[23,64,128]{2,1,0:T(8,128)(2,1)S(1)}, u32[]{:S(2)}, u32[]{:S(2)}) %collective-permute-start.6) | collective-permute-done | bytes 376864 | tf_op jit(solution)/shard_map/ppermute | solution.py:20
  19.7 0.9 %collective-permute-start.7 = (bf16[23,32,128]{2,1,0:T(8,128)(2,1)S(1)}, bf16[23,32,128]{2,1,0:T(8,128)(2,1)S(1)}, u32[]{:S(2)}, u32[]{:S(2)}) collective-permute-start(bf16[23,32,128]{2,1,0:T(8,128)(2,1)S(1)} %get-tuple-element.72), channel_id=1, source_target_pairs={{0,8},{1,25},{2,10},{3,27},{4,12},{5,29},{6,14},{7,31},{8,0},{9,17... | collective-permute-start | bytes 565256 | tf_op jit(solution)/shard_map/ppermute | solution.py:28
  20.6 1.3 %collective-permute-start.4 = (bf16[18,32,128]{2,1,0:T(8,128)(2,1)S(1)}, bf16[18,32,128]{2,1,0:T(8,128)(2,1)S(1)}, u32[]{:S(2)}, u32[]{:S(2)}) collective-permute-start(bf16[18,32,128]{2,1,0:T(8,128)(2,1)S(1)} %get-tuple-element.66), channel_id=1, source_target_pairs={{0,8},{1,25},{2,10},{3,27},{4,12},{5,29},{6,14},{7,31},{8,0},{9,17... | collective-permute-start | bytes 442376 | tf_op jit(solution)/shard_map/ppermute | solution.py:28
  21.9 3.4 %collective-permute-done.7.got_ref = bf16[23,32,128]{2,1,0:T(8,128)(2,1)S(1)} collective-permute-done((bf16[23,32,128]{2,1,0:T(8,128)(2,1)S(1)}, bf16[23,32,128]{2,1,0:T(8,128)(2,1)S(1)}, u32[]{:S(2)}, u32[]{:S(2)}) %collective-permute-start.7) | collective-permute-done | bytes 188448 | tf_op jit(solution)/shard_map/ppermute | solution.py:28
  25.4 1.7 %collective-permute-start.8 = (bf16[23,16,128]{2,1,0:T(8,128)(2,1)S(1)}, bf16[23,16,128]{2,1,0:T(8,128)(2,1)S(1)}, u32[]{:S(2)}, u32[]{:S(2)}) collective-permute-start(bf16[23,16,128]{2,1,0:T(8,128)(2,1)S(1)} %get-tuple-element.74), channel_id=1, source_target_pairs={{0,24},{1,9},{2,26},{3,11},{4,28},{5,13},{6,30},{7,15},{8,16},{9,1... | collective-permute-start | bytes 282632 | tf_op jit(solution)/shard_map/ppermute | solution.py:28
  27.1 1.7 %collective-permute-start.5 = (bf16[18,16,128]{2,1,0:T(8,128)(2,1)S(1)}, bf16[18,16,128]{2,1,0:T(8,128)(2,1)S(1)}, u32[]{:S(2)}, u32[]{:S(2)}) collective-permute-start(bf16[18,16,128]{2,1,0:T(8,128)(2,1)S(1)} %get-tuple-element.68), channel_id=1, source_target_pairs={{0,24},{1,9},{2,26},{3,11},{4,28},{5,13},{6,30},{7,15},{8,16},{9,1... | collective-permute-start | bytes 221192 | tf_op jit(solution)/shard_map/ppermute | solution.py:28
  28.8 3.9 %collective-permute-done.5.got_ref = bf16[18,16,128]{2,1,0:T(8,128)(2,1)S(1)} collective-permute-done((bf16[18,16,128]{2,1,0:T(8,128)(2,1)S(1)}, bf16[18,16,128]{2,1,0:T(8,128)(2,1)S(1)}, u32[]{:S(2)}, u32[]{:S(2)}) %collective-permute-start.5) | collective-permute-done | bytes 73760 | tf_op jit(solution)/shard_map/ppermute | solution.py:28
  32.8 7.2 %collective-permute-start.10 = (bf16[41,4,128]{2,1,0:T(4,128)(2,1)S(1)}, bf16[41,4,128]{2,1,0:T(4,128)(2,1)S(1)}, u32[]{:S(2)}, u32[]{:S(2)}) collective-permute-start(bf16[41,4,128]{2,1,0:T(4,128)(2,1)S(1)} %get-tuple-element.77), channel_id=1, source_target_pairs={{0,4},{1,5},{2,6},{3,7},{4,0},{5,1},{6,2},{7,3},{8,12},{9,13},{10,... | collective-permute-start | bytes 125960 | tf_op jit(solution)/shard_map/ppermute | solution.py:32
  40.0 3.2 %collective-permute-start.11 = (bf16[41,4,128]{2,1,0:T(4,128)(2,1)S(1)}, bf16[41,4,128]{2,1,0:T(4,128)(2,1)S(1)}, u32[]{:S(2)}, u32[]{:S(2)}) collective-permute-start(bf16[41,4,128]{2,1,0:T(4,128)(2,1)S(1)} %get-tuple-element.78), channel_id=1, source_target_pairs={{0,6},{1,7},{2,4},{3,5},{4,2},{5,3},{6,0},{7,1},{8,14},{9,15},{10,... | collective-permute-start | bytes 125960 | tf_op jit(solution)/shard_map/ppermute | solution.py:32
  43.2 2.9 %collective-permute-done.11.refs_2_ = bf16[41,4,128]{2,1,0:T(4,128)(2,1)S(1)} collective-permute-done((bf16[41,4,128]{2,1,0:T(4,128)(2,1)S(1)}, bf16[41,4,128]{2,1,0:T(4,128)(2,1)S(1)}, u32[]{:S(2)}, u32[]{:S(2)}) %collective-permute-start.11) | collective-permute-done | bytes 42016 | tf_op jit(solution)/shard_map/ppermute | solution.py:32
  46.1 2.0 %collective-permute-done.9.refs_0_ = bf16[41,4,128]{2,1,0:T(4,128)(2,1)S(1)} collective-permute-done((bf16[41,4,128]{2,1,0:T(4,128)(2,1)S(1)}, bf16[41,4,128]{2,1,0:T(4,128)(2,1)S(1)}, u32[]{:S(2)}, u32[]{:S(2)}) %collective-permute-start.9) | collective-permute-done | bytes 42016 | tf_op jit(solution)/shard_map/ppermute | solution.py:32
  48.1 3.3 %collective-permute-start.12 = (bf16[41,4,128]{2,1,0:T(4,128)(2,1)S(1)}, bf16[41,4,128]{2,1,0:T(4,128)(2,1)S(1)}, u32[]{:S(2)}, u32[]{:S(2)}) collective-permute-start(bf16[41,4,128]{2,1,0:T(4,128)(2,1)S(1)} %shard_map.77.own_ref), channel_id=1, source_target_pairs={{0,64},{32,96},{64,0},{96,32},{128,192},{160,224},{192,128},{224,1... | collective-permute-start | bytes 125960 | tf_op jit(solution)/shard_map/ppermute | solution.py:36
  51.4 0.7 %collective-permute-start.13 = (bf16[41,4,128]{2,1,0:T(4,128)(2,1)S(1)}, bf16[41,4,128]{2,1,0:T(4,128)(2,1)S(1)}, u32[]{:S(2)}, u32[]{:S(2)}) collective-permute-start(bf16[41,4,128]{2,1,0:T(4,128)(2,1)S(1)} %shard_map.77.own_ref), channel_id=1, source_target_pairs={{0,32},{32,0},{64,96},{96,64},{128,160},{160,128},{192,224},{224,1... | collective-permute-start | bytes 125960 | tf_op jit(solution)/shard_map/ppermute | solution.py:36
  52.1 0.4 collective-permute-start.14
  52.5 1.3 %collective-permute-done.12.refs_0_ = bf16[41,4,128]{2,1,0:T(4,128)(2,1)S(1)} collective-permute-done((bf16[41,4,128]{2,1,0:T(4,128)(2,1)S(1)}, bf16[41,4,128]{2,1,0:T(4,128)(2,1)S(1)}, u32[]{:S(2)}, u32[]{:S(2)}) %collective-permute-start.12) | collective-permute-done | bytes 42016 | tf_op jit(solution)/shard_map/ppermute | solution.py:36
  53.7 1.7 %collective-permute-done.13.refs_1_ = bf16[41,4,128]{2,1,0:T(4,128)(2,1)S(1)} collective-permute-done((bf16[41,4,128]{2,1,0:T(4,128)(2,1)S(1)}, bf16[41,4,128]{2,1,0:T(4,128)(2,1)S(1)}, u32[]{:S(2)}, u32[]{:S(2)}) %collective-permute-start.13) | collective-permute-done | bytes 42016 | tf_op jit(solution)/shard_map/ppermute | solution.py:36
  55.4 1.9 %collective-permute-done.14.refs_2_ = bf16[41,4,128]{2,1,0:T(4,128)(2,1)S(1)} collective-permute-done((bf16[41,4,128]{2,1,0:T(4,128)(2,1)S(1)}, bf16[41,4,128]{2,1,0:T(4,128)(2,1)S(1)}, u32[]{:S(2)}, u32[]{:S(2)}) %collective-permute-start.14) | collective-permute-done | bytes 42016 | tf_op jit(solution)/shard_map/ppermute | solution.py:36
  57.4 0.1 collective-permute-start.15
  57.5 4.0 %collective-permute-done.15.got_ref = bf16[41,4,128]{2,1,0:T(4,128)(2,1)S(1)} collective-permute-done((bf16[41,4,128]{2,1,0:T(4,128)(2,1)S(1)}, bf16[41,4,128]{2,1,0:T(4,128)(2,1)S(1)}, u32[]{:S(2)}, u32[]{:S(2)}) %collective-permute-start.15) | collective-permute-done | bytes 42016 | tf_op jit(solution)/shard_map/ppermute | solution.py:40
  61.5 0.7 %shard_map.79 = (f32[27,4,64]{2,1,0:T(4,128)}, f32[27,4,128]{2,1,0:T(4,128)}) custom-call(bf16[41,4,128]{2,1,0:T(4,128)(2,1)S(1)} %shard_map.78.own_ref, bf16[41,4,128]{2,1,0:T(4,128)(2,1)S(1)} %collective-permute-done.15.got_ref), custom_call_target="tpu_custom_call" | custom-call | flops 1000000 | bytes 83968 | tf_op jit(solution)/shard_map/pallas_call | solution.py:316
  (16 shorter events, 0.4 us)
Async XLA Ops:
  1.6 11.4 %collective-permute-start = (bf16[32,4096]{1,0:T(8,128)(2,1)S(1)}, bf16[32,4096]{1,0:T(8,128)(2,1)S(1)}, u32[]{:S(2)}, u32[]{:S(2)}) collective-permute-start(bf16[32,4096]{1,0:T(8,128)(2,1)S(1)} %slice_bitcast_fusion.rim_ref), channel_id=1, source_target_pairs={{0,1},{1,2},{2,3},{3,4},{4,5},{5,6},{6,7},{7,8},{8,9},{9,10},{10,1... | collective-permute-start | bytes 786440 | tf_op jit(solution)/shard_map/ppermute | solution.py:16
  4.4 8.6 %collective-permute-start.1 = (f32[128,128]{1,0:T(8,128)S(1)}, f32[128,128]{1,0:T(8,128)S(1)}, u32[]{:S(2)}, u32[]{:S(2)}) collective-permute-start(f32[128,128]{1,0:T(8,128)S(1)} %get-tuple-element.42), channel_id=1, source_target_pairs={{0,1},{1,2},{2,3},{3,4},{4,5},{5,6},{6,7},{7,8},{8,9},{9,10},{10,1... | collective-permute-start | bytes 196616 | tf_op jit(solution)/shard_map/ppermute | solution.py:16
  7.9 5.2 %copy-start = (bf16[1,1,8,16,128]{4,3,2,1,0:T(8,128)(2,1)S(1)}, bf16[1,1,8,16,128]{4,3,2,1,0:T(8,128)(2,1)}, u32[]{:S(2)}) copy-start(bf16[1,1,8,16,128]{4,3,2,1,0:T(8,128)(2,1)} %param.7) | copy-start | bytes 98308
  14.0 1.9 %collective-permute-start.2 = (bf16[128,128]{1,0:T(8,128)(2,1)S(1)}, bf16[128,128]{1,0:T(8,128)(2,1)S(1)}, u32[]{:S(2)}, u32[]{:S(2)}) collective-permute-start(bf16[128,128]{1,0:T(8,128)(2,1)S(1)} %get-tuple-element.50.gp_ref), channel_id=1, source_target_pairs={{0,31},{1,0},{2,1},{3,2},{4,3},{5,4},{6,5},{7,6},{8,7},{9,8},{10,9... | collective-permute-start | bytes 98312 | tf_op jit(solution)/shard_map/ppermute | solution.py:16
  16.9 2.7 %collective-permute-start.6 = (bf16[23,64,128]{2,1,0:T(8,128)(2,1)S(1)}, bf16[23,64,128]{2,1,0:T(8,128)(2,1)S(1)}, u32[]{:S(2)}, u32[]{:S(2)}) collective-permute-start(bf16[23,64,128]{2,1,0:T(8,128)(2,1)S(1)} %get-tuple-element.70), channel_id=1, source_target_pairs={{0,1},{1,0},{2,3},{3,2},{4,5},{5,4},{6,7},{7,6},{8,9},{9,8},{10,11... | collective-permute-start | bytes 1130504 | tf_op jit(solution)/shard_map/ppermute | solution.py:20
  18.3 2.3 %collective-permute-start.3 = (bf16[18,64,128]{2,1,0:T(8,128)(2,1)S(1)}, bf16[18,64,128]{2,1,0:T(8,128)(2,1)S(1)}, u32[]{:S(2)}, u32[]{:S(2)}) collective-permute-start(bf16[18,64,128]{2,1,0:T(8,128)(2,1)S(1)} %get-tuple-element.64), channel_id=1, source_target_pairs={{0,1},{1,0},{2,3},{3,2},{4,5},{5,4},{6,7},{7,6},{8,9},{9,8},{10,11... | collective-permute-start | bytes 884744 | tf_op jit(solution)/shard_map/ppermute | solution.py:20
  19.7 5.7 %collective-permute-start.7 = (bf16[23,32,128]{2,1,0:T(8,128)(2,1)S(1)}, bf16[23,32,128]{2,1,0:T(8,128)(2,1)S(1)}, u32[]{:S(2)}, u32[]{:S(2)}) collective-permute-start(bf16[23,32,128]{2,1,0:T(8,128)(2,1)S(1)} %get-tuple-element.72), channel_id=1, source_target_pairs={{0,8},{1,25},{2,10},{3,27},{4,12},{5,29},{6,14},{7,31},{8,0},{9,17... | collective-permute-start | bytes 565256 | tf_op jit(solution)/shard_map/ppermute | solution.py:28
  20.6 6.4 %collective-permute-start.4 = (bf16[18,32,128]{2,1,0:T(8,128)(2,1)S(1)}, bf16[18,32,128]{2,1,0:T(8,128)(2,1)S(1)}, u32[]{:S(2)}, u32[]{:S(2)}) collective-permute-start(bf16[18,32,128]{2,1,0:T(8,128)(2,1)S(1)} %get-tuple-element.66), channel_id=1, source_target_pairs={{0,8},{1,25},{2,10},{3,27},{4,12},{5,29},{6,14},{7,31},{8,0},{9,17... | collective-permute-start | bytes 442376 | tf_op jit(solution)/shard_map/ppermute | solution.py:28
  25.4 7.4 %collective-permute-start.8 = (bf16[23,16,128]{2,1,0:T(8,128)(2,1)S(1)}, bf16[23,16,128]{2,1,0:T(8,128)(2,1)S(1)}, u32[]{:S(2)}, u32[]{:S(2)}) collective-permute-start(bf16[23,16,128]{2,1,0:T(8,128)(2,1)S(1)} %get-tuple-element.74), channel_id=1, source_target_pairs={{0,24},{1,9},{2,26},{3,11},{4,28},{5,13},{6,30},{7,15},{8,16},{9,1... | collective-permute-start | bytes 282632 | tf_op jit(solution)/shard_map/ppermute | solution.py:28
  27.1 5.7 %collective-permute-start.5 = (bf16[18,16,128]{2,1,0:T(8,128)(2,1)S(1)}, bf16[18,16,128]{2,1,0:T(8,128)(2,1)S(1)}, u32[]{:S(2)}, u32[]{:S(2)}) collective-permute-start(bf16[18,16,128]{2,1,0:T(8,128)(2,1)S(1)} %get-tuple-element.68), channel_id=1, source_target_pairs={{0,24},{1,9},{2,26},{3,11},{4,28},{5,13},{6,30},{7,15},{8,16},{9,1... | collective-permute-start | bytes 221192 | tf_op jit(solution)/shard_map/ppermute | solution.py:28
  32.8 10.4 %collective-permute-start.10 = (bf16[41,4,128]{2,1,0:T(4,128)(2,1)S(1)}, bf16[41,4,128]{2,1,0:T(4,128)(2,1)S(1)}, u32[]{:S(2)}, u32[]{:S(2)}) collective-permute-start(bf16[41,4,128]{2,1,0:T(4,128)(2,1)S(1)} %get-tuple-element.77), channel_id=1, source_target_pairs={{0,4},{1,5},{2,6},{3,7},{4,0},{5,1},{6,2},{7,3},{8,12},{9,13},{10,... | collective-permute-start | bytes 125960 | tf_op jit(solution)/shard_map/ppermute | solution.py:32
  40.0 6.1 %collective-permute-start.11 = (bf16[41,4,128]{2,1,0:T(4,128)(2,1)S(1)}, bf16[41,4,128]{2,1,0:T(4,128)(2,1)S(1)}, u32[]{:S(2)}, u32[]{:S(2)}) collective-permute-start(bf16[41,4,128]{2,1,0:T(4,128)(2,1)S(1)} %get-tuple-element.78), channel_id=1, source_target_pairs={{0,6},{1,7},{2,4},{3,5},{4,2},{5,3},{6,0},{7,1},{8,14},{9,15},{10,... | collective-permute-start | bytes 125960 | tf_op jit(solution)/shard_map/ppermute | solution.py:32
  43.2 4.9 %collective-permute-start.9 = (bf16[41,4,128]{2,1,0:T(4,128)(2,1)S(1)}, bf16[41,4,128]{2,1,0:T(4,128)(2,1)S(1)}, u32[]{:S(2)}, u32[]{:S(2)}) collective-permute-start(bf16[41,4,128]{2,1,0:T(4,128)(2,1)S(1)} %get-tuple-element.76), channel_id=1, source_target_pairs={{0,2},{1,3},{2,0},{3,1},{4,6},{5,7},{6,4},{7,5},{8,10},{9,11},{10,... | collective-permute-start | bytes 125960 | tf_op jit(solution)/shard_map/ppermute | solution.py:32
  48.1 5.6 %collective-permute-start.12 = (bf16[41,4,128]{2,1,0:T(4,128)(2,1)S(1)}, bf16[41,4,128]{2,1,0:T(4,128)(2,1)S(1)}, u32[]{:S(2)}, u32[]{:S(2)}) collective-permute-start(bf16[41,4,128]{2,1,0:T(4,128)(2,1)S(1)} %shard_map.77.own_ref), channel_id=1, source_target_pairs={{0,64},{32,96},{64,0},{96,32},{128,192},{160,224},{192,128},{224,1... | collective-permute-start | bytes 125960 | tf_op jit(solution)/shard_map/ppermute | solution.py:36
  51.4 4.0 %collective-permute-start.13 = (bf16[41,4,128]{2,1,0:T(4,128)(2,1)S(1)}, bf16[41,4,128]{2,1,0:T(4,128)(2,1)S(1)}, u32[]{:S(2)}, u32[]{:S(2)}) collective-permute-start(bf16[41,4,128]{2,1,0:T(4,128)(2,1)S(1)} %shard_map.77.own_ref), channel_id=1, source_target_pairs={{0,32},{32,0},{64,96},{96,64},{128,160},{160,128},{192,224},{224,1... | collective-permute-start | bytes 125960 | tf_op jit(solution)/shard_map/ppermute | solution.py:36
  52.1 5.2 %collective-permute-start.14 = (bf16[41,4,128]{2,1,0:T(4,128)(2,1)S(1)}, bf16[41,4,128]{2,1,0:T(4,128)(2,1)S(1)}, u32[]{:S(2)}, u32[]{:S(2)}) collective-permute-start(bf16[41,4,128]{2,1,0:T(4,128)(2,1)S(1)} %shard_map.77.own_ref), channel_id=1, source_target_pairs={{0,96},{32,64},{64,32},{96,0},{128,224},{160,192},{192,160},{224,1... | collective-permute-start | bytes 125960 | tf_op jit(solution)/shard_map/ppermute | solution.py:36
  57.4 4.1 %collective-permute-start.15 = (bf16[41,4,128]{2,1,0:T(4,128)(2,1)S(1)}, bf16[41,4,128]{2,1,0:T(4,128)(2,1)S(1)}, u32[]{:S(2)}, u32[]{:S(2)}) collective-permute-start(bf16[41,4,128]{2,1,0:T(4,128)(2,1)S(1)} %shard_map.78.own_ref), channel_id=1, source_target_pairs={{0,128},{32,160},{64,192},{96,224},{128,0},{160,32},{192,64},{224,... | collective-permute-start | bytes 125960 | tf_op jit(solution)/shard_map/ppermute | solution.py:40
